TPU v7x, 256 devices: a whole 4x4x8 slice. The times are simulated.
256 devices in a mesh: gx: 16 (over x_hi, z), gy: 16 (over y, x_lo, core).
Axes of the slice: x: 4 (x_hi: 2, x_lo: 2; x = x_hi * 2 + x_lo), y: 4, z: 8, core: 2. Of those that a mesh axis runs over, the one named last changes fastest.
Arguments:
- tangent: float32 [256, 256, 512], P('gx', 'gy'), may hold values from -6 to 6
- hessian: bfloat16 [5, 5, 256, 256, 512], P(None, None, 'gx', 'gy'), may hold values from -1.5 to 8, as said below
- kernel_rows: float32 [5, 17], replicated, may hold values from -1 to 1
- kernel_cols: float32 [5, 17], replicated, may hold values from -1 to 1
- kernel_depth: bfloat16 [5, 17], replicated, may hold values from -1 to 1
Outputs:
- hessian_product: float32 [256, 256, 512], P('gx', 'gy')
Inputs may be any that keep to these rules, and one draw needn't show every extreme that they name: `hessian`: Off-diagonal entries lie within -1.5 to 1.5; diagonal entries are positive, between 0.3 and 8.
All inputs are finite; a program needn't handle non-finite values.
Results may differ from a plain program's by a relative error of at most 0.0022.
Values sent between devices are 32-bit elements; how exact they have to be, the bound alone decides.
No kernel may reach another device: no remote copies, remote signals or barrier semaphores. Data moves between devices by JAX's collectives and lax.ppermute only.
A program may use at most 128 MiB of HBM per device.

v0:
```python
import jax
import jax.numpy as jnp
from jax import lax
from jax.sharding import PartitionSpec as P

RADIUS = 8
DENSITIES = 5


def padded(cells, sides, width):
    for axis, dim in sides:
        count = lax.axis_size(axis)
        head = lax.slice_in_dim(cells, 0, width, axis=dim)
        tail = lax.slice_in_dim(cells, cells.shape[dim] - width, cells.shape[dim], axis=dim)
        cells = jnp.concatenate(
            [
                lax.ppermute(tail, axis, [(i, (i + 1) % count) for i in range(count)]),
                cells,
                lax.ppermute(head, axis, [((i + 1) % count, i) for i in range(count)]),
            ],
            axis=dim,
        )
    return cells


def depth_bands(kernel_depth, depth):
    rows_index = lax.broadcasted_iota(jnp.int32, (depth, depth), 0)
    cols_index = lax.broadcasted_iota(jnp.int32, (depth, depth), 1)
    offsets = cols_index - rows_index
    weights = kernel_depth.astype(jnp.float32)
    bands = []
    for density in range(DENSITIES):
        matrix = jnp.zeros((depth, depth), jnp.float32)
        for shift_tap in range(2 * RADIUS + 1):
            matrix = matrix + jnp.where(
                offsets == shift_tap - RADIUS, weights[density, shift_tap], 0.0
            )
        bands.append(matrix.astype(jnp.bfloat16))
    return bands


def per_device(tangent, hessian, kernel_rows, kernel_cols, kernel_depth):
    span_rows, span_cols, depth = tangent.shape
    reach = RADIUS
    extended = padded(tangent, (("gx", 0), ("gy", 1)), RADIUS)
    bands = depth_bands(kernel_depth, depth)
    densities = []
    for density in range(DENSITIES):
        along_rows = jnp.zeros((span_rows, span_cols + 2 * reach, depth), jnp.float32)
        for shift_tap in range(2 * reach + 1):
            along_rows = (
                along_rows
                + kernel_rows[density, shift_tap] * extended[shift_tap : shift_tap + span_rows]
            )
        along_cols = jnp.zeros((span_rows, span_cols, depth), jnp.float32)
        for shift_tap in range(2 * reach + 1):
            along_cols = (
                along_cols
                + kernel_cols[density, shift_tap] * along_rows[:, shift_tap : shift_tap + span_cols]
            )
        lowered = along_cols.astype(jnp.bfloat16).reshape(-1, depth)
        flat = jnp.dot(lowered, bands[density].T, preferred_element_type=jnp.float32)
        densities.append(flat.reshape(span_rows, span_cols, depth))
    transformed = []
    for density in range(DENSITIES):
        gradient = jnp.zeros((span_rows, span_cols, depth), jnp.float32)
        for other in range(DENSITIES):
            gradient = gradient + hessian[density, other].astype(jnp.float32) * densities[other]
        lowered = gradient.astype(jnp.bfloat16).reshape(-1, depth)
        flat = jnp.dot(lowered, bands[density], preferred_element_type=jnp.float32)
        transformed.append(flat.reshape(span_rows, span_cols, depth))
    stacked = jnp.stack(transformed, 0)
    row_weights = kernel_rows[:, :, None, None, None]
    col_weights = kernel_cols[:, :, None, None, None]
    gathered = padded(stacked, (("gx", 1), ("gy", 2)), RADIUS)
    along_rows = jnp.zeros((DENSITIES, span_rows, span_cols + 2 * reach, depth), jnp.float32)
    for shift_tap in range(2 * reach + 1):
        start = 2 * reach - shift_tap
        along_rows = along_rows + row_weights[:, shift_tap] * gathered[:, start : start + span_rows]
    along_cols = jnp.zeros((DENSITIES, span_rows, span_cols, depth), jnp.float32)
    for shift_tap in range(2 * reach + 1):
        start = 2 * reach - shift_tap
        along_cols = (
            along_cols + col_weights[:, shift_tap] * along_rows[:, :, start : start + span_cols]
        )
    return jnp.sum(along_cols, 0)


def solution(mesh):
    return jax.shard_map(
        per_device,
        mesh=mesh,
        in_specs=(P("gx", "gy", None), P(None, None, "gx", "gy", None), P(), P(), P()),
        out_specs=P("gx", "gy", None),
        check_vma=False,
    )
```

profile of v0, /device:TPU:4, one launch (start us, length us, event | category | flops | bytes accessed | tf_op | source)
XLA Modules:
  0.0 430.2 jit_solution(10056630881273614908)
XLA Ops:
  0.0 1.1 fusion.458
  1.1 2.0 collective-permute-start
  3.1 4.0 collective-permute-start.1
  7.1 2.1 fusion.470
  9.2 2.1 fusion.469
  11.3 2.7 fusion.466
  14.0 2.7 fusion.467
  16.7 2.1 fusion.461
  18.8 2.1 fusion.462
  20.9 2.1 fusion.472
  23.0 1.9 fusion.468
  24.9 2.7 fusion.465
  27.6 1.7 fusion.463
  29.3 1.1 constant_dynamic-update-slice_fusion.1
  30.6 3.8 collective-permute-start.3
  34.4 0.7 fusion.473
  35.1 0.7 fusion.460
  35.9 0.7 fusion.471
  36.6 0.7 fusion.464
  37.3 0.7 fusion.459
  38.0 6.1 %collective-permute-done.2 = f32[32,8,512]{2,1,0:T(8,128)S(1)} collective-permute-done((f32[32,8,512]{2,1,0:T(8,128)S(1)}, f32[32,8,512]{2,1,0:T(8,128)S(1)}, u32[]{:S(2)}, u32[]{:S(2)}) %collective-permute-start.2) | collective-permute-done | bytes 524320 | tf_op jit(solution)/shard_map/ppermute | solution.py:17
  44.6 13.0 %multiply_add_fusion.1 = f32[16,32,512]{2,1,0:T(8,128)S(1)} fusion(f32[32,32,512]{2,1,0:T(8,128)S(1)} %pad_maximum_fusion.2, f32[]{:T(128)} %bitcast.179, f32[]{:T(128)} %bitcast.178, f32[]{:T(128)} %bitcast.177, f32[]{:T(128)} %bitcast.176, f32[]{:T(128)} %bitcast.175, f32[]{:T(128)} %bitcast.174, f32[]{:T(128)} %bitcast.173, f32[]{:T(128)} %bitcast.172, ...), kind=kLoop, calls=%fused_computation.83 | loop fusion | flops 8650752 | bytes 18874436 | tf_op jit(solution)/shard_map/add | solution.py:52
  57.6 13.0 %multiply_add_fusion.2 = f32[16,32,512]{2,1,0:T(8,128)S(1)} fusion(f32[32,32,512]{2,1,0:T(8,128)S(1)} %pad_maximum_fusion.2, f32[]{:T(128)} %bitcast.126, f32[]{:T(128)} %bitcast.125, f32[]{:T(128)} %bitcast.124, f32[]{:T(128)} %bitcast.123, f32[]{:T(128)} %bitcast.122, f32[]{:T(128)} %bitcast.121, f32[]{:T(128)} %bitcast.120, f32[]{:T(128)} %bitcast.119, ...), kind=kLoop, calls=%fused_computation.85 | loop fusion | flops 8650752 | bytes 18874436 | tf_op jit(solution)/shard_map/add | solution.py:52
  70.6 12.9 %multiply_add_fusion.3 = f32[16,32,512]{2,1,0:T(8,128)S(1)} fusion(f32[32,32,512]{2,1,0:T(8,128)S(1)} %pad_maximum_fusion.2, f32[]{:T(128)} %bitcast.73, f32[]{:T(128)} %bitcast.72, f32[]{:T(128)} %bitcast.71, f32[]{:T(128)} %bitcast.70, f32[]{:T(128)} %bitcast.69, f32[]{:T(128)} %bitcast.68, f32[]{:T(128)} %bitcast.67, f32[]{:T(128)} %bitcast.66, ...), kind=kLoop, calls=%fused_computation.87 | loop fusion | flops 8650752 | bytes 18874436 | tf_op jit(solution)/shard_map/add | solution.py:52
  83.5 12.7 %multiply_add_fusion.4 = f32[16,32,512]{2,1,0:T(8,128)S(1)} fusion(f32[32,32,512]{2,1,0:T(8,128)S(1)} %pad_maximum_fusion.2, f32[]{:T(128)} %bitcast.20, f32[]{:T(128)} %bitcast.19, f32[]{:T(128)} %bitcast.18, f32[]{:T(128)} %bitcast.17, f32[]{:T(128)} %bitcast.16, f32[]{:T(128)} %bitcast.15, f32[]{:T(128)} %bitcast.14, f32[]{:T(128)} %bitcast.13, ...), kind=kLoop, calls=%fused_computation.107 | loop fusion | flops 8650752 | bytes 18874436 | tf_op jit(solution)/shard_map/add | solution.py:52
  96.2 13.0 %multiply_add_fusion = f32[16,32,512]{2,1,0:T(8,128)S(1)} fusion(f32[32,32,512]{2,1,0:T(8,128)S(1)} %pad_maximum_fusion.2, f32[]{:T(128)} %bitcast.232, f32[]{:T(128)} %bitcast.231, f32[]{:T(128)} %bitcast.230, f32[]{:T(128)} %bitcast.229, f32[]{:T(128)} %bitcast.228, f32[]{:T(128)} %bitcast.227, f32[]{:T(128)} %bitcast.226, f32[]{:T(128)} %bitcast.225, ...), kind=kLoop, calls=%fused_computation.81 | loop fusion | flops 8650752 | bytes 18874436 | tf_op jit(solution)/shard_map/add | solution.py:52
  109.2 22.3 %fusion.174 = f32[16,16,512]{2,1,0:T(8,128)S(1)} fusion(f32[]{:T(128)} %bitcast.212, f32[]{:T(128)} %bitcast.211, f32[]{:T(128)} %bitcast.210, f32[]{:T(128)} %bitcast.209, f32[]{:T(128)} %bitcast.208, f32[]{:T(128)} %bitcast.207, f32[]{:T(128)} %bitcast.206, f32[]{:T(128)} %bitcast.205, f32[]{:T(128)} %bitcast.204, f32[]{:T(128)} %bitcast.203, ...), kind=kOutput, calls=%fused_computation.334 | convolution fusion | flops 152305664 | bytes 9437320 | tf_op jit(solution)/shard_map/dot_general | solution.py:62
  131.5 22.7 %fusion.177 = f32[16,16,512]{2,1,0:T(8,128)S(1)} fusion(f32[]{:T(128)} %bitcast.159, f32[]{:T(128)} %bitcast.158, f32[]{:T(128)} %bitcast.157, f32[]{:T(128)} %bitcast.156, f32[]{:T(128)} %bitcast.155, f32[]{:T(128)} %bitcast.154, f32[]{:T(128)} %bitcast.153, f32[]{:T(128)} %bitcast.152, f32[]{:T(128)} %bitcast.151, f32[]{:T(128)} %bitcast.150, ...), kind=kOutput, calls=%fused_computation.335 | convolution fusion | flops 152305664 | bytes 9437320 | tf_op jit(solution)/shard_map/dot_general | solution.py:62
  154.3 22.8 %fusion.180 = f32[16,16,512]{2,1,0:T(8,128)S(1)} fusion(f32[]{:T(128)} %bitcast.106, f32[]{:T(128)} %bitcast.105, f32[]{:T(128)} %bitcast.104, f32[]{:T(128)} %bitcast.103, f32[]{:T(128)} %bitcast.102, f32[]{:T(128)} %bitcast.101, f32[]{:T(128)} %bitcast.100, f32[]{:T(128)} %bitcast.99, f32[]{:T(128)} %bitcast.98, f32[]{:T(128)} %bitcast.97, f32[]{:T(128)} %bitcast.96, ...), kind=kOutput, calls=%fused_computation.336 | convolution fusion | flops 152305664 | bytes 9437320 | tf_op jit(solution)/shard_map/dot_general | solution.py:62
  177.0 22.6 %fusion.191 = f32[16,16,512]{2,1,0:T(8,128)S(1)} fusion(f32[]{:T(128)} %bitcast.53, f32[]{:T(128)} %bitcast.52, f32[]{:T(128)} %bitcast.51, f32[]{:T(128)} %bitcast.50, f32[]{:T(128)} %bitcast.49, f32[]{:T(128)} %bitcast.48, f32[]{:T(128)} %bitcast.47, f32[]{:T(128)} %bitcast.46, f32[]{:T(128)} %bitcast.45, f32[]{:T(128)} %bitcast.44, f32[]{:T(128)} %bitcast.43, ...), kind=kOutput, calls=%fused_computation.345 | convolution fusion | flops 152305664 | bytes 9437320 | tf_op jit(solution)/shard_map/dot_general | solution.py:62
  199.7 22.7 %fusion.171 = f32[16,16,512]{2,1,0:T(8,128)S(1)} fusion(f32[]{:T(128)} %bitcast.265, f32[]{:T(128)} %bitcast.264, f32[]{:T(128)} %bitcast.263, f32[]{:T(128)} %bitcast.262, f32[]{:T(128)} %bitcast.261, f32[]{:T(128)} %bitcast.260, f32[]{:T(128)} %bitcast.259, f32[]{:T(128)} %bitcast.258, f32[]{:T(128)} %bitcast.257, f32[]{:T(128)} %bitcast.256, ...), kind=kOutput, calls=%fused_computation.333 | convolution fusion | flops 152305664 | bytes 9437320 | tf_op jit(solution)/shard_map/dot_general | solution.py:62
  222.4 12.7 %fusion.37 = f32[5,16,16,512]{3,2,1,0:T(8,128)S(1)} fusion(f32[]{:T(128)} %bitcast.53, f32[]{:T(128)} %bitcast.52, f32[]{:T(128)} %bitcast.51, f32[]{:T(128)} %bitcast.50, f32[]{:T(128)} %bitcast.49, f32[]{:T(128)} %bitcast.48, f32[]{:T(128)} %bitcast.47, f32[]{:T(128)} %bitcast.46, f32[]{:T(128)} %bitcast.45, f32[]{:T(128)} %bitcast.44, f32[]{:T(128)} %bitcast.43, ...), kind=kOutput, calls=%fused_computation.79 | convolution fusion | flops 149815296 | bytes 4465152 | tf_op jit(solution)/shard_map/dot_general | solution.py:70
  235.1 12.8 %fusion.36 = f32[5,16,16,512]{3,2,1,0:T(8,128)S(1)} fusion(f32[5,16,16,512]{3,2,1,0:T(8,128)S(1)} %fusion.37, f32[]{:T(128)} %bitcast.106, f32[]{:T(128)} %bitcast.105, f32[]{:T(128)} %bitcast.104, f32[]{:T(128)} %bitcast.103, f32[]{:T(128)} %bitcast.102, f32[]{:T(128)} %bitcast.101, f32[]{:T(128)} %bitcast.100, f32[]{:T(128)} %bitcast.99, f32[]{:T(128)} %bitcast.98, ...), kind=kOutput, calls=%fused_computation.77 | convolution fusion | flops 149815296 | bytes 4465152 | tf_op jit(solution)/shard_map/dot_general | solution.py:70
  247.9 12.7 %fusion.35 = f32[5,16,16,512]{3,2,1,0:T(8,128)S(1)} fusion(f32[5,16,16,512]{3,2,1,0:T(8,128)S(1)} %fusion.36, f32[]{:T(128)} %bitcast.159, f32[]{:T(128)} %bitcast.158, f32[]{:T(128)} %bitcast.157, f32[]{:T(128)} %bitcast.156, f32[]{:T(128)} %bitcast.155, f32[]{:T(128)} %bitcast.154, f32[]{:T(128)} %bitcast.153, f32[]{:T(128)} %bitcast.152, f32[]{:T(128)} %bitcast.151, ...), kind=kOutput, calls=%fused_computation.75 | convolution fusion | flops 149815296 | bytes 4465152 | tf_op jit(solution)/shard_map/dot_general | solution.py:70
  260.6 12.8 %fusion.34 = f32[5,16,16,512]{3,2,1,0:T(8,128)S(1)} fusion(f32[5,16,16,512]{3,2,1,0:T(8,128)S(1)} %fusion.35, f32[]{:T(128)} %bitcast.212, f32[]{:T(128)} %bitcast.211, f32[]{:T(128)} %bitcast.210, f32[]{:T(128)} %bitcast.209, f32[]{:T(128)} %bitcast.208, f32[]{:T(128)} %bitcast.207, f32[]{:T(128)} %bitcast.206, f32[]{:T(128)} %bitcast.205, f32[]{:T(128)} %bitcast.204, ...), kind=kOutput, calls=%fused_computation.73 | convolution fusion | flops 149815296 | bytes 4465152 | tf_op jit(solution)/shard_map/dot_general | solution.py:70
  273.4 12.6 %fusion.33 = f32[5,16,16,512]{3,2,1,0:T(8,128)S(1)} fusion(f32[5,16,16,512]{3,2,1,0:T(8,128)S(1)} %fusion.34, f32[]{:T(128)} %bitcast.265, f32[]{:T(128)} %bitcast.264, f32[]{:T(128)} %bitcast.263, f32[]{:T(128)} %bitcast.262, f32[]{:T(128)} %bitcast.261, f32[]{:T(128)} %bitcast.260, f32[]{:T(128)} %bitcast.259, f32[]{:T(128)} %bitcast.258, f32[]{:T(128)} %bitcast.257, ...), kind=kOutput, calls=%fused_computation.71 | convolution fusion | flops 149815296 | bytes 4465152 | tf_op jit(solution)/shard_map/dot_general | solution.py:70
  286.0 0.4 fusion.456
  286.6 5.6 %collective-permute-start.5 = (f32[5,8,16,512]{3,2,1,0:T(8,128)S(1)}, f32[5,8,16,512]{3,2,1,0:T(8,128)S(1)}, u32[]{:S(2)}, u32[]{:S(2)}) collective-permute-start(f32[5,8,16,512]{3,2,1,0:T(8,128)S(1)} %get-tuple-element.42), channel_id=1, source_target_pairs={{16,0},{32,16},{48,32},{64,48},{80,64},{96,80},{112,96},{128,112},... | collective-permute-start | bytes 3932168 | tf_op jit(solution)/shard_map/ppermute | solution.py:19
  292.2 29.4 %collective-permute-done.4 = f32[5,8,16,512]{3,2,1,0:T(8,128)S(1)} collective-permute-done((f32[5,8,16,512]{3,2,1,0:T(8,128)S(1)}, f32[5,8,16,512]{3,2,1,0:T(8,128)S(1)}, u32[]{:S(2)}, u32[]{:S(2)}) %collective-permute-start.4) | collective-permute-done | bytes 1310752 | tf_op jit(solution)/shard_map/ppermute | solution.py:17
  321.6 1.0 pad_maximum_fusion.1
  322.6 0.6 fusion.455
  323.4 3.7 collective-permute-start.7
  327.2 0.4 slice_reduce_fusion.32
  327.6 0.4 slice_reduce_fusion.33
  328.0 54.6 %collective-permute-done.6 = f32[5,32,8,512]{3,2,1,0:T(8,128)S(1)} collective-permute-done((f32[5,32,8,512]{3,2,1,0:T(8,128)S(1)}, f32[5,32,8,512]{3,2,1,0:T(8,128)S(1)}, u32[]{:S(2)}, u32[]{:S(2)}) %collective-permute-start.6) | collective-permute-done | bytes 2621472 | tf_op jit(solution)/shard_map/ppermute | solution.py:17
  382.6 5.0 %pad_maximum_fusion = f32[5,32,32,512]{3,2,1,0:T(8,128)} fusion(f32[5,32,8,512]{3,2,1,0:T(8,128)S(1)} %collective-permute-done.7, f32[5,8,16,512]{3,2,1,0:T(8,128)S(1)} %collective-permute-done.5, f32[5,16,16,512]{3,2,1,0:T(8,128)S(1)} %fusion.33, f32[5,8,16,512]{3,2,1,0:T(8,128)S(1)} %collective-permute-done.4, f32[5,32,8,512]{3,2,1,0:T(8,128)S(1)} %collective-permute-done.6), kind=kLoop, calls=%fused_computation | loop fusion | flops 10485760 | bytes 20971520 | tf_op jit(solution)/shard_map/concatenate | solution.py:15
  387.7 35.5 %fusion = f32[5,16,32,512]{3,2,1,0:T(8,128)S(1)} fusion(f32[5,32,32,512]{3,2,1,0:T(8,128)} %pad_maximum_fusion, f32[5]{0:T(128)S(1)} %get-tuple-element.23, f32[5]{0:T(128)S(1)} %get-tuple-element.24, f32[5]{0:T(128)S(1)} %get-tuple-element.25, f32[5]{0:T(128)S(1)} %get-tuple-element.26, f32[5]{0:T(128)S(1)} %get-tuple-element.27, ...), kind=kLoop, calls=%fused_computation.2 | loop fusion | flops 43253760 | bytes 94372176 | tf_op jit(solution)/shard_map/add | solution.py:79
  423.2 7.0 %fusion.17 = f32[16,16,512]{2,1,0:T(8,128)} fusion(f32[5,16,32,512]{3,2,1,0:T(8,128)S(1)} %fusion, f32[5]{0:T(128)S(1)} %get-tuple-element.6, f32[5]{0:T(128)S(1)} %get-tuple-element.7, f32[5]{0:T(128)S(1)} %get-tuple-element.8, f32[5]{0:T(128)S(1)} %get-tuple-element.9, f32[5]{0:T(128)S(1)} %get-tuple-element.10, f32[5]{0:T(128)S(1)} %get-tuple-element.11, ...), kind=kLoop, calls=%fused_computation.37 | loop fusion | flops 22151168 | bytes 45089108 | tf_op jit(solution)/shard_map/reduce_sum | solution.py:86
  (18 shorter events, 1.0 us)
Async XLA Ops:
  0.0 34.4 %copy-start.2 = (bf16[5,17]{1,0:T(8,128)(2,1)S(1)}, bf16[5,17]{1,0:T(8,128)(2,1)}, u32[]{:S(2)}) copy-start(bf16[5,17]{1,0:T(8,128)(2,1)} %param.9) | copy-start | bytes 514
  0.0 36.6 %copy-start = (f32[5,17]{1,0:T(8,128)S(1)}, f32[5,17]{1,0:T(8,128)}, u32[]{:S(2)}) copy-start(f32[5,17]{1,0:T(8,128)} %param.7) | copy-start | bytes 1024
  0.0 35.1 %copy-start.1 = (f32[5,17]{1,0:T(8,128)S(1)}, f32[5,17]{1,0:T(8,128)}, u32[]{:S(2)}) copy-start(f32[5,17]{1,0:T(8,128)} %param.8) | copy-start | bytes 1024
  1.1 28.2 %collective-permute-start = (f32[8,16,512]{2,1,0:T(8,128)S(1)}, f32[8,16,512]{2,1,0:T(8,128)S(1)}, u32[]{:S(2)}, u32[]{:S(2)}) collective-permute-start(f32[8,16,512]{2,1,0:T(8,128)S(1)} %get-tuple-element.46), channel_id=1, source_target_pairs={{0,16},{16,32},{32,48},{48,64},{64,80},{80,96},{96,112},{112,128},... | collective-permute-start | bytes 786440 | tf_op jit(solution)/shard_map/ppermute | solution.py:17
  3.1 27.3 %collective-permute-start.1 = (f32[8,16,512]{2,1,0:T(8,128)S(1)}, f32[8,16,512]{2,1,0:T(8,128)S(1)}, u32[]{:S(2)}, u32[]{:S(2)}) collective-permute-start(f32[8,16,512]{2,1,0:T(8,128)S(1)} %get-tuple-element.45), channel_id=1, source_target_pairs={{16,0},{32,16},{48,32},{64,48},{80,64},{96,80},{112,96},{128,112},... | collective-permute-start | bytes 786440 | tf_op jit(solution)/shard_map/ppermute | solution.py:19
  30.5 13.6 %collective-permute-start.2 = (f32[32,8,512]{2,1,0:T(8,128)S(1)}, f32[32,8,512]{2,1,0:T(8,128)S(1)}, u32[]{:S(2)}, u32[]{:S(2)}) collective-permute-start(f32[32,8,512]{2,1,0:T(8,128)S(1)} %get-tuple-element.43), channel_id=1, source_target_pairs={{0,1},{1,2},{2,3},{3,4},{4,5},{5,6},{6,7},{7,8},{8,9},{9,10},{10,1... | collective-permute-start | bytes 1572872 | tf_op jit(solution)/shard_map/ppermute | solution.py:17
  30.6 13.8 %collective-permute-start.3 = (f32[32,8,512]{2,1,0:T(8,128)S(1)}, f32[32,8,512]{2,1,0:T(8,128)S(1)}, u32[]{:S(2)}, u32[]{:S(2)}) collective-permute-start(f32[32,8,512]{2,1,0:T(8,128)S(1)} %get-tuple-element.44), channel_id=1, source_target_pairs={{1,0},{2,1},{3,2},{4,3},{5,4},{6,5},{7,6},{8,7},{9,8},{10,9},{11,1... | collective-permute-start | bytes 1572872 | tf_op jit(solution)/shard_map/ppermute | solution.py:19
  286.5 35.1 %collective-permute-start.4 = (f32[5,8,16,512]{3,2,1,0:T(8,128)S(1)}, f32[5,8,16,512]{3,2,1,0:T(8,128)S(1)}, u32[]{:S(2)}, u32[]{:S(2)}) collective-permute-start(f32[5,8,16,512]{3,2,1,0:T(8,128)S(1)} %get-tuple-element.41), channel_id=1, source_target_pairs={{0,16},{16,32},{32,48},{48,64},{64,80},{80,96},{96,112},{112,128},... | collective-permute-start | bytes 3932168 | tf_op jit(solution)/shard_map/ppermute | solution.py:17
  286.6 35.0 %collective-permute-start.5 = (f32[5,8,16,512]{3,2,1,0:T(8,128)S(1)}, f32[5,8,16,512]{3,2,1,0:T(8,128)S(1)}, u32[]{:S(2)}, u32[]{:S(2)}) collective-permute-start(f32[5,8,16,512]{3,2,1,0:T(8,128)S(1)} %get-tuple-element.42), channel_id=1, source_target_pairs={{16,0},{32,16},{48,32},{64,48},{80,64},{96,80},{112,96},{128,112},... | collective-permute-start | bytes 3932168 | tf_op jit(solution)/shard_map/ppermute | solution.py:19
  323.2 59.4 %collective-permute-start.6 = (f32[5,32,8,512]{3,2,1,0:T(8,128)S(1)}, f32[5,32,8,512]{3,2,1,0:T(8,128)S(1)}, u32[]{:S(2)}, u32[]{:S(2)}) collective-permute-start(f32[5,32,8,512]{3,2,1,0:T(8,128)S(1)} %get-tuple-element.39), channel_id=1, source_target_pairs={{0,1},{1,2},{2,3},{3,4},{4,5},{5,6},{6,7},{7,8},{8,9},{9,10},{10,1... | collective-permute-start | bytes 7864328 | tf_op jit(solution)/shard_map/ppermute | solution.py:17
  323.4 59.2 %collective-permute-start.7 = (f32[5,32,8,512]{3,2,1,0:T(8,128)S(1)}, f32[5,32,8,512]{3,2,1,0:T(8,128)S(1)}, u32[]{:S(2)}, u32[]{:S(2)}) collective-permute-start(f32[5,32,8,512]{3,2,1,0:T(8,128)S(1)} %get-tuple-element.40), channel_id=1, source_target_pairs={{1,0},{2,1},{3,2},{4,3},{5,4},{6,5},{7,6},{8,7},{9,8},{10,9},{11,1... | collective-permute-start | bytes 7864328 | tf_op jit(solution)/shard_map/ppermute | solution.py:19
where the time goes:
time: 438 us; the launch traced here: 430 us
  matrix products  177 us (40%)
  other arithmetic  113 us (26%)
  waiting for transfers between devices  90.4 us (21%)
  local copies, waits for them, and re-layouts  29.9 us (7%)
  starting transfers between devices  19.5 us (4%)
    dot_general x5, matrix products, per_device(): jnp.dot(lowered, bands[density].T, preferred_element_type=jnp.float32)  113 us
    ppermute x4, waiting for transfers between devices, padded(): lax.ppermute(tail, axis, [(i, (i + 1) % count) for i in range(count)])  90.1 us
    add x5, other arithmetic, per_device(): along_rows + kernel_rows[density, shift_tap] * extended[shift_tap:shift_t...  64.5 us
    dot_general x5, matrix products, per_device(): flat = jnp.dot(lowered, bands[density], preferred_element_type=jnp.float32)  63.6 us
    add x1, other arithmetic, per_device(): along_rows + row_weights[:, shift_tap] * gathered[:, start:start + span_r...  35.5 us
    ppermute x4, starting transfers between devices, padded(): lax.ppermute(head, axis, [((i + 1) % count, i) for i in range(count)])  17.2 us
    slice x5, local copies, waits for them, and re-layouts, per_device(): kernel_rows[density, shift_tap] * extended[shift_tap:shift_tap + span_rows]  10.7 us
  transfers between devices with their start and end apart: 8, of which 4 were waited for; matrix products, arithmetic and copies ran while one was open for 6% of the time, Pallas kernels for 0%

commit v1 on v0

v1 whole, which is shorter than its diff:
```python
import functools

import jax
import jax.numpy as jnp
import numpy as np
from jax import lax
from jax.experimental import pallas as pl
from jax.experimental.pallas import tpu as pltpu
from jax.sharding import PartitionSpec as P

RADIUS = 8
DENSITIES = 5
TAPS = 2 * RADIUS + 1
TILE = 16
CELLS = TILE * TILE


def piece_cells():
    inner = list(range(TILE))
    outer = list(range(-RADIUS, 0)) + list(range(TILE, TILE + RADIUS))
    west, east = list(range(-RADIUS, 0)), list(range(TILE, TILE + RADIUS))
    blocks = [
        (inner, inner),
        (outer, inner),
        (inner, west),
        (inner, east),
        (outer, west),
        (outer, east),
    ]
    return blocks


def cell_arrays():
    rows, cols = [], []
    for block_rows, block_cols in piece_cells():
        for row in block_rows:
            for col in block_cols:
                rows.append(row)
                cols.append(col)
    return np.array(rows, np.int32), np.array(cols, np.int32)


def taps_at(weights, offsets):
    shape = (DENSITIES,) + (1,) * offsets.ndim
    total = jnp.zeros((DENSITIES,) + offsets.shape, jnp.float32)
    for tap in range(TAPS):
        total = jnp.where((offsets == tap - RADIUS)[None], weights[:, tap].reshape(shape), total)
    return total


def split(values):
    high = lax.reduce_precision(values, 8, 7)
    return high.astype(jnp.bfloat16), (values - high).astype(jnp.bfloat16)


def lateral_matrices(kernel_rows, kernel_cols):
    rows, cols = cell_arrays()
    tile = np.arange(TILE, dtype=np.int32)
    by_row = taps_at(kernel_rows, jnp.asarray(rows[None, :] - tile[:, None]))
    by_col = taps_at(kernel_cols, jnp.asarray(cols[None, :] - tile[:, None]))
    product = by_row[:, :, None, :] * by_col[:, None, :, :]
    return split(product.reshape(DENSITIES * CELLS, rows.size))


def lateral_transposes(kernel_rows, kernel_cols):
    span = np.arange(-RADIUS, TILE + RADIUS, dtype=np.int32)
    tile = np.repeat(np.arange(TILE, dtype=np.int32), TILE)
    tile_cols = np.tile(np.arange(TILE, dtype=np.int32), TILE)
    by_row = taps_at(kernel_rows, jnp.asarray(span[:, None] - tile[None, :]))
    by_col = taps_at(kernel_cols, jnp.asarray(span[:, None] - tile_cols[None, :]))
    by_row = jnp.moveaxis(by_row, 0, 1).reshape(span.size, DENSITIES * CELLS)
    by_col = jnp.moveaxis(by_col, 0, 1).reshape(span.size, DENSITIES * CELLS)
    parts = []
    for block_rows, block_cols in piece_cells():
        low, high = block_cols[0] + RADIUS, block_cols[-1] + RADIUS + 1
        if block_rows[0] == 0:
            chosen = by_row[RADIUS : RADIUS + TILE]
        else:
            chosen = jnp.concatenate([by_row[:RADIUS], by_row[RADIUS + TILE :]], 0)
        product = chosen[:, None, :] * by_col[None, low:high, :]
        parts.append(product.reshape(-1, DENSITIES * CELLS))
    return split(jnp.concatenate(parts, 0))


def depth_bands(kernel_depth, depth):
    weights = kernel_depth.astype(jnp.float32)
    block = 128
    span = np.arange(3 * block)[None, :] - block - np.arange(block)[:, None]
    count = depth // block
    out = []
    for sign in (-1, 1):
        window = taps_at(weights, jnp.asarray((sign * span).astype(np.int32))).astype(jnp.bfloat16)
        rows = []
        for index in range(count):
            low, high = (index - 1) * block, (index + 2) * block
            part = window[:, :, max(0, -low) : 3 * block - max(0, high - depth)]
            rows.append(
                jnp.pad(part, ((0, 0), (0, 0), (max(0, low), max(0, depth - high))))
            )
        out.append(jnp.concatenate(rows, 1))
    return out


def halves(values):
    high = values.astype(jnp.bfloat16)
    return high, (values - high.astype(jnp.float32)).astype(jnp.bfloat16)


def dot3(left_high, left_low, right_high, right_low):
    left = jnp.concatenate([left_high, left_low, left_high], 1)
    right = jnp.concatenate([right_high, right_high, right_low], 0)
    return jnp.dot(left, right, preferred_element_type=jnp.float32)


def near_kernel(own, north, south, west, east, wh, wl, out, xh, xl):
    @pl.when(pl.program_id(0) == 0)
    def _():
        depth = own.shape[-1]
        start = 0
        for ref in (own, north, south, west, east):
            size = ref.shape[0] * ref.shape[1]
            high, low = halves(ref[...].reshape(size, depth))
            xh[start : start + size] = high
            xl[start : start + size] = low
            start += size

    out[...] = dot3(wh[...], wl[...], xh[...], xl[...])


def near(pieces, wh, wl):
    depth = pieces[0].shape[-1]
    keys = 3 * CELLS
    whole = lambda a: pl.BlockSpec(a.shape, lambda i: (0,) * a.ndim)
    weights = pl.BlockSpec((CELLS, keys), lambda i: (i, 0))
    return pl.pallas_call(
        near_kernel,
        grid=(DENSITIES,),
        out_shape=jax.ShapeDtypeStruct((DENSITIES * CELLS, depth), jnp.float32),
        in_specs=[whole(a) for a in pieces] + [weights, weights],
        out_specs=pl.BlockSpec((CELLS, depth), lambda i: (i, 0)),
        scratch_shapes=[pltpu.VMEM((keys, depth), jnp.bfloat16)] * 2,
        compiler_params=pltpu.CompilerParams(vmem_limit_bytes=32 << 20),
        cost_estimate=pl.CostEstimate(
            flops=6 * DENSITIES * CELLS * keys * depth, bytes_accessed=10 << 20, transcendentals=0
        ),
        name="near",
    )(*pieces, wh, wl)


def middle_kernel(
    partial, corner_w, corner_e, wh, wl, hessian, bands, bands_t, th, tl, out_w, out_e, bh, bl, xh, xl, dens, low
):
    depth = partial.shape[-1]
    half = CELLS // 2
    for start, ref in ((0, corner_w), (half, corner_e)):
        high, rest = halves(ref[...].reshape(half, depth))
        xh[start : start + half] = high
        xl[start : start + half] = rest
    for b in range(DENSITIES):
        rows = slice(b * CELLS, (b + 1) * CELLS)
        lateral = partial[rows] + dot3(wh[rows], wl[rows], xh[...], xl[...])
        dens[b] = jnp.dot(lateral.astype(jnp.bfloat16), bands[b], preferred_element_type=jnp.float32)
    total = None
    for a in range(DENSITIES):
        for r in range(TILE):
            cells = slice(r * TILE, (r + 1) * TILE)
            grad = hessian[a, 0, r].astype(jnp.float32) * dens[0, cells]
            for b in range(1, DENSITIES):
                grad = grad + hessian[a, b, r].astype(jnp.float32) * dens[b, cells]
            low[a, cells] = grad.astype(jnp.bfloat16)
        back = jnp.dot(low[a], bands_t[a], preferred_element_type=jnp.float32)
        rows = slice(a * CELLS, (a + 1) * CELLS)
        high, rest = halves(back)
        bh[rows] = high
        bl[rows] = rest
        term = dot3(th[:, rows], tl[:, rows], high, rest)
        total = term if total is None else total + term
    out_w[...] = total[:half].reshape(out_w.shape)
    out_e[...] = total[half:].reshape(out_e.shape)


def middle(partial, corner_w, corner_e, wh, wl, hessian, bands, bands_t, th, tl):
    depth = partial.shape[-1]
    edge = jax.ShapeDtypeStruct(corner_w.shape, jnp.float32)
    back = jax.ShapeDtypeStruct((DENSITIES * CELLS, depth), jnp.bfloat16)
    vmem = pl.BlockSpec(memory_space=pltpu.VMEM)
    return pl.pallas_call(
        middle_kernel,
        out_shape=[edge, edge, back, back],
        in_specs=[vmem] * 10,
        out_specs=[vmem] * 4,
        scratch_shapes=[
            pltpu.VMEM((CELLS, depth), jnp.bfloat16),
            pltpu.VMEM((CELLS, depth), jnp.bfloat16),
            pltpu.VMEM((DENSITIES, CELLS, depth), jnp.float32),
            pltpu.VMEM((DENSITIES, CELLS, depth), jnp.bfloat16),
        ],
        compiler_params=pltpu.CompilerParams(vmem_limit_bytes=48 << 20),
        cost_estimate=pl.CostEstimate(
            flops=DENSITIES * CELLS * depth * (12 * CELLS + 4 * depth), bytes_accessed=16 << 20, transcendentals=0
        ),
        name="middle",
    )(partial, corner_w, corner_e, wh, wl, hessian, bands, bands_t, th, tl)


def spread_kernel(th, tl, bh, bl, *outs):
    total = dot3(th[...], tl[...], bh[...], bl[...])
    start = 0
    for out in outs:
        size = out.shape[0] * out.shape[1]
        out[...] = total[start : start + size].reshape(out.shape)
        start += size


def spread(th, tl, bh, bl, shapes):
    depth = bh.shape[-1]
    vmem = pl.BlockSpec(memory_space=pltpu.VMEM)
    return pl.pallas_call(
        spread_kernel,
        out_shape=[jax.ShapeDtypeStruct(s + (depth,), jnp.float32) for s in shapes],
        in_specs=[vmem] * 4,
        out_specs=[vmem] * len(shapes),
        compiler_params=pltpu.CompilerParams(vmem_limit_bytes=32 << 20),
        cost_estimate=pl.CostEstimate(
            flops=6 * th.shape[0] * th.shape[1] * depth, bytes_accessed=6 << 20, transcendentals=0
        ),
        name="spread",
    )(th, tl, bh, bl)


def shift(cells, axis, step):
    count = lax.axis_size(axis)
    return lax.ppermute(cells, axis, [(i, (i + step) % count) for i in range(count)])


def per_device(tangent, hessian, kernel_rows, kernel_cols, kernel_depth):
    span_rows, span_cols, depth = tangent.shape
    reach = RADIUS

    north = shift(tangent[reach:], "gx", 1)
    south = shift(tangent[:reach], "gx", -1)
    west = shift(tangent[:, reach:], "gy", 1)
    east = shift(tangent[:, :reach], "gy", -1)

    wh, wl = lateral_matrices(kernel_rows, kernel_cols)
    th, tl = lateral_transposes(kernel_rows, kernel_cols)
    bands, bands_t = depth_bands(kernel_depth, depth)

    sides = jnp.concatenate([north, south], 0)
    corner_w = shift(sides[:, reach:], "gy", 1)
    corner_e = shift(sides[:, :reach], "gy", -1)

    inner, outer = slice(0, 3 * CELLS), slice(3 * CELLS, 4 * CELLS)
    partial = near((tangent, north, south, west, east), wh[:, inner], wl[:, inner])
    to_w, to_e, bh, bl = middle(
        partial, corner_w, corner_e, wh[:, outer], wl[:, outer], hessian, bands, bands_t, th[outer], tl[outer]
    )
    from_e = shift(to_w, "gy", -1)
    from_w = shift(to_e, "gy", 1)

    sides = slice(2 * CELLS, 3 * CELLS)
    edge_w, edge_e = spread(th[sides], tl[sides], bh, bl, [(span_rows, reach)] * 2)
    edge_from_e = shift(edge_w, "gy", -1)
    edge_from_w = shift(edge_e, "gy", 1)

    rest = slice(0, 2 * CELLS)
    own, around = spread(th[rest], tl[rest], bh, bl, [(span_rows, span_cols)] * 2)
    around = around + jnp.concatenate([from_w, from_e], 1)
    side_from_s = shift(around[:reach], "gx", -1)
    side_from_n = shift(around[reach:], "gx", 1)
    own = own + jnp.concatenate([edge_from_w, edge_from_e], 1)
    return own + jnp.concatenate([side_from_n, side_from_s], 0)


def solution(mesh):
    return jax.shard_map(
        per_device,
        mesh=mesh,
        in_specs=(P("gx", "gy", None), P(None, None, "gx", "gy", None), P(), P(), P()),
        out_specs=P("gx", "gy", None),
        check_vma=False,
    )
```

time: 438 us -> 90.6 us (0.21)
  the two profiles are of different devices: /device:TPU:4 before, /device:TPU:0 now
where the time goes in v1:
time: 90.6 us; the launch traced here: 89.6 us
  starting transfers between devices  22.8 us (25%)
  local copies, waits for them, and re-layouts  22.7 us (25%)
  Pallas kernels  18.5 us (20%)
  other arithmetic  12.6 us (14%)
  waiting for transfers between devices  11.4 us (13%)
  between operations  1.62 us (2%)
    ppermute x12, starting transfers between devices, shift(): lax.ppermute(cells, axis, [(i, (i + step) % count) for i in range(count)])  22.8 us
    unnamed x202, local copies, waits for them, and re-layouts  16 us
    ppermute x12, waiting for transfers between devices, shift(): lax.ppermute(cells, axis, [(i, (i + step) % count) for i in range(count)])  11.4 us
    pallas_call x1, Pallas kernels, middle(): pl.pallas_call(middle_kernel, out_shape=[edge, edge, back, back], in_spec...  11 us
    pallas_call x1, Pallas kernels, near(): pl.pallas_call(near_kernel, grid=(DENSITIES,), out_shape=jax.ShapeDtypeSt...  4.15 us
    pallas_call x2, Pallas kernels, spread(): pl.pallas_call(spread_kernel, out_shape=[jax.ShapeDtypeStruct(s + (depth,...  3.35 us
    concatenate x1, other arithmetic, depth_bands(): out.append(jnp.concatenate(rows, 1))  3.32 us
    slice x3, local copies, waits for them, and re-layouts, taps_at(): weights[:, tap].reshape(shape)  3.24 us
  transfers between devices with their start and end apart: 12, of which 5 were waited for; matrix products, arithmetic and copies ran while one was open for 33% of the time, Pallas kernels for 8%

profile of v1, /device:TPU:0, one launch (start us, length us, event | category | flops | bytes accessed | tf_op | source)
XLA Modules:
  0.0 89.6 jit_solution(12683022973315513609)
XLA Ops:
  0.4 1.3 %fusion.24 = (f32[8,16,512]{2,1,0:T(8,128)S(1)}, f32[8,16,512]{2,1,0:T(8,128)S(1)}) fusion(f32[16,16,512]{2,1,0:T(8,128)} %own.1), kind=kLoop, calls=%fused_computation.107 | loop fusion | bytes 1048576 | tf_op jit(solution)/shard_map/slice | solution.py:241
  1.9 6.5 %collective-permute-start.1 = (f32[8,16,512]{2,1,0:T(8,128)S(1)}, f32[8,16,512]{2,1,0:T(8,128)S(1)}, u32[]{:S(2)}, u32[]{:S(2)}) collective-permute-start(f32[8,16,512]{2,1,0:T(8,128)S(1)} %get-tuple-element.86), channel_id=1, source_target_pairs={{0,240},{16,0},{32,16},{48,32},{64,48},{80,64},{96,80},{112,96},{1... | collective-permute-start | bytes 786440 | tf_op jit(solution)/shard_map/ppermute | solution.py:233
  8.4 1.1 %fusion.23 = (f32[16,8,512]{2,1,0:T(8,128)S(1)}, f32[16,8,512]{2,1,0:T(8,128)S(1)}) fusion(f32[16,16,512]{2,1,0:T(8,128)} %own.1), kind=kLoop, calls=%fused_computation.106 | loop fusion | bytes 1048576 | tf_op jit(solution)/shard_map/slice | solution.py:243
  9.6 3.8 %collective-permute-start.3 = (f32[16,8,512]{2,1,0:T(8,128)S(1)}, f32[16,8,512]{2,1,0:T(8,128)S(1)}, u32[]{:S(2)}, u32[]{:S(2)}) collective-permute-start(f32[16,8,512]{2,1,0:T(8,128)S(1)} %get-tuple-element.84), channel_id=1, source_target_pairs={{0,15},{1,0},{2,1},{3,2},{4,3},{5,4},{6,5},{7,6},{8,7},{9,8},{10,9... | collective-permute-start | bytes 786440 | tf_op jit(solution)/shard_map/ppermute | solution.py:233
  13.4 2.3 %slice_reduce_fusion.50 = (f32[5]{0:T(128)S(1)}, f32[5]{0:T(128)S(1)}, f32[5]{0:T(128)S(1)}, f32[5]{0:T(128)S(1)}, f32[5]{0:T(128)S(1)}, /*index=5*/f32[5]{0:T(1...) fusion(f32[5,17]{1,0:T(8,128)} %param.13), kind=kLoop, calls=%fused_computation.101 | loop fusion | bytes 680 | tf_op jit(solution)/shard_map/slice | solution.py:47
  15.7 0.7 copy.24
  16.4 0.7 copy.25
  17.1 0.7 copy.26
  17.8 0.7 copy.27
  18.5 0.7 copy.28
  19.2 0.7 copy.29
  19.9 0.7 copy.30
  20.6 0.7 copy.31
  21.3 0.7 copy.32
  22.0 0.7 copy.33
  22.7 0.7 copy.34
  23.4 0.7 copy.35
  24.1 0.7 copy.36
  24.8 0.7 copy.37
  25.5 0.7 copy.38
  26.2 0.7 copy.39
  26.9 0.7 copy.40
  28.0 0.5 slice_reduce_fusion.33
  29.3 0.5 slice_reduce_fusion.16
  30.4 1.6 %select_convert_fusion.1 = bf16[5,128,384]{2,1,0:T(8,128)(2,1)S(1)} fusion(bf16[5]{0:T(256)(128)(2,1)S(1)} %get-tuple-element.22, bf16[5]{0:T(256)(128)(2,1)S(1)} %get-tuple-element.23, bf16[5]{0:T(256)(128)(2,1)S(1)} %get-tuple-element.24, bf16[5]{0:T(256)(128)(2,1)S(1)} %get-tuple-element.25, bf16[5]{0:T(256)(128)(2,1)S(1)} %get-tuple-element.26, ...), kind=kLoop, calls=%fused_computation.30 | loop fusion | flops 4177920 | bytes 1327274 | tf_op jit(solution)/shard_map/convert_element_type | solution.py:92
  32.0 1.6 %select_convert_fusion = bf16[5,128,384]{2,1,0:T(8,128)(2,1)S(1)} fusion(bf16[5]{0:T(256)(128)(2,1)S(1)} %get-tuple-element.22, bf16[5]{0:T(256)(128)(2,1)S(1)} %get-tuple-element.23, bf16[5]{0:T(256)(128)(2,1)S(1)} %get-tuple-element.24, bf16[5]{0:T(256)(128)(2,1)S(1)} %get-tuple-element.25, bf16[5]{0:T(256)(128)(2,1)S(1)} %get-tuple-element.26, ...), kind=kLoop, calls=%fused_computation.29 | loop fusion | flops 4177920 | bytes 1327274 | tf_op jit(solution)/shard_map/convert_element_type | solution.py:92
  34.7 0.8 fusion
  35.7 0.7 select_select_fusion
  36.6 0.7 select_select_fusion.1
  37.2 0.8 broadcast_multiply_fusion
  38.0 1.0 %fusion.1 = (bf16[1280,1024]{1,0:T(8,128)(2,1)S(1)}, bf16[1280,1024]{1,0:T(8,128)(2,1)S(1)}) fusion(f32[5,16,16,1024]{3,2,1,0:T(8,128)S(1)} %broadcast_multiply_fusion), kind=kLoop, calls=%fused_computation.9 | loop fusion | flops 5242880 | bytes 10485760 | tf_op jit(solution)/shard_map/convert_element_type | solution.py:53
  39.2 3.3 %fusion.14 = (bf16[5,512,512]{2,1,0:T(8,128)(2,1)}, bf16[5,512,512]{2,1,0:T(8,128)(2,1)}) fusion(bf16[5,128,256]{2,1,0:T(8,128)(2,1)S(1)} %get-tuple-element.91, bf16[5,128,384]{2,1,0:T(8,128)(2,1)S(1)} %select_convert_fusion.1, bf16[5,128,256]{2,1,0:T(8,128)(2,1)S(1)} %get-tuple-element.90, bf16[5,128,256]{2,1,0:T(8,128)(2,1)S(1)} %get-tuple-element.89, ...), kind=kLoop, calls=%fused_computation.24 | loop fusion | flops 41943040 | bytes 7536640 | tf_op jit(solution)/shard_map/concatenate | solution.py:100
  43.9 3.8 %collective-permute-start.5 = (f32[16,8,512]{2,1,0:T(8,128)S(1)}, f32[16,8,512]{2,1,0:T(8,128)S(1)}, u32[]{:S(2)}, u32[]{:S(2)}) collective-permute-start(f32[16,8,512]{2,1,0:T(8,128)S(1)} %get-tuple-element.82), channel_id=1, source_target_pairs={{0,15},{1,0},{2,1},{3,2},{4,3},{5,4},{6,5},{7,6},{8,7},{9,8},{10,9... | collective-permute-start | bytes 786440 | tf_op jit(solution)/shard_map/ppermute | solution.py:233
  47.7 4.2 %near.1.partial = f32[1280,512]{1,0:T(8,128)S(1)} custom-call(f32[16,16,512]{2,1,0:T(8,128)S(1)} %copy-done.1, f32[8,16,512]{2,1,0:T(8,128)S(1)} %collective-permute-done.north, f32[8,16,512]{2,1,0:T(8,128)S(1)} %collective-permute-done.1.south, f32[16,8,512]{2,1,0:T(8,128)S(1)} %collective-permute-done.2.west, ...), custom_call_target="tpu_custom_call" | custom-call | flops 3019898880 | bytes 10485760 | tf_op jit(solution)/shard_map/near/pallas_call | solution.py:135
  51.9 1.5 %copy-done = f32[1280,512]{1,0:T(8,128)} copy-done((f32[1280,512]{1,0:T(8,128)}, f32[1280,512]{1,0:T(8,128)S(1)}, u32[]{:S(2)}) %copy-start) | copy-done | bytes 2621464
  53.7 11.0 %middle.1 = (f32[16,8,512]{2,1,0:T(8,128)S(1)}, f32[16,8,512]{2,1,0:T(8,128)S(1)}, bf16[1280,512]{1,0:T(8,128)(2,1)S(1)}, bf16[1280,512]{1,0:T(8,128)(2,1)}) custom-call(f32[1280,512]{1,0:T(8,128)} %copy-done, f32[16,8,512]{2,1,0:T(8,128)S(1)} %collective-permute-done.4.corner_w, f32[16,8,512]{2,1,0:T(8,128)S(1)} %collective-permute-done.5.corner_e, ...), custom_call_target="tpu_custom_call" | custom-call | flops 3355443200 | bytes 16777216 | tf_op jit(solution)/shard_map/middle/pallas_call | solution.py:187
  64.7 1.9 %collective-permute-start.9 = (f32[16,8,512]{2,1,0:T(8,128)S(1)}, f32[16,8,512]{2,1,0:T(8,128)S(1)}, u32[]{:S(2)}, u32[]{:S(2)}) collective-permute-start(f32[16,8,512]{2,1,0:T(8,128)S(1)} %get-tuple-element.20), channel_id=1, source_target_pairs={{0,15},{1,0},{2,1},{3,2},{4,3},{5,4},{6,5},{7,6},{8,7},{9,8},{10,9... | collective-permute-start | bytes 786440 | tf_op jit(solution)/shard_map/ppermute | solution.py:233
  66.7 1.3 %copy-done.2 = bf16[1280,512]{1,0:T(8,128)(2,1)S(1)} copy-done((bf16[1280,512]{1,0:T(8,128)(2,1)S(1)}, bf16[1280,512]{1,0:T(8,128)(2,1)}, u32[]{:S(2)}) %copy-start.2) | copy-done | bytes 1310744
  68.0 1.2 %spread.3 = (f32[16,8,512]{2,1,0:T(8,128)S(1)}, f32[16,8,512]{2,1,0:T(8,128)S(1)}) custom-call(bf16[256,1280]{1,0:T(8,128)(2,1)S(1)} %get-tuple-element.99.th, bf16[256,1280]{1,0:T(8,128)(2,1)S(1)} %get-tuple-element.76.tl, bf16[1280,512]{1,0:T(8,128)(2,1)S(1)} %get-tuple-element.13.bh, bf16[1280,512]{1,0:T(8,128)(2,1)S(1)} %copy-done.2), custom_call_target="tpu_custom_call" | custom-call | flops 1006632960 | bytes 6291456 | tf_op jit(solution)/shard_map/spread/pallas_call | solution.py:218
  69.1 3.9 %collective-permute-start.7 = (f32[16,8,512]{2,1,0:T(8,128)S(1)}, f32[16,8,512]{2,1,0:T(8,128)S(1)}, u32[]{:S(2)}, u32[]{:S(2)}) collective-permute-start(f32[16,8,512]{2,1,0:T(8,128)S(1)} %get-tuple-element.17), channel_id=1, source_target_pairs={{0,15},{1,0},{2,1},{3,2},{4,3},{5,4},{6,5},{7,6},{8,7},{9,8},{10,9... | collective-permute-start | bytes 786440 | tf_op jit(solution)/shard_map/ppermute | solution.py:233
  73.1 2.2 %spread.2 = (f32[16,16,512]{2,1,0:T(8,128)S(1)}, f32[16,16,512]{2,1,0:T(8,128)S(1)}) custom-call(bf16[512,1280]{1,0:T(8,128)(2,1)S(1)} %slice.394.th, bf16[512,1280]{1,0:T(8,128)(2,1)S(1)} %slice.395.tl, bf16[1280,512]{1,0:T(8,128)(2,1)S(1)} %get-tuple-element.13.bh, bf16[1280,512]{1,0:T(8,128)(2,1)S(1)} %copy-done.2), custom_call_target="tpu_custom_call" | custom-call | flops 2013265920 | bytes 6291456 | tf_op jit(solution)/shard_map/spread/pallas_call | solution.py:218
  75.3 1.8 %collective-permute-done.8 = f32[16,8,512]{2,1,0:T(8,128)S(1)} collective-permute-done((f32[16,8,512]{2,1,0:T(8,128)S(1)}, f32[16,8,512]{2,1,0:T(8,128)S(1)}, u32[]{:S(2)}, u32[]{:S(2)}) %collective-permute-start.8) | collective-permute-done | bytes 262176 | tf_op jit(solution)/shard_map/ppermute | solution.py:233
  77.2 1.4 %collective-permute-start.11 = (f32[8,16,512]{2,1,0:T(8,128)S(1)}, f32[8,16,512]{2,1,0:T(8,128)S(1)}, u32[]{:S(2)}, u32[]{:S(2)}) collective-permute-start(f32[8,16,512]{2,1,0:T(8,128)S(1)} %get-tuple-element.81), channel_id=1, source_target_pairs={{0,240},{16,0},{32,16},{48,32},{64,48},{80,64},{96,80},{112,96},{1... | collective-permute-start | bytes 786440 | tf_op jit(solution)/shard_map/ppermute | solution.py:233
  78.6 0.7 collective-permute-start.10
  79.3 1.6 %collective-permute-done.6 = f32[16,8,512]{2,1,0:T(8,128)S(1)} collective-permute-done((f32[16,8,512]{2,1,0:T(8,128)S(1)}, f32[16,8,512]{2,1,0:T(8,128)S(1)}, u32[]{:S(2)}, u32[]{:S(2)}) %collective-permute-start.6) | collective-permute-done | bytes 262176 | tf_op jit(solution)/shard_map/ppermute | solution.py:233
  81.0 2.7 %collective-permute-done.11 = f32[8,16,512]{2,1,0:T(8,128)S(1)} collective-permute-done((f32[8,16,512]{2,1,0:T(8,128)S(1)}, f32[8,16,512]{2,1,0:T(8,128)S(1)}, u32[]{:S(2)}, u32[]{:S(2)}) %collective-permute-start.11) | collective-permute-done | bytes 262176 | tf_op jit(solution)/shard_map/ppermute | solution.py:233
  83.7 5.0 %collective-permute-done.10 = f32[8,16,512]{2,1,0:T(8,128)S(1)} collective-permute-done((f32[8,16,512]{2,1,0:T(8,128)S(1)}, f32[8,16,512]{2,1,0:T(8,128)S(1)}, u32[]{:S(2)}, u32[]{:S(2)}) %collective-permute-start.10) | collective-permute-done | bytes 262176 | tf_op jit(solution)/shard_map/ppermute | solution.py:233
  88.6 1.0 %fusion.18 = f32[16,16,512]{2,1,0:T(8,128)} fusion(f32[16,16,512]{2,1,0:T(8,128)S(1)} %get-tuple-element.15, f32[16,8,512]{2,1,0:T(8,128)S(1)} %collective-permute-done.7, f32[16,8,512]{2,1,0:T(8,128)S(1)} %collective-permute-done.6, f32[8,16,512]{2,1,0:T(8,128)S(1)} %collective-permute-done.11, f32[8,16,512]{2,1,0:T(8,128)S(1)} %collective-permute-done.10), kind=kLoop, calls=%fused_computation.38 | loop fusion | flops 524288 | bytes 2097152 | tf_op jit(solution)/shard_map/add | solution.py:272
  (222 shorter events, 4.5 us)
Async XLA Ops:
  0.0 28.5 %copy-start.71 = (pred[32,256]{1,0:T(32,128)(4,1)S(1)}, pred[32,256]{1,0:T(32,128)(4,1)}, u32[]{:S(2)}) copy-start(pred[32,256]{1,0:T(32,128)(4,1)} %constant.142) | copy-start | bytes 24580
  0.0 28.5 %copy-start.70 = (pred[32,256]{1,0:T(32,128)(4,1)S(1)}, pred[32,256]{1,0:T(32,128)(4,1)}, u32[]{:S(2)}) copy-start(pred[32,256]{1,0:T(32,128)(4,1)} %constant.141) | copy-start | bytes 24580
  0.0 28.5 %copy-start.69 = (pred[32,256]{1,0:T(32,128)(4,1)S(1)}, pred[32,256]{1,0:T(32,128)(4,1)}, u32[]{:S(2)}) copy-start(pred[32,256]{1,0:T(32,128)(4,1)} %constant.140) | copy-start | bytes 24580
  0.0 28.5 %copy-start.68 = (pred[32,256]{1,0:T(32,128)(4,1)S(1)}, pred[32,256]{1,0:T(32,128)(4,1)}, u32[]{:S(2)}) copy-start(pred[32,256]{1,0:T(32,128)(4,1)} %constant.139) | copy-start | bytes 24580
  0.0 28.6 %copy-start.67 = (pred[32,256]{1,0:T(32,128)(4,1)S(1)}, pred[32,256]{1,0:T(32,128)(4,1)}, u32[]{:S(2)}) copy-start(pred[32,256]{1,0:T(32,128)(4,1)} %constant.138) | copy-start | bytes 24580
  0.0 28.6 %copy-start.66 = (pred[32,256]{1,0:T(32,128)(4,1)S(1)}, pred[32,256]{1,0:T(32,128)(4,1)}, u32[]{:S(2)}) copy-start(pred[32,256]{1,0:T(32,128)(4,1)} %constant.137) | copy-start | bytes 24580
  0.0 28.6 %copy-start.65 = (pred[32,256]{1,0:T(32,128)(4,1)S(1)}, pred[32,256]{1,0:T(32,128)(4,1)}, u32[]{:S(2)}) copy-start(pred[32,256]{1,0:T(32,128)(4,1)} %constant.136) | copy-start | bytes 24580
  0.0 28.6 %copy-start.64 = (pred[32,256]{1,0:T(32,128)(4,1)S(1)}, pred[32,256]{1,0:T(32,128)(4,1)}, u32[]{:S(2)}) copy-start(pred[32,256]{1,0:T(32,128)(4,1)} %constant.135) | copy-start | bytes 24580
  0.1 28.6 %copy-start.63 = (pred[32,256]{1,0:T(32,128)(4,1)S(1)}, pred[32,256]{1,0:T(32,128)(4,1)}, u32[]{:S(2)}) copy-start(pred[32,256]{1,0:T(32,128)(4,1)} %constant.134) | copy-start | bytes 24580
  0.1 28.6 %copy-start.62 = (pred[32,256]{1,0:T(32,128)(4,1)S(1)}, pred[32,256]{1,0:T(32,128)(4,1)}, u32[]{:S(2)}) copy-start(pred[32,256]{1,0:T(32,128)(4,1)} %constant.133) | copy-start | bytes 24580
  0.1 28.6 %copy-start.61 = (pred[32,256]{1,0:T(32,128)(4,1)S(1)}, pred[32,256]{1,0:T(32,128)(4,1)}, u32[]{:S(2)}) copy-start(pred[32,256]{1,0:T(32,128)(4,1)} %constant.132) | copy-start | bytes 24580
  0.1 28.6 %copy-start.60 = (pred[32,256]{1,0:T(32,128)(4,1)S(1)}, pred[32,256]{1,0:T(32,128)(4,1)}, u32[]{:S(2)}) copy-start(pred[32,256]{1,0:T(32,128)(4,1)} %constant.131) | copy-start | bytes 24580
  0.1 28.7 %copy-start.59 = (pred[32,256]{1,0:T(32,128)(4,1)S(1)}, pred[32,256]{1,0:T(32,128)(4,1)}, u32[]{:S(2)}) copy-start(pred[32,256]{1,0:T(32,128)(4,1)} %constant.130) | copy-start | bytes 24580
  0.1 28.7 %copy-start.58 = (pred[32,256]{1,0:T(32,128)(4,1)S(1)}, pred[32,256]{1,0:T(32,128)(4,1)}, u32[]{:S(2)}) copy-start(pred[32,256]{1,0:T(32,128)(4,1)} %constant.129) | copy-start | bytes 24580
  0.1 28.7 %copy-start.57 = (pred[32,256]{1,0:T(32,128)(4,1)S(1)}, pred[32,256]{1,0:T(32,128)(4,1)}, u32[]{:S(2)}) copy-start(pred[32,256]{1,0:T(32,128)(4,1)} %constant.128) | copy-start | bytes 24580
  0.1 28.7 %copy-start.56 = (pred[32,256]{1,0:T(32,128)(4,1)S(1)}, pred[32,256]{1,0:T(32,128)(4,1)}, u32[]{:S(2)}) copy-start(pred[32,256]{1,0:T(32,128)(4,1)} %constant.127) | copy-start | bytes 24580
  0.2 28.7 %copy-start.55 = (pred[32,256]{1,0:T(32,128)(4,1)S(1)}, pred[32,256]{1,0:T(32,128)(4,1)}, u32[]{:S(2)}) copy-start(pred[32,256]{1,0:T(32,128)(4,1)} %constant.126) | copy-start | bytes 24580
  0.2 29.6 %copy-start.20 = (pred[128,384]{1,0:T(32,128)(4,1)S(1)}, pred[128,384]{1,0:T(32,128)(4,1)}, u32[]{:S(2)}) copy-start(pred[128,384]{1,0:T(32,128)(4,1)} %constant.193) | copy-start | bytes 147460
  0.2 29.6 %copy-start.19 = (pred[128,384]{1,0:T(32,128)(4,1)S(1)}, pred[128,384]{1,0:T(32,128)(4,1)}, u32[]{:S(2)}) copy-start(pred[128,384]{1,0:T(32,128)(4,1)} %constant.192) | copy-start | bytes 147460
  0.2 29.7 %copy-start.18 = (pred[128,384]{1,0:T(32,128)(4,1)S(1)}, pred[128,384]{1,0:T(32,128)(4,1)}, u32[]{:S(2)}) copy-start(pred[128,384]{1,0:T(32,128)(4,1)} %constant.191) | copy-start | bytes 147460
  0.2 29.7 %copy-start.17 = (pred[128,384]{1,0:T(32,128)(4,1)S(1)}, pred[128,384]{1,0:T(32,128)(4,1)}, u32[]{:S(2)}) copy-start(pred[128,384]{1,0:T(32,128)(4,1)} %constant.190) | copy-start | bytes 147460
  0.2 29.7 %copy-start.16 = (pred[128,384]{1,0:T(32,128)(4,1)S(1)}, pred[128,384]{1,0:T(32,128)(4,1)}, u32[]{:S(2)}) copy-start(pred[128,384]{1,0:T(32,128)(4,1)} %constant.189) | copy-start | bytes 147460
  0.2 29.7 %copy-start.15 = (pred[128,384]{1,0:T(32,128)(4,1)S(1)}, pred[128,384]{1,0:T(32,128)(4,1)}, u32[]{:S(2)}) copy-start(pred[128,384]{1,0:T(32,128)(4,1)} %constant.188) | copy-start | bytes 147460
  0.2 29.8 %copy-start.14 = (pred[128,384]{1,0:T(32,128)(4,1)S(1)}, pred[128,384]{1,0:T(32,128)(4,1)}, u32[]{:S(2)}) copy-start(pred[128,384]{1,0:T(32,128)(4,1)} %constant.187) | copy-start | bytes 147460
  0.3 29.8 %copy-start.13 = (pred[128,384]{1,0:T(32,128)(4,1)S(1)}, pred[128,384]{1,0:T(32,128)(4,1)}, u32[]{:S(2)}) copy-start(pred[128,384]{1,0:T(32,128)(4,1)} %constant.186) | copy-start | bytes 147460
  0.3 29.8 %copy-start.12 = (pred[128,384]{1,0:T(32,128)(4,1)S(1)}, pred[128,384]{1,0:T(32,128)(4,1)}, u32[]{:S(2)}) copy-start(pred[128,384]{1,0:T(32,128)(4,1)} %constant.185) | copy-start | bytes 147460
  0.3 29.8 %copy-start.11 = (pred[128,384]{1,0:T(32,128)(4,1)S(1)}, pred[128,384]{1,0:T(32,128)(4,1)}, u32[]{:S(2)}) copy-start(pred[128,384]{1,0:T(32,128)(4,1)} %constant.184) | copy-start | bytes 147460
  0.3 29.9 %copy-start.10 = (pred[128,384]{1,0:T(32,128)(4,1)S(1)}, pred[128,384]{1,0:T(32,128)(4,1)}, u32[]{:S(2)}) copy-start(pred[128,384]{1,0:T(32,128)(4,1)} %constant.183) | copy-start | bytes 147460
  0.3 29.9 %copy-start.9 = (pred[128,384]{1,0:T(32,128)(4,1)S(1)}, pred[128,384]{1,0:T(32,128)(4,1)}, u32[]{:S(2)}) copy-start(pred[128,384]{1,0:T(32,128)(4,1)} %constant.182) | copy-start | bytes 147460
  0.3 29.9 %copy-start.8 = (pred[128,384]{1,0:T(32,128)(4,1)S(1)}, pred[128,384]{1,0:T(32,128)(4,1)}, u32[]{:S(2)}) copy-start(pred[128,384]{1,0:T(32,128)(4,1)} %constant.181) | copy-start | bytes 147460
  0.3 30.0 %copy-start.7 = (pred[128,384]{1,0:T(32,128)(4,1)S(1)}, pred[128,384]{1,0:T(32,128)(4,1)}, u32[]{:S(2)}) copy-start(pred[128,384]{1,0:T(32,128)(4,1)} %constant.180) | copy-start | bytes 147460
  0.3 30.0 %copy-start.6 = (pred[128,384]{1,0:T(32,128)(4,1)S(1)}, pred[128,384]{1,0:T(32,128)(4,1)}, u32[]{:S(2)}) copy-start(pred[128,384]{1,0:T(32,128)(4,1)} %constant.179) | copy-start | bytes 147460
  0.4 30.0 %copy-start.5 = (pred[128,384]{1,0:T(32,128)(4,1)S(1)}, pred[128,384]{1,0:T(32,128)(4,1)}, u32[]{:S(2)}) copy-start(pred[128,384]{1,0:T(32,128)(4,1)} %constant.178) | copy-start | bytes 147460
  0.4 27.6 %copy-start.3 = (f32[5,17]{1,0:T(8,128)S(1)}, f32[5,17]{1,0:T(8,128)}, u32[]{:S(2)}) copy-start(f32[5,17]{1,0:T(8,128)} %param.14) | copy-start | bytes 1024
  0.4 28.9 %copy-start.72 = (bf16[5,17]{1,0:T(8,128)(2,1)S(1)}, bf16[5,17]{1,0:T(8,128)(2,1)}, u32[]{:S(2)}) copy-start(bf16[5,17]{1,0:T(8,128)(2,1)} %param.15) | copy-start | bytes 514
  1.7 28.7 %copy-start.4 = (pred[128,384]{1,0:T(32,128)(4,1)S(1)}, pred[128,384]{1,0:T(32,128)(4,1)}, u32[]{:S(2)}) copy-start(pred[128,384]{1,0:T(32,128)(4,1)} %constant.177) | copy-start | bytes 147460
  1.7 41.8 %collective-permute-start = (f32[8,16,512]{2,1,0:T(8,128)S(1)}, f32[8,16,512]{2,1,0:T(8,128)S(1)}, u32[]{:S(2)}, u32[]{:S(2)}) collective-permute-start(f32[8,16,512]{2,1,0:T(8,128)S(1)} %get-tuple-element.87), channel_id=1, source_target_pairs={{0,16},{16,32},{32,48},{48,64},{64,80},{80,96},{96,112},{112,128},... | collective-permute-start | bytes 786440 | tf_op jit(solution)/shard_map/ppermute | solution.py:233
  1.9 41.6 %collective-permute-start.1 = (f32[8,16,512]{2,1,0:T(8,128)S(1)}, f32[8,16,512]{2,1,0:T(8,128)S(1)}, u32[]{:S(2)}, u32[]{:S(2)}) collective-permute-start(f32[8,16,512]{2,1,0:T(8,128)S(1)} %get-tuple-element.86), channel_id=1, source_target_pairs={{0,240},{16,0},{32,16},{48,32},{64,48},{80,64},{96,80},{112,96},{1... | collective-permute-start | bytes 786440 | tf_op jit(solution)/shard_map/ppermute | solution.py:233
  9.5 38.2 %collective-permute-start.2 = (f32[16,8,512]{2,1,0:T(8,128)S(1)}, f32[16,8,512]{2,1,0:T(8,128)S(1)}, u32[]{:S(2)}, u32[]{:S(2)}) collective-permute-start(f32[16,8,512]{2,1,0:T(8,128)S(1)} %get-tuple-element.85), channel_id=1, source_target_pairs={{0,1},{1,2},{2,3},{3,4},{4,5},{5,6},{6,7},{7,8},{8,9},{9,10},{10,1... | collective-permute-start | bytes 786440 | tf_op jit(solution)/shard_map/ppermute | solution.py:233
  9.6 38.2 %collective-permute-start.3 = (f32[16,8,512]{2,1,0:T(8,128)S(1)}, f32[16,8,512]{2,1,0:T(8,128)S(1)}, u32[]{:S(2)}, u32[]{:S(2)}) collective-permute-start(f32[16,8,512]{2,1,0:T(8,128)S(1)} %get-tuple-element.84), channel_id=1, source_target_pairs={{0,15},{1,0},{2,1},{3,2},{4,3},{5,4},{6,5},{7,6},{8,7},{9,8},{10,9... | collective-permute-start | bytes 786440 | tf_op jit(solution)/shard_map/ppermute | solution.py:233
  43.6 10.1 %collective-permute-start.4 = (f32[16,8,512]{2,1,0:T(8,128)S(1)}, f32[16,8,512]{2,1,0:T(8,128)S(1)}, u32[]{:S(2)}, u32[]{:S(2)}) collective-permute-start(f32[16,8,512]{2,1,0:T(8,128)S(1)} %get-tuple-element.83), channel_id=1, source_target_pairs={{0,1},{1,2},{2,3},{3,4},{4,5},{5,6},{6,7},{7,8},{8,9},{9,10},{10,1... | collective-permute-start | bytes 786440 | tf_op jit(solution)/shard_map/ppermute | solution.py:233
  43.9 9.8 %collective-permute-start.5 = (f32[16,8,512]{2,1,0:T(8,128)S(1)}, f32[16,8,512]{2,1,0:T(8,128)S(1)}, u32[]{:S(2)}, u32[]{:S(2)}) collective-permute-start(f32[16,8,512]{2,1,0:T(8,128)S(1)} %get-tuple-element.82), channel_id=1, source_target_pairs={{0,15},{1,0},{2,1},{3,2},{4,3},{5,4},{6,5},{7,6},{8,7},{9,8},{10,9... | collective-permute-start | bytes 786440 | tf_op jit(solution)/shard_map/ppermute | solution.py:233
  64.7 10.5 %collective-permute-start.9 = (f32[16,8,512]{2,1,0:T(8,128)S(1)}, f32[16,8,512]{2,1,0:T(8,128)S(1)}, u32[]{:S(2)}, u32[]{:S(2)}) collective-permute-start(f32[16,8,512]{2,1,0:T(8,128)S(1)} %get-tuple-element.20), channel_id=1, source_target_pairs={{0,15},{1,0},{2,1},{3,2},{4,3},{5,4},{6,5},{7,6},{8,7},{9,8},{10,9... | collective-permute-start | bytes 786440 | tf_op jit(solution)/shard_map/ppermute | solution.py:233
  66.7 10.4 %collective-permute-start.8 = (f32[16,8,512]{2,1,0:T(8,128)S(1)}, f32[16,8,512]{2,1,0:T(8,128)S(1)}, u32[]{:S(2)}, u32[]{:S(2)}) collective-permute-start(f32[16,8,512]{2,1,0:T(8,128)S(1)} %get-tuple-element.19), channel_id=1, source_target_pairs={{0,1},{1,2},{2,3},{3,4},{4,5},{5,6},{6,7},{7,8},{8,9},{9,10},{10,1... | collective-permute-start | bytes 786440 | tf_op jit(solution)/shard_map/ppermute | solution.py:233
  69.1 10.2 %collective-permute-start.7 = (f32[16,8,512]{2,1,0:T(8,128)S(1)}, f32[16,8,512]{2,1,0:T(8,128)S(1)}, u32[]{:S(2)}, u32[]{:S(2)}) collective-permute-start(f32[16,8,512]{2,1,0:T(8,128)S(1)} %get-tuple-element.17), channel_id=1, source_target_pairs={{0,15},{1,0},{2,1},{3,2},{4,3},{5,4},{6,5},{7,6},{8,7},{9,8},{10,9... | collective-permute-start | bytes 786440 | tf_op jit(solution)/shard_map/ppermute | solution.py:233
  73.1 7.9 %collective-permute-start.6 = (f32[16,8,512]{2,1,0:T(8,128)S(1)}, f32[16,8,512]{2,1,0:T(8,128)S(1)}, u32[]{:S(2)}, u32[]{:S(2)}) collective-permute-start(f32[16,8,512]{2,1,0:T(8,128)S(1)} %get-tuple-element.16), channel_id=1, source_target_pairs={{0,1},{1,2},{2,3},{3,4},{4,5},{5,6},{6,7},{7,8},{8,9},{9,10},{10,1... | collective-permute-start | bytes 786440 | tf_op jit(solution)/shard_map/ppermute | solution.py:233
  77.2 6.5 %collective-permute-start.11 = (f32[8,16,512]{2,1,0:T(8,128)S(1)}, f32[8,16,512]{2,1,0:T(8,128)S(1)}, u32[]{:S(2)}, u32[]{:S(2)}) collective-permute-start(f32[8,16,512]{2,1,0:T(8,128)S(1)} %get-tuple-element.81), channel_id=1, source_target_pairs={{0,240},{16,0},{32,16},{48,32},{64,48},{80,64},{96,80},{112,96},{1... | collective-permute-start | bytes 786440 | tf_op jit(solution)/shard_map/ppermute | solution.py:233
  78.6 10.0 %collective-permute-start.10 = (f32[8,16,512]{2,1,0:T(8,128)S(1)}, f32[8,16,512]{2,1,0:T(8,128)S(1)}, u32[]{:S(2)}, u32[]{:S(2)}) collective-permute-start(f32[8,16,512]{2,1,0:T(8,128)S(1)} %get-tuple-element.80), channel_id=1, source_target_pairs={{0,16},{16,32},{32,48},{48,64},{64,80},{80,96},{96,112},{112,128},... | collective-permute-start | bytes 786440 | tf_op jit(solution)/shard_map/ppermute | solution.py:233
  (37 other events, 60.8 us)

commit v2 on v1

v2 whole, which is shorter than its diff:
```python
import jax
import jax.numpy as jnp
import numpy as np
from jax import lax
from jax.experimental import pallas as pl
from jax.experimental.pallas import tpu as pltpu
from jax.sharding import PartitionSpec as P

RADIUS = 8
DENSITIES = 5
TAPS = 2 * RADIUS + 1
TILE = 16
CELLS = TILE * TILE


def piece_cells():
    inner = list(range(TILE))
    outer = list(range(-RADIUS, 0)) + list(range(TILE, TILE + RADIUS))
    west, east = list(range(-RADIUS, 0)), list(range(TILE, TILE + RADIUS))
    blocks = [
        (inner, inner),
        (outer, inner),
        (inner, west),
        (inner, east),
        (outer, west),
        (outer, east),
    ]
    return blocks


def cell_arrays():
    rows, cols = [], []
    for block_rows, block_cols in piece_cells():
        for row in block_rows:
            for col in block_cols:
                rows.append(row)
                cols.append(col)
    return np.array(rows, np.int32), np.array(cols, np.int32)


def offset_tables():
    rows, cols = cell_arrays()
    tile = np.arange(TILE, dtype=np.int32)
    span = np.arange(-RADIUS, TILE + RADIUS, dtype=np.int32)
    tile_rows, tile_cols = np.repeat(tile, TILE), np.tile(tile, TILE)
    return (
        rows[None, :] - tile[:, None],
        cols[None, :] - tile[:, None],
        span[:, None] - tile_rows[None, :],
        span[:, None] - tile_cols[None, :],
    )


def taps_at(weights, density, offsets):
    total = jnp.zeros(offsets.shape, jnp.float32)
    for tap in range(TAPS):
        total = jnp.where(offsets == tap - RADIUS, weights[density, tap], total)
    return total


def taps_of_all(weights, offsets):
    totals = [jnp.zeros(offsets.shape, jnp.float32)] * DENSITIES
    for tap in range(TAPS):
        here = offsets == tap - RADIUS
        totals = [jnp.where(here, weights[a, tap], totals[a]) for a in range(DENSITIES)]
    return totals


LANES = 128


def build_kernel(
    kr, kc, kd, row_off, col_off, row_span, col_span, nh, nl, ch, cl, sh, sl, rh, rl, eh, el, bands, bands_t
):
    def put(high_ref, low_ref, start, lanes, values):
        high, low = halves(values)
        high_ref[start : start + TILE, lanes] = high
        low_ref[start : start + TILE, lanes] = low

    def forward(high_ref, low_ref, first):
        def chunk(index, carry):
            source = pl.ds(pl.multiple_of(first + index * LANES, LANES), LANES)
            lanes = pl.ds(pl.multiple_of(index * LANES, LANES), LANES)
            by_row = taps_of_all(kr, row_off[:, source])
            by_col = taps_of_all(kc, col_off[:, source])
            for a in range(DENSITIES):
                for r in range(TILE):
                    put(high_ref, low_ref, a * CELLS + r * TILE, lanes, by_row[a][r : r + 1] * by_col[a])
            return carry

        lax.fori_loop(0, high_ref.shape[1] // LANES, chunk, 0)

    forward(nh, nl, 0)
    forward(ch, cl, 3 * CELLS)

    def transposes(index, carry):
        density = index // 2
        source = pl.ds(pl.multiple_of((index % 2) * LANES, LANES), LANES)
        lanes = pl.ds(pl.multiple_of(index * LANES, LANES), LANES)
        by_row = taps_at(kr, density, row_span[:, source])
        by_col = taps_at(kc, density, col_span[:, source])
        row = lambda r: by_row[r + RADIUS : r + RADIUS + 1]
        inner = list(range(TILE))
        outer = list(range(-RADIUS, 0)) + list(range(TILE, TILE + RADIUS))
        mid = by_col[RADIUS : RADIUS + TILE]
        for place, r in enumerate(inner + outer):
            put(rh, rl, place * TILE, lanes, row(r) * mid)
        for high_ref, low_ref, rows in ((sh, sl, inner), (eh, el, outer)):
            for side, edge in enumerate((by_col[:RADIUS], by_col[RADIUS + TILE :])):
                for pair in range(TILE // 2):
                    both = [row(rows[2 * pair]) * edge, row(rows[2 * pair + 1]) * edge]
                    put(high_ref, low_ref, side * CELLS // 2 + pair * TILE, lanes, jnp.concatenate(both, 0))
        return carry

    lax.fori_loop(0, DENSITIES * CELLS // LANES, transposes, 0)

    depth = bands.shape[-1]
    count = depth // LANES

    def band(density, carry):
        for ref, sign in ((bands, 1), (bands_t, -1)):
            ref[density] = jnp.zeros((depth, depth), jnp.bfloat16)
            for start in range(0, LANES, TILE):
                shape = (TILE, LANES)
                offsets = sign * (
                    start + lax.broadcasted_iota(jnp.int32, shape, 0) - lax.broadcasted_iota(jnp.int32, shape, 1)
                )
                part = taps_at(kd, density, offsets).astype(jnp.bfloat16)
                for block in range(count):
                    base = block * LANES
                    ref[density, base + start : base + start + TILE, base : base + LANES] = part
                for step, near_edge in ((1, start == 0), (-1, start == LANES - TILE)):
                    if near_edge:
                        part = taps_at(kd, density, offsets + sign * step * LANES).astype(jnp.bfloat16)
                        for block in range(count):
                            if 0 <= block + step < count:
                                base, across = (block + step) * LANES, block * LANES
                                ref[density, base + start : base + start + TILE, across : across + LANES] = part
        return carry

    lax.fori_loop(0, DENSITIES, band, 0)


def build(kernel_rows, kernel_cols, kernel_depth, depth):
    cells = DENSITIES * CELLS
    shapes = [(cells, 3 * CELLS)] * 2 + [(cells, CELLS)] * 2
    shapes += [(CELLS, cells)] * 2 + [(2 * CELLS, cells)] * 2 + [(CELLS, cells)] * 2
    shapes += [(DENSITIES, depth, depth)] * 2
    vmem = pl.BlockSpec(memory_space=pltpu.VMEM)
    smem = pl.BlockSpec(memory_space=pltpu.SMEM)
    return pl.pallas_call(
        build_kernel,
        out_shape=[jax.ShapeDtypeStruct(s, jnp.bfloat16) for s in shapes],
        in_specs=[smem] * 3 + [vmem] * 4,
        out_specs=[vmem] * len(shapes),
        compiler_params=pltpu.CompilerParams(vmem_limit_bytes=24 << 20),
        cost_estimate=pl.CostEstimate(flops=30 << 20, bytes_accessed=16 << 20, transcendentals=0),
        name="build",
    )(
        kernel_rows,
        kernel_cols,
        kernel_depth.astype(jnp.float32),
        *[jnp.asarray(table.astype(np.int32)) for table in offset_tables()],
    )


def halves(values):
    high = values.astype(jnp.bfloat16)
    return high, (values - high.astype(jnp.float32)).astype(jnp.bfloat16)


def dot3(left_high, left_low, right_high, right_low):
    left = jnp.concatenate([left_high, left_low, left_high], 1)
    right = jnp.concatenate([right_high, right_high, right_low], 0)
    return jnp.dot(left, right, preferred_element_type=jnp.float32)


def near_kernel(own, north, south, west, east, wh, wl, out, xh, xl):
    depth = own.shape[-1]
    start = 0
    for ref in (own, north, south, west, east):
        size = ref.shape[0] * ref.shape[1]
        high, low = halves(ref[...].reshape(size, depth))
        xh[start : start + size] = high
        xl[start : start + size] = low
        start += size

    def density(index, carry):
        rows = pl.ds(pl.multiple_of(index * CELLS, CELLS), CELLS)
        out[rows] = dot3(wh[rows], wl[rows], xh[...], xl[...])
        return carry

    lax.fori_loop(0, DENSITIES, density, 0)


def near(pieces, wh, wl):
    depth = pieces[0].shape[-1]
    keys = 3 * CELLS
    vmem = pl.BlockSpec(memory_space=pltpu.VMEM)
    return pl.pallas_call(
        near_kernel,
        out_shape=jax.ShapeDtypeStruct((DENSITIES * CELLS, depth), jnp.float32),
        in_specs=[vmem] * 7,
        out_specs=vmem,
        scratch_shapes=[pltpu.VMEM((keys, depth), jnp.bfloat16)] * 2,
        compiler_params=pltpu.CompilerParams(vmem_limit_bytes=16 << 20),
        cost_estimate=pl.CostEstimate(
            flops=6 * DENSITIES * CELLS * keys * depth, bytes_accessed=10 << 20, transcendentals=0
        ),
        name="near",
    )(*pieces, wh, wl)


def middle_kernel(
    partial, corner_w, corner_e, wh, wl, bands, bands_t, th, tl, hessian_hbm, out_w, out_e, bh, bl,
    xh, xl, dens, low, hessian, sems
):
    depth = partial.shape[-1]
    half = CELLS // 2
    copies = [
        pltpu.make_async_copy(hessian_hbm.at[a], hessian.at[a], sems.at[a]) for a in range(DENSITIES)
    ]
    for copy in copies:
        copy.start()
    for start, ref in ((0, corner_w), (half, corner_e)):
        high, rest = halves(ref[...].reshape(half, depth))
        xh[start : start + half] = high
        xl[start : start + half] = rest
    for b in range(DENSITIES):
        rows = slice(b * CELLS, (b + 1) * CELLS)
        lateral = partial[rows] + dot3(wh[rows], wl[rows], xh[...], xl[...])
        dens[b] = jnp.dot(lateral.astype(jnp.bfloat16), bands[b], preferred_element_type=jnp.float32)
    for a in range(DENSITIES):
        copies[a].wait()
        for r in range(TILE):
            cells = slice(r * TILE, (r + 1) * TILE)
            grad = hessian[a, 0, r].astype(jnp.float32) * dens[0, cells]
            for b in range(1, DENSITIES):
                grad = grad + hessian[a, b, r].astype(jnp.float32) * dens[b, cells]
            low[a, cells] = grad.astype(jnp.bfloat16)
        back = jnp.dot(low[a], bands_t[a], preferred_element_type=jnp.float32)
        rows = slice(a * CELLS, (a + 1) * CELLS)
        high, rest = halves(back)
        bh[rows] = high
        bl[rows] = rest
    total = dot3(th[...], tl[...], bh[...], bl[...])
    out_w[...] = total[:half].reshape(out_w.shape)
    out_e[...] = total[half:].reshape(out_e.shape)


def middle(partial, corner_w, corner_e, wh, wl, bands, bands_t, th, tl, hessian):
    depth = partial.shape[-1]
    edge = jax.ShapeDtypeStruct(corner_w.shape, jnp.float32)
    back = jax.ShapeDtypeStruct((DENSITIES * CELLS, depth), jnp.bfloat16)
    vmem = pl.BlockSpec(memory_space=pltpu.VMEM)
    return pl.pallas_call(
        middle_kernel,
        out_shape=[edge, edge, back, back],
        in_specs=[vmem] * 9 + [pl.BlockSpec(memory_space=pl.ANY)],
        out_specs=[vmem] * 4,
        scratch_shapes=[
            pltpu.VMEM((CELLS, depth), jnp.bfloat16),
            pltpu.VMEM((CELLS, depth), jnp.bfloat16),
            pltpu.VMEM((DENSITIES, CELLS, depth), jnp.float32),
            pltpu.VMEM((DENSITIES, CELLS, depth), jnp.bfloat16),
            pltpu.VMEM(hessian.shape, jnp.bfloat16),
            pltpu.SemaphoreType.DMA((DENSITIES,)),
        ],
        compiler_params=pltpu.CompilerParams(vmem_limit_bytes=32 << 20),
        cost_estimate=pl.CostEstimate(
            flops=DENSITIES * CELLS * depth * (12 * CELLS + 4 * depth), bytes_accessed=16 << 20, transcendentals=0
        ),
        name="middle",
    )(partial, corner_w, corner_e, wh, wl, bands, bands_t, th, tl, hessian)


def spread_kernel(th, tl, bh, bl, *outs):
    total = dot3(th[...], tl[...], bh[...], bl[...])
    start = 0
    for out in outs:
        size = out.shape[0] * out.shape[1]
        out[...] = total[start : start + size].reshape(out.shape)
        start += size


def spread(th, tl, bh, bl, shapes):
    depth = bh.shape[-1]
    vmem = pl.BlockSpec(memory_space=pltpu.VMEM)
    return pl.pallas_call(
        spread_kernel,
        out_shape=[jax.ShapeDtypeStruct(s + (depth,), jnp.float32) for s in shapes],
        in_specs=[vmem] * 4,
        out_specs=[vmem] * len(shapes),
        compiler_params=pltpu.CompilerParams(vmem_limit_bytes=16 << 20),
        cost_estimate=pl.CostEstimate(
            flops=6 * th.shape[0] * th.shape[1] * depth, bytes_accessed=6 << 20, transcendentals=0
        ),
        name="spread",
    )(th, tl, bh, bl)


def shift(cells, axis, step):
    count = lax.axis_size(axis)
    return lax.ppermute(cells, axis, [(i, (i + step) % count) for i in range(count)])


def per_device(tangent, hessian, kernel_rows, kernel_cols, kernel_depth):
    span_rows, span_cols, depth = tangent.shape
    reach = RADIUS

    north = shift(tangent[reach:], "gx", 1)
    south = shift(tangent[:reach], "gx", -1)
    west = shift(tangent[:, reach:], "gy", 1)
    east = shift(tangent[:, :reach], "gy", -1)

    nh, nl, ch, cl, sh, sl, rh, rl, eh, el, bands, bands_t = build(kernel_rows, kernel_cols, kernel_depth, depth)

    sides = jnp.concatenate([north, south], 0)
    corner_w = shift(sides[:, reach:], "gy", 1)
    corner_e = shift(sides[:, :reach], "gy", -1)

    partial = near((tangent, north, south, west, east), nh, nl)
    to_w, to_e, bh, bl = middle(partial, corner_w, corner_e, ch, cl, bands, bands_t, eh, el, hessian)
    from_e = shift(to_w, "gy", -1)
    from_w = shift(to_e, "gy", 1)

    edge_w, edge_e = spread(sh, sl, bh, bl, [(span_rows, reach)] * 2)
    edge_from_e = shift(edge_w, "gy", -1)
    edge_from_w = shift(edge_e, "gy", 1)

    own, around = spread(rh, rl, bh, bl, [(span_rows, span_cols)] * 2)
    around = around + jnp.concatenate([from_w, from_e], 1)
    side_from_s = shift(around[:reach], "gx", -1)
    side_from_n = shift(around[reach:], "gx", 1)
    own = own + jnp.concatenate([edge_from_w, edge_from_e], 1)
    return own + jnp.concatenate([side_from_n, side_from_s], 0)


def solution(mesh):
    return jax.shard_map(
        per_device,
        mesh=mesh,
        in_specs=(P("gx", "gy", None), P(None, None, "gx", "gy", None), P(), P(), P()),
        out_specs=P("gx", "gy", None),
        check_vma=False,
    )
```

time: 90.6 us -> 57.2 us (0.63)
  the two profiles are of different devices: /device:TPU:0 before, /device:TPU:4 now
where the time goes in v2:
time: 57.2 us; the launch traced here: 56.7 us
  starting transfers between devices  27.4 us (48%)
  Pallas kernels  19 us (33%)
  waiting for transfers between devices  6.62 us (12%)
  local copies, waits for them, and re-layouts  2.41 us (4%)
  other arithmetic  1.05 us (2%)
    ppermute x12, starting transfers between devices, shift(): lax.ppermute(cells, axis, [(i, (i + step) % count) for i in range(count)])  27.4 us
    ppermute x12, waiting for transfers between devices, shift(): lax.ppermute(cells, axis, [(i, (i + step) % count) for i in range(count)])  6.62 us
    pallas_call x1, Pallas kernels, middle(): pl.pallas_call(middle_kernel, out_shape=[edge, edge, back, back], in_spec...  5.88 us
    pallas_call x1, Pallas kernels, build(): pl.pallas_call(build_kernel, out_shape=[jax.ShapeDtypeStruct(s, jnp.bfloa...  5.66 us
    pallas_call x1, Pallas kernels, near(): pl.pallas_call(near_kernel, out_shape=jax.ShapeDtypeStruct((DENSITIES * C...  4.12 us
    pallas_call x2, Pallas kernels, spread(): pl.pallas_call(spread_kernel, out_shape=[jax.ShapeDtypeStruct(s + (depth,...  3.35 us
    slice x1, local copies, waits for them, and re-layouts, per_device(): south = shift(tangent[:reach], 'gx', -1)  1.18 us
  transfers between devices with their start and end apart: 12, of which 4 were waited for; matrix products, arithmetic and copies ran while one was open for 2% of the time, Pallas kernels for 23%

profile of v2, /device:TPU:4, one launch (start us, length us, event | category | flops | bytes accessed | tf_op | source)
XLA Modules:
  0.0 56.7 jit_solution(3399336975548096969)
XLA Ops:
  0.0 0.0 copy-start.2
  0.0 0.0 copy-start
  0.0 0.0 copy-start.7
  0.0 0.0 copy-start.5
  0.1 0.0 copy-start.6
  0.1 1.2 %fusion.4 = (f32[8,16,512]{2,1,0:T(8,128)S(1)}, f32[8,16,512]{2,1,0:T(8,128)S(1)}) fusion(f32[16,16,512]{2,1,0:T(8,128)} %own.1), kind=kLoop, calls=%fused_computation.8 | loop fusion | bytes 1048576 | tf_op jit(solution)/shard_map/slice | solution.py:312
  1.3 2.0 %collective-permute-start = (f32[8,16,512]{2,1,0:T(8,128)S(1)}, f32[8,16,512]{2,1,0:T(8,128)S(1)}, u32[]{:S(2)}, u32[]{:S(2)}) collective-permute-start(f32[8,16,512]{2,1,0:T(8,128)S(1)} %get-tuple-element.52), channel_id=1, source_target_pairs={{0,16},{16,32},{32,48},{48,64},{64,80},{80,96},{96,112},{112,128},... | collective-permute-start | bytes 786440 | tf_op jit(solution)/shard_map/ppermute | solution.py:304
  3.2 4.0 %collective-permute-start.1 = (f32[8,16,512]{2,1,0:T(8,128)S(1)}, f32[8,16,512]{2,1,0:T(8,128)S(1)}, u32[]{:S(2)}, u32[]{:S(2)}) collective-permute-start(f32[8,16,512]{2,1,0:T(8,128)S(1)} %get-tuple-element.51), channel_id=1, source_target_pairs={{0,240},{16,0},{32,16},{48,32},{64,48},{80,64},{96,80},{112,96},{1... | collective-permute-start | bytes 786440 | tf_op jit(solution)/shard_map/ppermute | solution.py:304
  7.2 1.1 %fusion.3 = (f32[16,8,512]{2,1,0:T(8,128)S(1)}, f32[16,8,512]{2,1,0:T(8,128)S(1)}) fusion(f32[16,16,512]{2,1,0:T(8,128)} %own.1), kind=kLoop, calls=%fused_computation.7 | loop fusion | bytes 1048576 | tf_op jit(solution)/shard_map/slice | solution.py:314
  8.3 0.1 collective-permute-start.2
  8.4 3.8 %collective-permute-start.3 = (f32[16,8,512]{2,1,0:T(8,128)S(1)}, f32[16,8,512]{2,1,0:T(8,128)S(1)}, u32[]{:S(2)}, u32[]{:S(2)}) collective-permute-start(f32[16,8,512]{2,1,0:T(8,128)S(1)} %get-tuple-element.49), channel_id=1, source_target_pairs={{0,15},{1,0},{2,1},{3,2},{4,3},{5,4},{6,5},{7,6},{8,7},{9,8},{10,9... | collective-permute-start | bytes 786440 | tf_op jit(solution)/shard_map/ppermute | solution.py:304
  12.2 0.0 copy-done.7
  12.2 0.0 copy-done.3
  12.2 0.0 copy-done.4
  12.2 0.0 copy-done.1
  12.2 0.0 copy-done.2
  12.3 0.0 copy-done.5
  12.3 0.0 copy-done.6
  12.3 5.7 %build.1 = (bf16[1280,768]{1,0:T(8,128)(2,1)S(1)}, bf16[1280,768]{1,0:T(8,128)(2,1)S(1)}, bf16[1280,256]{1,0:T(8,128)(2,1)S(1)}, bf16[1280,256]{1,0:T(8,128)(2,1...) custom-call(f32[5,17]{1,0:T(8,128)S(1)} %copy-done.5, ...), custom_call_target="tpu_custom_call" | custom-call | flops 31457280 | bytes 16777216 | tf_op jit(solution)/shard_map/build/pallas_call | solution.py:151
  17.9 0.0 collective-permute-done.north
  18.0 0.0 collective-permute-done.1.south
  18.0 0.0 slice-start
  18.1 0.1 collective-permute-start.4
  18.2 3.8 %collective-permute-start.5 = (f32[16,8,512]{2,1,0:T(8,128)S(1)}, f32[16,8,512]{2,1,0:T(8,128)S(1)}, u32[]{:S(2)}, u32[]{:S(2)}) collective-permute-start(f32[16,8,512]{2,1,0:T(8,128)S(1)} %get-tuple-element.47), channel_id=1, source_target_pairs={{0,15},{1,0},{2,1},{3,2},{4,3},{5,4},{6,5},{7,6},{8,7},{9,8},{10,9... | collective-permute-start | bytes 786440 | tf_op jit(solution)/shard_map/ppermute | solution.py:304
  22.0 0.1 collective-permute-done.2.west
  22.1 0.0 collective-permute-done.3.east
  22.1 0.0 copy-done
  22.1 4.1 %near.1.partial = f32[1280,512]{1,0:T(8,128)S(1)} custom-call(f32[16,16,512]{2,1,0:T(8,128)S(1)} %copy-done, f32[8,16,512]{2,1,0:T(8,128)S(1)} %collective-permute-done.north, f32[8,16,512]{2,1,0:T(8,128)S(1)} %collective-permute-done.1.south, f32[16,8,512]{2,1,0:T(8,128)S(1)} %collective-permute-done.2.west, f32[16,8,512]{2,1,0:T(8,128)S(1)} %collective-permute-done.3.east, ...), custom_call_target="tpu_custom_call" | custom-call | flops 3019898880 | bytes 10485760 | tf_op jit(solution)/shard_map/near/pallas_call | solution.py:200
  26.2 2.1 %collective-permute-done.4.corner_w = f32[16,8,512]{2,1,0:T(8,128)S(1)} collective-permute-done((f32[16,8,512]{2,1,0:T(8,128)S(1)}, f32[16,8,512]{2,1,0:T(8,128)S(1)}, u32[]{:S(2)}, u32[]{:S(2)}) %collective-permute-start.4) | collective-permute-done | bytes 262176 | tf_op jit(solution)/shard_map/ppermute | solution.py:304
  28.3 0.0 collective-permute-done.5.corner_e
  28.3 0.0 slice-done
  28.3 5.9 %middle.1 = (f32[16,8,512]{2,1,0:T(8,128)S(1)}, f32[16,8,512]{2,1,0:T(8,128)S(1)}, bf16[1280,512]{1,0:T(8,128)(2,1)S(1)}, bf16[1280,512]{1,0:T(8,128)(2,1)S(1)}) custom-call(f32[1280,512]{1,0:T(8,128)S(1)} %near.1.partial, f32[16,8,512]{2,1,0:T(8,128)S(1)} %collective-permute-done.4.corner_w, f32[16,8,512]{2,1,0:T(8,128)S(1)} %collective-permute-done.5.corner_e, ...), custom_call_target="tpu_custom_call" | custom-call | flops 3355443200 | bytes 16777216 | tf_op jit(solution)/shard_map/middle/pallas_call | solution.py:256
  34.2 0.1 collective-permute-start.8
  34.3 3.8 %collective-permute-start.9 = (f32[16,8,512]{2,1,0:T(8,128)S(1)}, f32[16,8,512]{2,1,0:T(8,128)S(1)}, u32[]{:S(2)}, u32[]{:S(2)}) collective-permute-start(f32[16,8,512]{2,1,0:T(8,128)S(1)} %get-tuple-element.44), channel_id=1, source_target_pairs={{0,15},{1,0},{2,1},{3,2},{4,3},{5,4},{6,5},{7,6},{8,7},{9,8},{10,9... | collective-permute-start | bytes 786440 | tf_op jit(solution)/shard_map/ppermute | solution.py:304
  38.1 1.2 %spread.3 = (f32[16,8,512]{2,1,0:T(8,128)S(1)}, f32[16,8,512]{2,1,0:T(8,128)S(1)}) custom-call(bf16[256,1280]{1,0:T(8,128)(2,1)S(1)} %get-tuple-element.38.th, bf16[256,1280]{1,0:T(8,128)(2,1)S(1)} %get-tuple-element.39.tl, bf16[1280,512]{1,0:T(8,128)(2,1)S(1)} %get-tuple-element.35.bh, bf16[1280,512]{1,0:T(8,128)(2,1)S(1)} %get-tuple-element.36.bl), custom_call_target="tpu_custom_call" | custom-call | flops 1006632960 | bytes 6291456 | tf_op jit(solution)/shard_map/spread/pallas_call | solution.py:289
  39.3 0.1 collective-permute-start.6
  39.4 3.8 %collective-permute-start.7 = (f32[16,8,512]{2,1,0:T(8,128)S(1)}, f32[16,8,512]{2,1,0:T(8,128)S(1)}, u32[]{:S(2)}, u32[]{:S(2)}) collective-permute-start(f32[16,8,512]{2,1,0:T(8,128)S(1)} %get-tuple-element.41), channel_id=1, source_target_pairs={{0,15},{1,0},{2,1},{3,2},{4,3},{5,4},{6,5},{7,6},{8,7},{9,8},{10,9... | collective-permute-start | bytes 786440 | tf_op jit(solution)/shard_map/ppermute | solution.py:304
  43.2 2.2 %spread.2 = (f32[16,16,512]{2,1,0:T(8,128)S(1)}, f32[16,16,512]{2,1,0:T(8,128)S(1)}) custom-call(bf16[512,1280]{1,0:T(8,128)(2,1)S(1)} %get-tuple-element.25.th, bf16[512,1280]{1,0:T(8,128)(2,1)S(1)} %get-tuple-element.26.tl, bf16[1280,512]{1,0:T(8,128)(2,1)S(1)} %get-tuple-element.35.bh, bf16[1280,512]{1,0:T(8,128)(2,1)S(1)} %get-tuple-element.36.bl), custom_call_target="tpu_custom_call" | custom-call | flops 2013265920 | bytes 6291456 | tf_op jit(solution)/shard_map/spread/pallas_call | solution.py:289
  45.4 0.0 collective-permute-done.8
  45.4 0.0 collective-permute-done.9
  45.5 0.1 maximum_add_fusion.1
  45.6 0.1 collective-permute-start.10
  45.7 5.6 %collective-permute-start.11 = (f32[8,16,512]{2,1,0:T(8,128)S(1)}, f32[8,16,512]{2,1,0:T(8,128)S(1)}, u32[]{:S(2)}, u32[]{:S(2)}) collective-permute-start(f32[8,16,512]{2,1,0:T(8,128)S(1)} %get-tuple-element.46), channel_id=1, source_target_pairs={{0,240},{16,0},{32,16},{48,32},{64,48},{80,64},{96,80},{112,96},{1... | collective-permute-start | bytes 786440 | tf_op jit(solution)/shard_map/ppermute | solution.py:304
  51.3 0.8 %collective-permute-done.6 = f32[16,8,512]{2,1,0:T(8,128)S(1)} collective-permute-done((f32[16,8,512]{2,1,0:T(8,128)S(1)}, f32[16,8,512]{2,1,0:T(8,128)S(1)}, u32[]{:S(2)}, u32[]{:S(2)}) %collective-permute-start.6) | collective-permute-done | bytes 262176 | tf_op jit(solution)/shard_map/ppermute | solution.py:304
  52.2 0.0 collective-permute-done.7
  52.2 3.6 %collective-permute-done.10 = f32[8,16,512]{2,1,0:T(8,128)S(1)} collective-permute-done((f32[8,16,512]{2,1,0:T(8,128)S(1)}, f32[8,16,512]{2,1,0:T(8,128)S(1)}, u32[]{:S(2)}, u32[]{:S(2)}) %collective-permute-start.10) | collective-permute-done | bytes 262176 | tf_op jit(solution)/shard_map/ppermute | solution.py:304
  55.8 0.0 collective-permute-done.11
  55.8 1.0 %fusion = f32[16,16,512]{2,1,0:T(8,128)} fusion(f32[16,16,512]{2,1,0:T(8,128)S(1)} %get-tuple-element.37, f32[16,8,512]{2,1,0:T(8,128)S(1)} %collective-permute-done.7, f32[16,8,512]{2,1,0:T(8,128)S(1)} %collective-permute-done.6, f32[8,16,512]{2,1,0:T(8,128)S(1)} %collective-permute-done.11, f32[8,16,512]{2,1,0:T(8,128)S(1)} %collective-permute-done.10), kind=kLoop, calls=%fused_computation.1 | loop fusion | flops 524288 | bytes 2097152 | tf_op jit(solution)/shard_map/add | solution.py:336
  (11 shorter events, 0.1 us)
Async XLA Ops:
  0.0 12.2 %copy-start.3 = (s32[32,256]{1,0:T(8,128)S(1)}, s32[32,256]{1,0:T(8,128)}, u32[]{:S(2)}) copy-start(s32[32,256]{1,0:T(8,128)} %constant.10.clone.row_span) | copy-start | bytes 98308
  0.0 12.2 %copy-start.4 = (s32[32,256]{1,0:T(8,128)S(1)}, s32[32,256]{1,0:T(8,128)}, u32[]{:S(2)}) copy-start(s32[32,256]{1,0:T(8,128)} %constant.11.clone.col_span) | copy-start | bytes 98308
  0.0 12.2 %copy-start.1 = (s32[16,1024]{1,0:T(8,128)S(1)}, s32[16,1024]{1,0:T(8,128)}, u32[]{:S(2)}) copy-start(s32[16,1024]{1,0:T(8,128)} %constant.8.clone.row_off) | copy-start | bytes 196612
  0.0 12.2 %copy-start.2 = (s32[16,1024]{1,0:T(8,128)S(1)}, s32[16,1024]{1,0:T(8,128)}, u32[]{:S(2)}) copy-start(s32[16,1024]{1,0:T(8,128)} %constant.9.clone.col_off) | copy-start | bytes 196612
  0.0 22.1 %copy-start = (f32[16,16,512]{2,1,0:T(8,128)S(1)}, f32[16,16,512]{2,1,0:T(8,128)}, u32[]{:S(2)}) copy-start(f32[16,16,512]{2,1,0:T(8,128)} %own.1) | copy-start | bytes 1572868
  0.0 12.2 %copy-start.7 = (bf16[5,17]{1,0:T(8,128)(2,1)S(1)}, bf16[5,17]{1,0:T(8,128)(2,1)}, u32[]{:S(2)}) copy-start(bf16[5,17]{1,0:T(8,128)(2,1)} %param.13) | copy-start | bytes 514
  0.0 12.2 %copy-start.5 = (f32[5,17]{1,0:T(8,128)S(1)}, f32[5,17]{1,0:T(8,128)}, u32[]{:S(2)}) copy-start(f32[5,17]{1,0:T(8,128)} %kr.1) | copy-start | bytes 1024
  0.1 12.2 %copy-start.6 = (f32[5,17]{1,0:T(8,128)S(1)}, f32[5,17]{1,0:T(8,128)}, u32[]{:S(2)}) copy-start(f32[5,17]{1,0:T(8,128)} %kc.1) | copy-start | bytes 1024
  1.3 16.7 %collective-permute-start = (f32[8,16,512]{2,1,0:T(8,128)S(1)}, f32[8,16,512]{2,1,0:T(8,128)S(1)}, u32[]{:S(2)}, u32[]{:S(2)}) collective-permute-start(f32[8,16,512]{2,1,0:T(8,128)S(1)} %get-tuple-element.52), channel_id=1, source_target_pairs={{0,16},{16,32},{32,48},{48,64},{64,80},{80,96},{96,112},{112,128},... | collective-permute-start | bytes 786440 | tf_op jit(solution)/shard_map/ppermute | solution.py:304
  3.2 14.7 %collective-permute-start.1 = (f32[8,16,512]{2,1,0:T(8,128)S(1)}, f32[8,16,512]{2,1,0:T(8,128)S(1)}, u32[]{:S(2)}, u32[]{:S(2)}) collective-permute-start(f32[8,16,512]{2,1,0:T(8,128)S(1)} %get-tuple-element.51), channel_id=1, source_target_pairs={{0,240},{16,0},{32,16},{48,32},{64,48},{80,64},{96,80},{112,96},{1... | collective-permute-start | bytes 786440 | tf_op jit(solution)/shard_map/ppermute | solution.py:304
  8.3 13.8 %collective-permute-start.2 = (f32[16,8,512]{2,1,0:T(8,128)S(1)}, f32[16,8,512]{2,1,0:T(8,128)S(1)}, u32[]{:S(2)}, u32[]{:S(2)}) collective-permute-start(f32[16,8,512]{2,1,0:T(8,128)S(1)} %get-tuple-element.50), channel_id=1, source_target_pairs={{0,1},{1,2},{2,3},{3,4},{4,5},{5,6},{6,7},{7,8},{8,9},{9,10},{10,1... | collective-permute-start | bytes 786440 | tf_op jit(solution)/shard_map/ppermute | solution.py:304
  8.4 13.7 %collective-permute-start.3 = (f32[16,8,512]{2,1,0:T(8,128)S(1)}, f32[16,8,512]{2,1,0:T(8,128)S(1)}, u32[]{:S(2)}, u32[]{:S(2)}) collective-permute-start(f32[16,8,512]{2,1,0:T(8,128)S(1)} %get-tuple-element.49), channel_id=1, source_target_pairs={{0,15},{1,0},{2,1},{3,2},{4,3},{5,4},{6,5},{7,6},{8,7},{9,8},{10,9... | collective-permute-start | bytes 786440 | tf_op jit(solution)/shard_map/ppermute | solution.py:304
  18.0 10.3 %slice-start = ((s8[6553600]{0:T(1024)(128)(4,1)}), s8[4194304]{0:T(1024)(128)(4,1)S(1)}, s32[]{:S(2)}) async-start(s8[6553600]{0:T(1024)(128)(4,1)} %bitcast), calls=%async_computation | async-start | bytes 8388608
  18.1 10.2 %collective-permute-start.4 = (f32[16,8,512]{2,1,0:T(8,128)S(1)}, f32[16,8,512]{2,1,0:T(8,128)S(1)}, u32[]{:S(2)}, u32[]{:S(2)}) collective-permute-start(f32[16,8,512]{2,1,0:T(8,128)S(1)} %get-tuple-element.48), channel_id=1, source_target_pairs={{0,1},{1,2},{2,3},{3,4},{4,5},{5,6},{6,7},{7,8},{8,9},{9,10},{10,1... | collective-permute-start | bytes 786440 | tf_op jit(solution)/shard_map/ppermute | solution.py:304
  18.2 10.1 %collective-permute-start.5 = (f32[16,8,512]{2,1,0:T(8,128)S(1)}, f32[16,8,512]{2,1,0:T(8,128)S(1)}, u32[]{:S(2)}, u32[]{:S(2)}) collective-permute-start(f32[16,8,512]{2,1,0:T(8,128)S(1)} %get-tuple-element.47), channel_id=1, source_target_pairs={{0,15},{1,0},{2,1},{3,2},{4,3},{5,4},{6,5},{7,6},{8,7},{9,8},{10,9... | collective-permute-start | bytes 786440 | tf_op jit(solution)/shard_map/ppermute | solution.py:304
  22.1 6.2 %slice-start.1 = ((s8[6553600]{0:T(1024)(128)(4,1)}), s8[2359296]{0:T(1024)(128)(4,1)S(1)}, s32[]{:S(2)}) async-start(s8[6553600]{0:T(1024)(128)(4,1)} %bitcast), calls=%async_computation.1 | async-start | bytes 4718592
  34.2 11.2 %collective-permute-start.8 = (f32[16,8,512]{2,1,0:T(8,128)S(1)}, f32[16,8,512]{2,1,0:T(8,128)S(1)}, u32[]{:S(2)}, u32[]{:S(2)}) collective-permute-start(f32[16,8,512]{2,1,0:T(8,128)S(1)} %get-tuple-element.43), channel_id=1, source_target_pairs={{0,1},{1,2},{2,3},{3,4},{4,5},{5,6},{6,7},{7,8},{8,9},{9,10},{10,1... | collective-permute-start | bytes 786440 | tf_op jit(solution)/shard_map/ppermute | solution.py:304
  34.3 11.2 %collective-permute-start.9 = (f32[16,8,512]{2,1,0:T(8,128)S(1)}, f32[16,8,512]{2,1,0:T(8,128)S(1)}, u32[]{:S(2)}, u32[]{:S(2)}) collective-permute-start(f32[16,8,512]{2,1,0:T(8,128)S(1)} %get-tuple-element.44), channel_id=1, source_target_pairs={{0,15},{1,0},{2,1},{3,2},{4,3},{5,4},{6,5},{7,6},{8,7},{9,8},{10,9... | collective-permute-start | bytes 786440 | tf_op jit(solution)/shard_map/ppermute | solution.py:304
  39.3 12.8 %collective-permute-start.6 = (f32[16,8,512]{2,1,0:T(8,128)S(1)}, f32[16,8,512]{2,1,0:T(8,128)S(1)}, u32[]{:S(2)}, u32[]{:S(2)}) collective-permute-start(f32[16,8,512]{2,1,0:T(8,128)S(1)} %get-tuple-element.40), channel_id=1, source_target_pairs={{0,1},{1,2},{2,3},{3,4},{4,5},{5,6},{6,7},{7,8},{8,9},{9,10},{10,1... | collective-permute-start | bytes 786440 | tf_op jit(solution)/shard_map/ppermute | solution.py:304
  39.4 12.8 %collective-permute-start.7 = (f32[16,8,512]{2,1,0:T(8,128)S(1)}, f32[16,8,512]{2,1,0:T(8,128)S(1)}, u32[]{:S(2)}, u32[]{:S(2)}) collective-permute-start(f32[16,8,512]{2,1,0:T(8,128)S(1)} %get-tuple-element.41), channel_id=1, source_target_pairs={{0,15},{1,0},{2,1},{3,2},{4,3},{5,4},{6,5},{7,6},{8,7},{9,8},{10,9... | collective-permute-start | bytes 786440 | tf_op jit(solution)/shard_map/ppermute | solution.py:304
  45.6 10.2 %collective-permute-start.10 = (f32[8,16,512]{2,1,0:T(8,128)S(1)}, f32[8,16,512]{2,1,0:T(8,128)S(1)}, u32[]{:S(2)}, u32[]{:S(2)}) collective-permute-start(f32[8,16,512]{2,1,0:T(8,128)S(1)} %get-tuple-element.45), channel_id=1, source_target_pairs={{0,16},{16,32},{32,48},{48,64},{64,80},{80,96},{96,112},{112,128},... | collective-permute-start | bytes 786440 | tf_op jit(solution)/shard_map/ppermute | solution.py:304
  45.7 10.1 %collective-permute-start.11 = (f32[8,16,512]{2,1,0:T(8,128)S(1)}, f32[8,16,512]{2,1,0:T(8,128)S(1)}, u32[]{:S(2)}, u32[]{:S(2)}) collective-permute-start(f32[8,16,512]{2,1,0:T(8,128)S(1)} %get-tuple-element.46), channel_id=1, source_target_pairs={{0,240},{16,0},{32,16},{48,32},{64,48},{80,64},{96,80},{112,96},{1... | collective-permute-start | bytes 786440 | tf_op jit(solution)/shard_map/ppermute | solution.py:304

commit v3 on v2

--- a/solution.py
+++ b/solution.py
@@ -1,3 +1,5 @@
+import functools
+
 import jax
 import jax.numpy as jnp
 import numpy as np
@@ -51,6 +53,13 @@
     )
 
 
+TURN = TILE + RADIUS
+
+
+def side_is_right():
+    return 1 - lax.rem(lax.axis_index("gy"), 2)
+
+
 def taps_at(weights, density, offsets):
     total = jnp.zeros(offsets.shape, jnp.float32)
     for tap in range(TAPS):
@@ -70,19 +79,23 @@
 
 
 def build_kernel(
-    kr, kc, kd, row_off, col_off, row_span, col_span, nh, nl, ch, cl, sh, sl, rh, rl, eh, el, bands, bands_t
+    kr, kc, kd, row_off, col_off, row_span, col_span,
+    nh, nl, ch, cl, th, tl, bands, bands_t
 ):
+    turn = TURN * side_is_right()
+
     def put(high_ref, low_ref, start, lanes, values):
         high, low = halves(values)
         high_ref[start : start + TILE, lanes] = high
         low_ref[start : start + TILE, lanes] = low
 
-    def forward(high_ref, low_ref, first):
+    def forward(high_ref, low_ref, first, side):
         def chunk(index, carry):
+            toward = turn * ((index == side).astype(jnp.int32) - (index == side + 1).astype(jnp.int32))
             source = pl.ds(pl.multiple_of(first + index * LANES, LANES), LANES)
             lanes = pl.ds(pl.multiple_of(index * LANES, LANES), LANES)
             by_row = taps_of_all(kr, row_off[:, source])
-            by_col = taps_of_all(kc, col_off[:, source])
+            by_col = taps_of_all(kc, col_off[:, source] + toward)
             for a in range(DENSITIES):
                 for r in range(TILE):
                     put(high_ref, low_ref, a * CELLS + r * TILE, lanes, by_row[a][r : r + 1] * by_col[a])
@@ -90,26 +103,28 @@
 
         lax.fori_loop(0, high_ref.shape[1] // LANES, chunk, 0)
 
-    forward(nh, nl, 0)
-    forward(ch, cl, 3 * CELLS)
+    forward(nh, nl, 0, 4)
+    forward(ch, cl, 3 * CELLS, 0)
 
     def transposes(index, carry):
         density = index // 2
         source = pl.ds(pl.multiple_of((index % 2) * LANES, LANES), LANES)
         lanes = pl.ds(pl.multiple_of(index * LANES, LANES), LANES)
         by_row = taps_at(kr, density, row_span[:, source])
-        by_col = taps_at(kc, density, col_span[:, source])
+        place = lax.broadcasted_iota(jnp.int32, (TILE + 2 * RADIUS, LANES), 0)
+        toward = jnp.where(place < RADIUS, turn, jnp.where(place < TILE + RADIUS, 0, -turn))
+        by_col = taps_at(kc, density, col_span[:, source] + toward)
         row = lambda r: by_row[r + RADIUS : r + RADIUS + 1]
         inner = list(range(TILE))
         outer = list(range(-RADIUS, 0)) + list(range(TILE, TILE + RADIUS))
         mid = by_col[RADIUS : RADIUS + TILE]
         for place, r in enumerate(inner + outer):
-            put(rh, rl, place * TILE, lanes, row(r) * mid)
-        for high_ref, low_ref, rows in ((sh, sl, inner), (eh, el, outer)):
+            put(th, tl, place * TILE, lanes, row(r) * mid)
+        for base, rows in ((2 * CELLS, inner), (3 * CELLS, outer)):
             for side, edge in enumerate((by_col[:RADIUS], by_col[RADIUS + TILE :])):
                 for pair in range(TILE // 2):
                     both = [row(rows[2 * pair]) * edge, row(rows[2 * pair + 1]) * edge]
-                    put(high_ref, low_ref, side * CELLS // 2 + pair * TILE, lanes, jnp.concatenate(both, 0))
+                    put(th, tl, base + side * CELLS // 2 + pair * TILE, lanes, jnp.concatenate(both, 0))
         return carry
 
     lax.fori_loop(0, DENSITIES * CELLS // LANES, transposes, 0)
@@ -144,7 +159,7 @@
 def build(kernel_rows, kernel_cols, kernel_depth, depth):
     cells = DENSITIES * CELLS
     shapes = [(cells, 3 * CELLS)] * 2 + [(cells, CELLS)] * 2
-    shapes += [(CELLS, cells)] * 2 + [(2 * CELLS, cells)] * 2 + [(CELLS, cells)] * 2
+    shapes += [(4 * CELLS, cells)] * 2
     shapes += [(DENSITIES, depth, depth)] * 2
     vmem = pl.BlockSpec(memory_space=pltpu.VMEM)
     smem = pl.BlockSpec(memory_space=pltpu.SMEM)
@@ -175,10 +190,10 @@
     return jnp.dot(left, right, preferred_element_type=jnp.float32)
 
 
-def near_kernel(own, north, south, west, east, wh, wl, out, xh, xl):
+def near_kernel(own, north, south, side_a, side_b, wh, wl, out, xh, xl):
     depth = own.shape[-1]
     start = 0
-    for ref in (own, north, south, west, east):
+    for ref in (own, north, south, side_a, side_b):
         size = ref.shape[0] * ref.shape[1]
         high, low = halves(ref[...].reshape(size, depth))
         xh[start : start + size] = high
@@ -212,17 +227,12 @@
 
 
 def middle_kernel(
-    partial, corner_w, corner_e, wh, wl, bands, bands_t, th, tl, hessian_hbm, out_w, out_e, bh, bl,
-    xh, xl, dens, low, hessian, sems
+    partial, corner_a, corner_b, wh, wl, bands, bands_t, th, tl, hessian, out_a, out_b, bh, bl,
+    xh, xl, dens, low
 ):
     depth = partial.shape[-1]
     half = CELLS // 2
-    copies = [
-        pltpu.make_async_copy(hessian_hbm.at[a], hessian.at[a], sems.at[a]) for a in range(DENSITIES)
-    ]
-    for copy in copies:
-        copy.start()
-    for start, ref in ((0, corner_w), (half, corner_e)):
+    for start, ref in ((0, corner_a), (half, corner_b)):
         high, rest = halves(ref[...].reshape(half, depth))
         xh[start : start + half] = high
         xl[start : start + half] = rest
@@ -231,7 +241,6 @@
         lateral = partial[rows] + dot3(wh[rows], wl[rows], xh[...], xl[...])
         dens[b] = jnp.dot(lateral.astype(jnp.bfloat16), bands[b], preferred_element_type=jnp.float32)
     for a in range(DENSITIES):
-        copies[a].wait()
         for r in range(TILE):
             cells = slice(r * TILE, (r + 1) * TILE)
             grad = hessian[a, 0, r].astype(jnp.float32) * dens[0, cells]
@@ -243,39 +252,39 @@
         high, rest = halves(back)
         bh[rows] = high
         bl[rows] = rest
-    total = dot3(th[...], tl[...], bh[...], bl[...])
-    out_w[...] = total[:half].reshape(out_w.shape)
-    out_e[...] = total[half:].reshape(out_e.shape)
-
-
-def middle(partial, corner_w, corner_e, wh, wl, bands, bands_t, th, tl, hessian):
+    corners = slice(3 * CELLS, 4 * CELLS)
+    total = dot3(th[corners], tl[corners], bh[...], bl[...])
+    out_a[...] = total[:half].reshape(out_a.shape)
+    out_b[...] = total[half:].reshape(out_b.shape)
+
+
+def middle(partial, corner_a, corner_b, wh, wl, bands, bands_t, th, tl, hessian):
     depth = partial.shape[-1]
-    edge = jax.ShapeDtypeStruct(corner_w.shape, jnp.float32)
+    edge = jax.ShapeDtypeStruct(corner_a.shape, jnp.float32)
     back = jax.ShapeDtypeStruct((DENSITIES * CELLS, depth), jnp.bfloat16)
     vmem = pl.BlockSpec(memory_space=pltpu.VMEM)
     return pl.pallas_call(
         middle_kernel,
         out_shape=[edge, edge, back, back],
-        in_specs=[vmem] * 9 + [pl.BlockSpec(memory_space=pl.ANY)],
+        in_specs=[vmem] * 10,
         out_specs=[vmem] * 4,
         scratch_shapes=[
             pltpu.VMEM((CELLS, depth), jnp.bfloat16),
             pltpu.VMEM((CELLS, depth), jnp.bfloat16),
             pltpu.VMEM((DENSITIES, CELLS, depth), jnp.float32),
             pltpu.VMEM((DENSITIES, CELLS, depth), jnp.bfloat16),
-            pltpu.VMEM(hessian.shape, jnp.bfloat16),
-            pltpu.SemaphoreType.DMA((DENSITIES,)),
         ],
-        compiler_params=pltpu.CompilerParams(vmem_limit_bytes=32 << 20),
+        compiler_params=pltpu.CompilerParams(vmem_limit_bytes=24 << 20),
         cost_estimate=pl.CostEstimate(
             flops=DENSITIES * CELLS * depth * (12 * CELLS + 4 * depth), bytes_accessed=16 << 20, transcendentals=0
         ),
         name="middle",
-    )(partial, corner_w, corner_e, wh, wl, bands, bands_t, th, tl, hessian)
-
-
-def spread_kernel(th, tl, bh, bl, *outs):
-    total = dot3(th[...], tl[...], bh[...], bl[...])
+    )(partial, corner_a, corner_b, wh, wl, bands, bands_t, th, tl, hessian)
+
+
+def spread_kernel(group, th, tl, bh, bl, *outs):
+    rows = slice(group * CELLS, (group + 1) * CELLS)
+    total = dot3(th[rows], tl[rows], bh[...], bl[...])
     start = 0
     for out in outs:
         size = out.shape[0] * out.shape[1]
@@ -283,17 +292,17 @@
         start += size
 
 
-def spread(th, tl, bh, bl, shapes):
+def spread(group, th, tl, bh, bl, shapes):
     depth = bh.shape[-1]
     vmem = pl.BlockSpec(memory_space=pltpu.VMEM)
     return pl.pallas_call(
-        spread_kernel,
+        functools.partial(spread_kernel, group),
         out_shape=[jax.ShapeDtypeStruct(s + (depth,), jnp.float32) for s in shapes],
         in_specs=[vmem] * 4,
         out_specs=[vmem] * len(shapes),
         compiler_params=pltpu.CompilerParams(vmem_limit_bytes=16 << 20),
         cost_estimate=pl.CostEstimate(
-            flops=6 * th.shape[0] * th.shape[1] * depth, bytes_accessed=6 << 20, transcendentals=0
+            flops=6 * CELLS * th.shape[1] * depth, bytes_accessed=6 << 20, transcendentals=0
         ),
         name="spread",
     )(th, tl, bh, bl)
@@ -304,35 +313,56 @@
     return lax.ppermute(cells, axis, [(i, (i + step) % count) for i in range(count)])
 
 
+def swap_a(cells):
+    count = lax.axis_size("gy")
+    return lax.ppermute(cells, "gy", [(j, j ^ 1) for j in range(count)])
+
+
+def swap_b(cells):
+    count = lax.axis_size("gy")
+    return lax.ppermute(cells, "gy", [(j, (j + (1 if j % 2 else -1)) % count) for j in range(count)])
+
+
 def per_device(tangent, hessian, kernel_rows, kernel_cols, kernel_depth):
     span_rows, span_cols, depth = tangent.shape
     reach = RADIUS
+    right = side_is_right()
+
+    def side_cols(cells, place):
+        return lax.dynamic_slice_in_dim(cells, place * reach, reach, 1)
+
+    def joined(from_a, from_b):
+        left, other = jnp.concatenate([from_a, from_b], 1), jnp.concatenate([from_b, from_a], 1)
+        return jnp.where(right == 1, other, left)
 
     north = shift(tangent[reach:], "gx", 1)
     south = shift(tangent[:reach], "gx", -1)
-    west = shift(tangent[:, reach:], "gy", 1)
-    east = shift(tangent[:, :reach], "gy", -1)
-
-    nh, nl, ch, cl, sh, sl, rh, rl, eh, el, bands, bands_t = build(kernel_rows, kernel_cols, kernel_depth, depth)
+    side_b = swap_b(side_cols(tangent, 1 - right))
+    side_a = swap_a(side_cols(tangent, right))
+
+    nh, nl, ch, cl, th, tl, bands, bands_t = build(kernel_rows, kernel_cols, kernel_depth, depth)
 
     sides = jnp.concatenate([north, south], 0)
-    corner_w = shift(sides[:, reach:], "gy", 1)
-    corner_e = shift(sides[:, :reach], "gy", -1)
-
-    partial = near((tangent, north, south, west, east), nh, nl)
-    to_w, to_e, bh, bl = middle(partial, corner_w, corner_e, ch, cl, bands, bands_t, eh, el, hessian)
-    from_e = shift(to_w, "gy", -1)
-    from_w = shift(to_e, "gy", 1)
-
-    edge_w, edge_e = spread(sh, sl, bh, bl, [(span_rows, reach)] * 2)
-    edge_from_e = shift(edge_w, "gy", -1)
-    edge_from_w = shift(edge_e, "gy", 1)
-
-    own, around = spread(rh, rl, bh, bl, [(span_rows, span_cols)] * 2)
-    around = around + jnp.concatenate([from_w, from_e], 1)
+    corner_b = swap_b(side_cols(sides, 1 - right))
+    corner_a = swap_a(side_cols(sides, right))
+
+    partial = near((tangent, north, south, side_a, side_b), nh, nl)
+    to_a, to_b, bh, bl = middle(partial, corner_a, corner_b, ch, cl, bands, bands_t, th, tl, hessian)
+    from_b = swap_b(to_b)
+    from_a = swap_a(to_a)
+
+    edge_a, edge_b = spread(2, th, tl, bh, bl, [(span_rows, reach)] * 2)
+    edge_from_b = swap_b(edge_b)
+    edge_from_a = swap_a(edge_a)
+
+    (around,) = spread(1, th, tl, bh, bl, [(span_rows, span_cols)])
+    around = around + joined(from_a, from_b)
     side_from_s = shift(around[:reach], "gx", -1)
     side_from_n = shift(around[reach:], "gx", 1)
-    own = own + jnp.concatenate([edge_from_w, edge_from_e], 1)
+
+    around, bh, bl = lax.optimization_barrier((around, bh, bl))
+    (own,) = spread(0, th, tl, bh, bl, [(span_rows, span_cols)])
+    own = lax.optimization_barrier(own + joined(edge_from_a, edge_from_b))
     return own + jnp.concatenate([side_from_n, side_from_s], 0)
 
 

time: 57.2 us -> 69.9 us (1.22)
  the two profiles are of different devices: /device:TPU:4 before, /device:TPU:1 now
where the time goes in v3:
time: 69.9 us; the launch traced here: 69.3 us
  starting transfers between devices  24.8 us (35%)
  Pallas kernels  19.2 us (27%)
  local copies, waits for them, and re-layouts  15.4 us (22%)
  waiting for transfers between devices  6.8 us (10%)
  other arithmetic  2.83 us (4%)
    ppermute x4, starting transfers between devices, shift(): lax.ppermute(cells, axis, [(i, (i + step) % count) for i in range(count)])  14 us
    unnamed x31, local copies, waits for them, and re-layouts  11.2 us
    ppermute x4, starting transfers between devices, swap_a(): return lax.ppermute(cells, 'gy', [(j, j ^ 1) for j in range(count)])  10.3 us
    pallas_call x1, Pallas kernels, build(): pl.pallas_call(build_kernel, out_shape=[jax.ShapeDtypeStruct(s, jnp.bfloa...  5.67 us
    pallas_call x1, Pallas kernels, near(): pl.pallas_call(near_kernel, out_shape=jax.ShapeDtypeStruct((DENSITIES * C...  5.22 us
    ppermute x4, waiting for transfers between devices, shift(): lax.ppermute(cells, axis, [(i, (i + step) % count) for i in range(count)])  5.18 us
    pallas_call x1, Pallas kernels, middle(): pl.pallas_call(middle_kernel, out_shape=[edge, edge, back, back], in_spec...  4.78 us
    pallas_call x3, Pallas kernels, spread(): pl.pallas_call(functools.partial(spread_kernel, group), out_shape=[jax.Sh...  3.5 us
  transfers between devices with their start and end apart: 12, of which 2 were waited for; matrix products, arithmetic and copies ran while one was open for 6% of the time, Pallas kernels for 21%

profile of v3, /device:TPU:1, one launch (start us, length us, event | category | flops | bytes accessed | tf_op | source)
XLA Modules:
  0.0 69.3 jit_solution(7917717640448796254)
XLA Ops:
  0.0 1.9 %fusion.3 = (f32[8,16,512]{2,1,0:T(8,128)}, f32[8,16,512]{2,1,0:T(8,128)}) fusion(f32[16,16,512]{2,1,0:T(8,128)} %own.1), kind=kLoop, calls=%fused_computation.12 | loop fusion | bytes 1048576 | tf_op jit(solution)/shard_map/slice | solution.py:339
  1.9 2.5 %collective-permute-start = (f32[8,16,512]{2,1,0:T(8,128)}, f32[8,16,512]{2,1,0:T(8,128)S(1)}, u32[]{:S(2)}, u32[]{:S(2)}) collective-permute-start(f32[8,16,512]{2,1,0:T(8,128)} %get-tuple-element.44), channel_id=1, source_target_pairs={{0,16},{16,32},{32,48},{48,64},{64,80},{80,96},{96,112},{112,128},... | collective-permute-start | bytes 786440 | tf_op jit(solution)/shard_map/ppermute | solution.py:313
  4.4 6.4 %collective-permute-start.1 = (f32[8,16,512]{2,1,0:T(8,128)}, f32[8,16,512]{2,1,0:T(8,128)}, u32[]{:S(2)}, u32[]{:S(2)}) collective-permute-start(f32[8,16,512]{2,1,0:T(8,128)} %get-tuple-element.43), channel_id=1, source_target_pairs={{0,240},{16,0},{32,16},{48,32},{64,48},{80,64},{96,80},{112,96},{1... | collective-permute-start | bytes 786440 | tf_op jit(solution)/shard_map/ppermute | solution.py:313
  10.8 1.1 %constant_dynamic-slice_fusion.2 = (f32[16,8,512]{2,1,0:T(8,128)S(1)}, f32[16,8,512]{2,1,0:T(8,128)S(1)}) fusion(f32[16,16,512]{2,1,0:T(8,128)} %own.1, s32[]{:T(128)S(6)} %select_n.21, s32[]{:T(128)S(6)} %select_n.20), kind=kLoop, calls=%fused_computation.9 | loop fusion | bytes 1048584 | tf_op jit(solution)/shard_map/dynamic_slice | solution.py:332
  11.8 1.0 %collective-permute-start.2 = (f32[16,8,512]{2,1,0:T(8,128)S(1)}, f32[16,8,512]{2,1,0:T(8,128)S(1)}, u32[]{:S(2)}, u32[]{:S(2)}) collective-permute-start(f32[16,8,512]{2,1,0:T(8,128)S(1)} %get-tuple-element.42), channel_id=1, source_target_pairs={{0,1},{1,0},{2,3},{3,2},{4,5},{5,4},{6,7},{7,6},{8,9},{9,8},{10,11... | collective-permute-start | bytes 786440 | tf_op jit(solution)/shard_map/ppermute | solution.py:318
  12.9 0.3 collective-permute-start.3
  13.2 0.7 convert_element_type.3.kd
  13.9 0.8 %copy-done.7 = s32[16,1024]{1,0:T(8,128)S(1)} copy-done((s32[16,1024]{1,0:T(8,128)S(1)}, s32[16,1024]{1,0:T(8,128)}, u32[]{:S(2)}) %copy-start.7) | copy-done | bytes 65560
  14.7 0.8 %copy-done.8 = s32[16,1024]{1,0:T(8,128)S(1)} copy-done((s32[16,1024]{1,0:T(8,128)S(1)}, s32[16,1024]{1,0:T(8,128)}, u32[]{:S(2)}) %copy-start.8) | copy-done | bytes 65560
  15.6 0.8 %copy-done.9 = s32[32,256]{1,0:T(8,128)S(1)} copy-done((s32[32,256]{1,0:T(8,128)S(1)}, s32[32,256]{1,0:T(8,128)}, u32[]{:S(2)}) %copy-start.9) | copy-done | bytes 32792
  16.3 0.8 %copy-done.10 = s32[32,256]{1,0:T(8,128)S(1)} copy-done((s32[32,256]{1,0:T(8,128)S(1)}, s32[32,256]{1,0:T(8,128)}, u32[]{:S(2)}) %copy-start.10) | copy-done | bytes 32792
  17.1 0.7 copy-done.11
  17.8 0.7 copy-done.12
  18.4 5.7 %build.1 = (bf16[1280,768]{1,0:T(8,128)(2,1)S(1)}, bf16[1280,768]{1,0:T(8,128)(2,1)S(1)}, bf16[1280,256]{1,0:T(8,128)(2,1)S(1)}, bf16[1280,256]{1,0:T(8,128)(2,1...) custom-call(f32[5,17]{1,0:T(8,128)S(1)} %copy-done.11, ...), custom_call_target="tpu_custom_call" | custom-call | flops 31457280 | bytes 16777216 | tf_op jit(solution)/shard_map/build/pallas_call | solution.py:166
  24.1 0.0 collective-permute-done.north
  24.2 0.0 collective-permute-done.1.south
  24.2 1.2 %constant_dynamic-update-slice_fusion = f32[16,16,512]{2,1,0:T(8,128)S(1)} fusion(f32[16,16,512]{2,1,0:T(8,128)S(1)} %constant_dynamic-update-slice_fusion.1, f32[8,16,512]{2,1,0:T(8,128)} %collective-permute-done.1.south), kind=kLoop, calls=%fused_computation.5 | loop fusion | bytes 524288 | tf_op jit(solution)/shard_map/concatenate | solution.py:345
  25.4 0.0 slice-start
  25.4 2.9 %collective-permute-start.4 = (f32[16,8,512]{2,1,0:T(8,128)S(1)}, f32[16,8,512]{2,1,0:T(8,128)S(1)}, u32[]{:S(2)}, u32[]{:S(2)}) collective-permute-start(f32[16,8,512]{2,1,0:T(8,128)S(1)} %get-tuple-element.40), channel_id=1, source_target_pairs={{0,1},{1,0},{2,3},{3,2},{4,5},{5,4},{6,7},{7,6},{8,9},{9,8},{10,11... | collective-permute-start | bytes 786440 | tf_op jit(solution)/shard_map/ppermute | solution.py:318
  28.4 0.0 collective-permute-start.5
  28.4 0.0 collective-permute-done.2.side_a
  28.4 0.0 collective-permute-done.3.side_b
  28.4 0.0 slice-start.1
  28.4 5.2 %near.1.partial = f32[1280,512]{1,0:T(8,128)S(1)} custom-call(f32[16,16,512]{2,1,0:T(8,128)S(1)} %copy-done.6, f32[8,16,512]{2,1,0:T(8,128)S(1)} %collective-permute-done.north, f32[8,16,512]{2,1,0:T(8,128)} %collective-permute-done.1.south, f32[16,8,512]{2,1,0:T(8,128)S(1)} %collective-permute-done.2.side_a, ...), custom_call_target="tpu_custom_call" | custom-call | flops 3019898880 | bytes 10485760 | tf_op jit(solution)/shard_map/near/pallas_call | solution.py:215
  33.6 0.0 collective-permute-done.4.corner_a
  33.6 1.6 %collective-permute-done.5.corner_b = f32[16,8,512]{2,1,0:T(8,128)S(1)} collective-permute-done((f32[16,8,512]{2,1,0:T(8,128)S(1)}, f32[16,8,512]{2,1,0:T(8,128)S(1)}, u32[]{:S(2)}, u32[]{:S(2)}) %collective-permute-start.5) | collective-permute-done | bytes 262176 | tf_op jit(solution)/shard_map/ppermute | solution.py:323
  35.3 4.8 %middle.1 = (f32[16,8,512]{2,1,0:T(8,128)S(1)}, f32[16,8,512]{2,1,0:T(8,128)S(1)}, bf16[1280,512]{1,0:T(8,128)(2,1)S(1)}, bf16[1280,512]{1,0:T(8,128)(2,1)S(1)}) custom-call(f32[1280,512]{1,0:T(8,128)S(1)} %near.1.partial, f32[16,8,512]{2,1,0:T(8,128)S(1)} %collective-permute-done.4.corner_a, f32[16,8,512]{2,1,0:T(8,128)S(1)} %collective-permute-done.5.corner_b, ...), custom_call_target="tpu_custom_call" | custom-call | flops 3355443200 | bytes 16777216 | tf_op jit(solution)/shard_map/middle/pallas_call | solution.py:266
  40.1 1.1 %copy-done.2 = bf16[1280,512]{1,0:T(8,128)(2,1)} copy-done((bf16[1280,512]{1,0:T(8,128)(2,1)}, bf16[1280,512]{1,0:T(8,128)(2,1)S(1)}, u32[]{:S(2)}) %copy-start.2) | copy-done | bytes 1310744
  41.1 1.1 %copy-done.4 = bf16[1280,512]{1,0:T(8,128)(2,1)} copy-done((bf16[1280,512]{1,0:T(8,128)(2,1)}, bf16[1280,512]{1,0:T(8,128)(2,1)S(1)}, u32[]{:S(2)}) %copy-start.4) | copy-done | bytes 1310744
  42.2 0.2 collective-permute-start.6
  42.4 3.5 %collective-permute-start.7 = (f32[16,8,512]{2,1,0:T(8,128)S(1)}, f32[16,8,512]{2,1,0:T(8,128)}, u32[]{:S(2)}, u32[]{:S(2)}) collective-permute-start(f32[16,8,512]{2,1,0:T(8,128)S(1)} %get-tuple-element.32), channel_id=1, source_target_pairs={{0,1},{1,0},{2,3},{3,2},{4,5},{5,4},{6,7},{7,6},{8,9},{9,8},{10,11... | collective-permute-start | bytes 786440 | tf_op jit(solution)/shard_map/ppermute | solution.py:318
  45.9 1.7 %copy-done.1 = bf16[1024,1280]{1,0:T(8,128)(2,1)S(1)} copy-done((bf16[1024,1280]{1,0:T(8,128)(2,1)S(1)}, bf16[1024,1280]{1,0:T(8,128)(2,1)}, u32[]{:S(2)}) %copy-start.1) | copy-done | bytes 2621464
  47.6 1.3 %copy-done.3 = bf16[1280,512]{1,0:T(8,128)(2,1)S(1)} copy-done((bf16[1280,512]{1,0:T(8,128)(2,1)S(1)}, bf16[1280,512]{1,0:T(8,128)(2,1)}, u32[]{:S(2)}) %copy-start.3) | copy-done | bytes 1310744
  49.0 1.3 %copy-done.5 = bf16[1280,512]{1,0:T(8,128)(2,1)S(1)} copy-done((bf16[1280,512]{1,0:T(8,128)(2,1)S(1)}, bf16[1280,512]{1,0:T(8,128)(2,1)}, u32[]{:S(2)}) %copy-start.5) | copy-done | bytes 1310744
  50.3 1.2 %spread.5 = (f32[16,8,512]{2,1,0:T(8,128)S(1)}, f32[16,8,512]{2,1,0:T(8,128)S(1)}) custom-call(bf16[1024,1280]{1,0:T(8,128)(2,1)S(1)} %get-tuple-element.21.th, bf16[1024,1280]{1,0:T(8,128)(2,1)S(1)} %copy-done.1, bf16[1280,512]{1,0:T(8,128)(2,1)S(1)} %copy-done.3, bf16[1280,512]{1,0:T(8,128)(2,1)S(1)} %copy-done.5), custom_call_target="tpu_custom_call" | custom-call | flops 1006632960 | bytes 6291456 | tf_op jit(solution)/shard_map/spread/pallas_call | solution.py:298
  51.4 0.1 collective-permute-start.8
  51.5 2.8 %collective-permute-start.9 = (f32[16,8,512]{2,1,0:T(8,128)S(1)}, f32[16,8,512]{2,1,0:T(8,128)S(1)}, u32[]{:S(2)}, u32[]{:S(2)}) collective-permute-start(f32[16,8,512]{2,1,0:T(8,128)S(1)} %get-tuple-element.36), channel_id=1, source_target_pairs={{0,1},{1,0},{2,3},{3,2},{4,5},{5,4},{6,7},{7,6},{8,9},{9,8},{10,11... | collective-permute-start | bytes 786440 | tf_op jit(solution)/shard_map/ppermute | solution.py:318
  54.3 1.2 %spread.3 = f32[16,16,512]{2,1,0:T(8,128)S(1)} custom-call(bf16[1024,1280]{1,0:T(8,128)(2,1)S(1)} %get-tuple-element.21.th, bf16[1024,1280]{1,0:T(8,128)(2,1)S(1)} %copy-done.1, bf16[1280,512]{1,0:T(8,128)(2,1)S(1)} %copy-done.3, bf16[1280,512]{1,0:T(8,128)(2,1)S(1)} %copy-done.5), custom_call_target="tpu_custom_call" | custom-call | flops 1006632960 | bytes 6291456 | tf_op jit(solution)/shard_map/spread/pallas_call | solution.py:298
  55.5 0.0 collective-permute-done.6
  55.5 0.0 collective-permute-done.7
  55.5 1.2 %fusion = f32[16,16,512]{2,1,0:T(8,128)S(1)} fusion(f32[16,16,512]{2,1,0:T(8,128)S(1)} %spread.3, f32[16,8,512]{2,1,0:T(8,128)} %collective-permute-done.7, f32[16,8,512]{2,1,0:T(8,128)S(1)} %collective-permute-done.6, pred[]{:T(512)S(6)} %eq.4), kind=kLoop, calls=%fused_computation.1 | loop fusion | flops 524288 | bytes 1572865 | tf_op jit(solution)/shard_map/add | solution.py:359
  56.7 0.1 collective-permute-start.10
  56.8 5.1 %collective-permute-start.11 = (f32[8,16,512]{2,1,0:T(8,128)S(1)}, f32[8,16,512]{2,1,0:T(8,128)S(1)}, u32[]{:S(2)}, u32[]{:S(2)}) collective-permute-start(f32[8,16,512]{2,1,0:T(8,128)S(1)} %get-tuple-element.38), channel_id=1, source_target_pairs={{0,240},{16,0},{32,16},{48,32},{64,48},{80,64},{96,80},{112,96},{1... | collective-permute-start | bytes 786440 | tf_op jit(solution)/shard_map/ppermute | solution.py:313
  61.9 1.2 %spread.4 = f32[16,16,512]{2,1,0:T(8,128)S(1)} custom-call(bf16[1024,1280]{1,0:T(8,128)(2,1)S(1)} %get-tuple-element.21.th, bf16[1024,1280]{1,0:T(8,128)(2,1)S(1)} %copy-done.1, bf16[1280,512]{1,0:T(8,128)(2,1)S(1)} %copy-done.3, bf16[1280,512]{1,0:T(8,128)(2,1)S(1)} %copy-done.5), custom_call_target="tpu_custom_call" | custom-call | flops 1006632960 | bytes 6291456 | tf_op jit(solution)/shard_map/spread/pallas_call | solution.py:298
  63.1 0.0 collective-permute-done.9
  63.1 0.1 fusion.1
  63.2 5.2 %collective-permute-done.10 = f32[8,16,512]{2,1,0:T(8,128)S(1)} collective-permute-done((f32[8,16,512]{2,1,0:T(8,128)S(1)}, f32[8,16,512]{2,1,0:T(8,128)S(1)}, u32[]{:S(2)}, u32[]{:S(2)}) %collective-permute-start.10) | collective-permute-done | bytes 262176 | tf_op jit(solution)/shard_map/ppermute | solution.py:313
  68.4 0.9 %maximum_add_fusion = f32[16,16,512]{2,1,0:T(8,128)} fusion(f32[16,16,512]{2,1,0:T(8,128)S(1)} %fusion.1, f32[8,16,512]{2,1,0:T(8,128)S(1)} %collective-permute-done.11, f32[8,16,512]{2,1,0:T(8,128)S(1)} %collective-permute-done.10), kind=kLoop, calls=%fused_computation.4 | loop fusion | flops 262144 | bytes 1572864 | tf_op jit(solution)/shard_map/add | solution.py:366
  (23 shorter events, 0.1 us)
Async XLA Ops:
  0.0 28.4 %copy-start.6 = (f32[16,16,512]{2,1,0:T(8,128)S(1)}, f32[16,16,512]{2,1,0:T(8,128)}, u32[]{:S(2)}) copy-start(f32[16,16,512]{2,1,0:T(8,128)} %own.1) | copy-start | bytes 1572868
  1.9 22.2 %collective-permute-start = (f32[8,16,512]{2,1,0:T(8,128)}, f32[8,16,512]{2,1,0:T(8,128)S(1)}, u32[]{:S(2)}, u32[]{:S(2)}) collective-permute-start(f32[8,16,512]{2,1,0:T(8,128)} %get-tuple-element.44), channel_id=1, source_target_pairs={{0,16},{16,32},{32,48},{48,64},{64,80},{80,96},{96,112},{112,128},... | collective-permute-start | bytes 786440 | tf_op jit(solution)/shard_map/ppermute | solution.py:313
  4.4 19.8 %collective-permute-start.1 = (f32[8,16,512]{2,1,0:T(8,128)}, f32[8,16,512]{2,1,0:T(8,128)}, u32[]{:S(2)}, u32[]{:S(2)}) collective-permute-start(f32[8,16,512]{2,1,0:T(8,128)} %get-tuple-element.43), channel_id=1, source_target_pairs={{0,240},{16,0},{32,16},{48,32},{64,48},{80,64},{96,80},{112,96},{1... | collective-permute-start | bytes 786440 | tf_op jit(solution)/shard_map/ppermute | solution.py:313
  11.8 16.5 %collective-permute-start.2 = (f32[16,8,512]{2,1,0:T(8,128)S(1)}, f32[16,8,512]{2,1,0:T(8,128)S(1)}, u32[]{:S(2)}, u32[]{:S(2)}) collective-permute-start(f32[16,8,512]{2,1,0:T(8,128)S(1)} %get-tuple-element.42), channel_id=1, source_target_pairs={{0,1},{1,0},{2,3},{3,2},{4,5},{5,4},{6,7},{7,6},{8,9},{9,8},{10,11... | collective-permute-start | bytes 786440 | tf_op jit(solution)/shard_map/ppermute | solution.py:318
  12.9 15.5 %collective-permute-start.3 = (f32[16,8,512]{2,1,0:T(8,128)S(1)}, f32[16,8,512]{2,1,0:T(8,128)S(1)}, u32[]{:S(2)}, u32[]{:S(2)}) collective-permute-start(f32[16,8,512]{2,1,0:T(8,128)S(1)} %get-tuple-element.41), channel_id=1, source_target_pairs={{0,15},{1,2},{2,1},{3,4},{4,3},{5,6},{6,5},{7,8},{8,7},{9,10},{10,... | collective-permute-start | bytes 786440 | tf_op jit(solution)/shard_map/ppermute | solution.py:323
  13.9 0.8 %copy-start.7 = (s32[16,1024]{1,0:T(8,128)S(1)}, s32[16,1024]{1,0:T(8,128)}, u32[]{:S(2)}) copy-start(s32[16,1024]{1,0:T(8,128)} %constant.23.clone.row_off) | copy-start | bytes 196612
  14.7 0.8 %copy-start.8 = (s32[16,1024]{1,0:T(8,128)S(1)}, s32[16,1024]{1,0:T(8,128)}, u32[]{:S(2)}) copy-start(s32[16,1024]{1,0:T(8,128)} %constant.24.clone.col_off) | copy-start | bytes 196612
  15.6 0.8 %copy-start.9 = (s32[32,256]{1,0:T(8,128)S(1)}, s32[32,256]{1,0:T(8,128)}, u32[]{:S(2)}) copy-start(s32[32,256]{1,0:T(8,128)} %constant.25.clone.row_span) | copy-start | bytes 98308
  16.3 0.8 %copy-start.10 = (s32[32,256]{1,0:T(8,128)S(1)}, s32[32,256]{1,0:T(8,128)}, u32[]{:S(2)}) copy-start(s32[32,256]{1,0:T(8,128)} %constant.26.clone.col_span) | copy-start | bytes 98308
  17.1 0.7 copy-start.11
  17.8 0.7 copy-start.12
  24.1 11.1 %copy-start = (bf16[1024,1280]{1,0:T(8,128)(2,1)}, bf16[1024,1280]{1,0:T(8,128)(2,1)S(1)}, u32[]{:S(2)}) copy-start(bf16[1024,1280]{1,0:T(8,128)(2,1)S(1)} %get-tuple-element.22.tl) | copy-start | bytes 7864324
  25.4 9.9 %slice-start = ((s8[6553600]{0:T(1024)(128)(4,1)}), s8[4194304]{0:T(1024)(128)(4,1)S(1)}, s32[]{:S(2)}) async-start(s8[6553600]{0:T(1024)(128)(4,1)} %bitcast), calls=%async_computation | async-start | bytes 8388608
  25.4 8.2 %collective-permute-start.4 = (f32[16,8,512]{2,1,0:T(8,128)S(1)}, f32[16,8,512]{2,1,0:T(8,128)S(1)}, u32[]{:S(2)}, u32[]{:S(2)}) collective-permute-start(f32[16,8,512]{2,1,0:T(8,128)S(1)} %get-tuple-element.40), channel_id=1, source_target_pairs={{0,1},{1,0},{2,3},{3,2},{4,5},{5,4},{6,7},{7,6},{8,9},{9,8},{10,11... | collective-permute-start | bytes 786440 | tf_op jit(solution)/shard_map/ppermute | solution.py:318
  28.4 6.9 %collective-permute-start.5 = (f32[16,8,512]{2,1,0:T(8,128)S(1)}, f32[16,8,512]{2,1,0:T(8,128)S(1)}, u32[]{:S(2)}, u32[]{:S(2)}) collective-permute-start(f32[16,8,512]{2,1,0:T(8,128)S(1)} %get-tuple-element.39), channel_id=1, source_target_pairs={{0,15},{1,2},{2,1},{3,4},{4,3},{5,6},{6,5},{7,8},{8,7},{9,10},{10,... | collective-permute-start | bytes 786440 | tf_op jit(solution)/shard_map/ppermute | solution.py:323
  28.4 6.9 %slice-start.1 = ((s8[6553600]{0:T(1024)(128)(4,1)}), s8[2359296]{0:T(1024)(128)(4,1)S(1)}, s32[]{:S(2)}) async-start(s8[6553600]{0:T(1024)(128)(4,1)} %bitcast), calls=%async_computation.1 | async-start | bytes 4718592
  40.0 1.1 %copy-start.2 = (bf16[1280,512]{1,0:T(8,128)(2,1)}, bf16[1280,512]{1,0:T(8,128)(2,1)S(1)}, u32[]{:S(2)}) copy-start(bf16[1280,512]{1,0:T(8,128)(2,1)S(1)} %get-tuple-element.33.bh) | copy-start | bytes 3932164
  41.1 1.1 %copy-start.4 = (bf16[1280,512]{1,0:T(8,128)(2,1)}, bf16[1280,512]{1,0:T(8,128)(2,1)S(1)}, u32[]{:S(2)}) copy-start(bf16[1280,512]{1,0:T(8,128)(2,1)S(1)} %get-tuple-element.34.bl) | copy-start | bytes 3932164
  42.2 13.3 %collective-permute-start.6 = (f32[16,8,512]{2,1,0:T(8,128)S(1)}, f32[16,8,512]{2,1,0:T(8,128)S(1)}, u32[]{:S(2)}, u32[]{:S(2)}) collective-permute-start(f32[16,8,512]{2,1,0:T(8,128)S(1)} %get-tuple-element.31), channel_id=1, source_target_pairs={{0,15},{1,2},{2,1},{3,4},{4,3},{5,6},{6,5},{7,8},{8,7},{9,10},{10,... | collective-permute-start | bytes 786440 | tf_op jit(solution)/shard_map/ppermute | solution.py:323
  42.4 13.1 %collective-permute-start.7 = (f32[16,8,512]{2,1,0:T(8,128)S(1)}, f32[16,8,512]{2,1,0:T(8,128)}, u32[]{:S(2)}, u32[]{:S(2)}) collective-permute-start(f32[16,8,512]{2,1,0:T(8,128)S(1)} %get-tuple-element.32), channel_id=1, source_target_pairs={{0,1},{1,0},{2,3},{3,2},{4,5},{5,4},{6,7},{7,6},{8,9},{9,8},{10,11... | collective-permute-start | bytes 786440 | tf_op jit(solution)/shard_map/ppermute | solution.py:318
  45.9 1.7 %copy-start.1 = (bf16[1024,1280]{1,0:T(8,128)(2,1)S(1)}, bf16[1024,1280]{1,0:T(8,128)(2,1)}, u32[]{:S(2)}) copy-start(bf16[1024,1280]{1,0:T(8,128)(2,1)} %copy-done) | copy-start | bytes 7864324
  47.6 1.3 %copy-start.3 = (bf16[1280,512]{1,0:T(8,128)(2,1)S(1)}, bf16[1280,512]{1,0:T(8,128)(2,1)}, u32[]{:S(2)}) copy-start(bf16[1280,512]{1,0:T(8,128)(2,1)} %copy-done.2) | copy-start | bytes 3932164
  49.0 1.3 %copy-start.5 = (bf16[1280,512]{1,0:T(8,128)(2,1)S(1)}, bf16[1280,512]{1,0:T(8,128)(2,1)}, u32[]{:S(2)}) copy-start(bf16[1280,512]{1,0:T(8,128)(2,1)} %copy-done.4) | copy-start | bytes 3932164
  51.4 11.6 %collective-permute-start.8 = (f32[16,8,512]{2,1,0:T(8,128)S(1)}, f32[16,8,512]{2,1,0:T(8,128)S(1)}, u32[]{:S(2)}, u32[]{:S(2)}) collective-permute-start(f32[16,8,512]{2,1,0:T(8,128)S(1)} %get-tuple-element.35), channel_id=1, source_target_pairs={{0,15},{1,2},{2,1},{3,4},{4,3},{5,6},{6,5},{7,8},{8,7},{9,10},{10,... | collective-permute-start | bytes 786440 | tf_op jit(solution)/shard_map/ppermute | solution.py:323
  51.5 11.5 %collective-permute-start.9 = (f32[16,8,512]{2,1,0:T(8,128)S(1)}, f32[16,8,512]{2,1,0:T(8,128)S(1)}, u32[]{:S(2)}, u32[]{:S(2)}) collective-permute-start(f32[16,8,512]{2,1,0:T(8,128)S(1)} %get-tuple-element.36), channel_id=1, source_target_pairs={{0,1},{1,0},{2,3},{3,2},{4,5},{5,4},{6,7},{7,6},{8,9},{9,8},{10,11... | collective-permute-start | bytes 786440 | tf_op jit(solution)/shard_map/ppermute | solution.py:318
  56.7 11.6 %collective-permute-start.10 = (f32[8,16,512]{2,1,0:T(8,128)S(1)}, f32[8,16,512]{2,1,0:T(8,128)S(1)}, u32[]{:S(2)}, u32[]{:S(2)}) collective-permute-start(f32[8,16,512]{2,1,0:T(8,128)S(1)} %get-tuple-element.37), channel_id=1, source_target_pairs={{0,16},{16,32},{32,48},{48,64},{64,80},{80,96},{96,112},{112,128},... | collective-permute-start | bytes 786440 | tf_op jit(solution)/shard_map/ppermute | solution.py:313
  56.8 11.5 %collective-permute-start.11 = (f32[8,16,512]{2,1,0:T(8,128)S(1)}, f32[8,16,512]{2,1,0:T(8,128)S(1)}, u32[]{:S(2)}, u32[]{:S(2)}) collective-permute-start(f32[8,16,512]{2,1,0:T(8,128)S(1)} %get-tuple-element.38), channel_id=1, source_target_pairs={{0,240},{16,0},{32,16},{48,32},{64,48},{80,64},{96,80},{112,96},{1... | collective-permute-start | bytes 786440 | tf_op jit(solution)/shard_map/ppermute | solution.py:313

commit v4 on v3

--- a/solution.py
+++ b/solution.py
@@ -2,7 +2,6 @@
 
 import jax
 import jax.numpy as jnp
-import numpy as np
 from jax import lax
 from jax.experimental import pallas as pl
 from jax.experimental.pallas import tpu as pltpu
@@ -15,44 +14,7 @@
 CELLS = TILE * TILE
 
 
-def piece_cells():
-    inner = list(range(TILE))
-    outer = list(range(-RADIUS, 0)) + list(range(TILE, TILE + RADIUS))
-    west, east = list(range(-RADIUS, 0)), list(range(TILE, TILE + RADIUS))
-    blocks = [
-        (inner, inner),
-        (outer, inner),
-        (inner, west),
-        (inner, east),
-        (outer, west),
-        (outer, east),
-    ]
-    return blocks
-
-
-def cell_arrays():
-    rows, cols = [], []
-    for block_rows, block_cols in piece_cells():
-        for row in block_rows:
-            for col in block_cols:
-                rows.append(row)
-                cols.append(col)
-    return np.array(rows, np.int32), np.array(cols, np.int32)
-
-
-def offset_tables():
-    rows, cols = cell_arrays()
-    tile = np.arange(TILE, dtype=np.int32)
-    span = np.arange(-RADIUS, TILE + RADIUS, dtype=np.int32)
-    tile_rows, tile_cols = np.repeat(tile, TILE), np.tile(tile, TILE)
-    return (
-        rows[None, :] - tile[:, None],
-        cols[None, :] - tile[:, None],
-        span[:, None] - tile_rows[None, :],
-        span[:, None] - tile_cols[None, :],
-    )
-
-
+LANES = 128
 TURN = TILE + RADIUS
 
 
@@ -60,42 +22,46 @@
     return 1 - lax.rem(lax.axis_index("gy"), 2)
 
 
-def taps_at(weights, density, offsets):
+def taps_at(weights, first, density, offsets):
     total = jnp.zeros(offsets.shape, jnp.float32)
     for tap in range(TAPS):
-        total = jnp.where(offsets == tap - RADIUS, weights[density, tap], total)
+        total = jnp.where(offsets == tap - RADIUS, weights[first + density, tap], total)
     return total
 
 
-def taps_of_all(weights, offsets):
+def taps_of_all(weights, first, offsets):
     totals = [jnp.zeros(offsets.shape, jnp.float32)] * DENSITIES
     for tap in range(TAPS):
         here = offsets == tap - RADIUS
-        totals = [jnp.where(here, weights[a, tap], totals[a]) for a in range(DENSITIES)]
+        totals = [jnp.where(here, weights[first + a, tap], totals[a]) for a in range(DENSITIES)]
     return totals
 
 
-LANES = 128
-
-
-def build_kernel(
-    kr, kc, kd, row_off, col_off, row_span, col_span,
-    nh, nl, ch, cl, th, tl, bands, bands_t
-):
-    turn = TURN * side_is_right()
+ROWS, COLS, DEPTH = 0, DENSITIES, 2 * DENSITIES
+
+
+def build_kernel(weights, nh, nl, ch, cl, th, tl, bands, bands_t):
+    right = side_is_right()
+    iota = lambda shape, dim: lax.broadcasted_iota(jnp.int32, shape, dim)
 
     def put(high_ref, low_ref, start, lanes, values):
         high, low = halves(values)
         high_ref[start : start + TILE, lanes] = high
         low_ref[start : start + TILE, lanes] = low
 
-    def forward(high_ref, low_ref, first, side):
+    def forward(high_ref, low_ref, first):
         def chunk(index, carry):
-            toward = turn * ((index == side).astype(jnp.int32) - (index == side + 1).astype(jnp.int32))
-            source = pl.ds(pl.multiple_of(first + index * LANES, LANES), LANES)
             lanes = pl.ds(pl.multiple_of(index * LANES, LANES), LANES)
-            by_row = taps_of_all(kr, row_off[:, source])
-            by_col = taps_of_all(kc, col_off[:, source] + toward)
+            group, half = (first + index) // 2, (first + index) % 2
+            lane, tile_place = iota((TILE, LANES), 1), iota((TILE, LANES), 0)
+            wide, slim = lane >> 4, lane >> 3
+            row = jnp.where(group == 2, slim, jnp.where(slim < RADIUS, slim - RADIUS, slim + RADIUS))
+            row = jnp.where(group == 1, wide - RADIUS + TURN * half, row)
+            row = jnp.where(group == 0, wide + RADIUS * half, row)
+            side = half + right - 2 * half * right
+            col = jnp.where(group < 2, lane & 15, (lane & 7) - RADIUS + TURN * side)
+            by_row = taps_of_all(weights, ROWS, row - tile_place)
+            by_col = taps_of_all(weights, COLS, col - tile_place)
             for a in range(DENSITIES):
                 for r in range(TILE):
                     put(high_ref, low_ref, a * CELLS + r * TILE, lanes, by_row[a][r : r + 1] * by_col[a])
@@ -103,17 +69,18 @@
 
         lax.fori_loop(0, high_ref.shape[1] // LANES, chunk, 0)
 
-    forward(nh, nl, 0, 4)
-    forward(ch, cl, 3 * CELLS, 0)
+    forward(nh, nl, 0)
+    forward(ch, cl, 6)
 
     def transposes(index, carry):
-        density = index // 2
-        source = pl.ds(pl.multiple_of((index % 2) * LANES, LANES), LANES)
+        density, half = index // 2, index % 2
         lanes = pl.ds(pl.multiple_of(index * LANES, LANES), LANES)
-        by_row = taps_at(kr, density, row_span[:, source])
-        place = lax.broadcasted_iota(jnp.int32, (TILE + 2 * RADIUS, LANES), 0)
-        toward = jnp.where(place < RADIUS, turn, jnp.where(place < TILE + RADIUS, 0, -turn))
-        by_col = taps_at(kc, density, col_span[:, source] + toward)
+        shape = (TILE + 2 * RADIUS, LANES)
+        place, lane = iota(shape, 0), iota(shape, 1)
+        turn = TURN * right
+        turned = place - RADIUS + jnp.where(place < RADIUS, turn, jnp.where(place < TILE + RADIUS, 0, -turn))
+        by_row = taps_at(weights, ROWS, density, place - RADIUS - (lane >> 4) - RADIUS * half)
+        by_col = taps_at(weights, COLS, density, turned - (lane & 15))
         row = lambda r: by_row[r + RADIUS : r + RADIUS + 1]
         inner = list(range(TILE))
         outer = list(range(-RADIUS, 0)) + list(range(TILE, TILE + RADIUS))
@@ -138,15 +105,15 @@
             for start in range(0, LANES, TILE):
                 shape = (TILE, LANES)
                 offsets = sign * (
-                    start + lax.broadcasted_iota(jnp.int32, shape, 0) - lax.broadcasted_iota(jnp.int32, shape, 1)
+                    start + iota(shape, 0) - iota(shape, 1)
                 )
-                part = taps_at(kd, density, offsets).astype(jnp.bfloat16)
+                part = taps_at(weights, DEPTH, density, offsets).astype(jnp.bfloat16)
                 for block in range(count):
                     base = block * LANES
                     ref[density, base + start : base + start + TILE, base : base + LANES] = part
                 for step, near_edge in ((1, start == 0), (-1, start == LANES - TILE)):
                     if near_edge:
-                        part = taps_at(kd, density, offsets + sign * step * LANES).astype(jnp.bfloat16)
+                        part = taps_at(weights, DEPTH, density, offsets + sign * step * LANES).astype(jnp.bfloat16)
                         for block in range(count):
                             if 0 <= block + step < count:
                                 base, across = (block + step) * LANES, block * LANES
@@ -166,17 +133,12 @@
     return pl.pallas_call(
         build_kernel,
         out_shape=[jax.ShapeDtypeStruct(s, jnp.bfloat16) for s in shapes],
-        in_specs=[smem] * 3 + [vmem] * 4,
+        in_specs=[smem],
         out_specs=[vmem] * len(shapes),
         compiler_params=pltpu.CompilerParams(vmem_limit_bytes=24 << 20),
         cost_estimate=pl.CostEstimate(flops=30 << 20, bytes_accessed=16 << 20, transcendentals=0),
         name="build",
-    )(
-        kernel_rows,
-        kernel_cols,
-        kernel_depth.astype(jnp.float32),
-        *[jnp.asarray(table.astype(np.int32)) for table in offset_tables()],
-    )
+    )(jnp.concatenate([kernel_rows, kernel_cols, kernel_depth.astype(jnp.float32)], 0))
 
 
 def halves(values):
@@ -308,6 +270,30 @@
     )(th, tl, bh, bl)
 
 
+def cut_kernel(tangent, last, first, side_a, side_b):
+    right = side_is_right()
+    cols = lambda place: pl.ds(pl.multiple_of(place * RADIUS, RADIUS), RADIUS)
+    last[...] = tangent[RADIUS:]
+    first[...] = tangent[:RADIUS]
+    side_a[...] = tangent[:, cols(right)]
+    side_b[...] = tangent[:, cols(1 - right)]
+
+
+def cut(tangent):
+    span_rows, span_cols, depth = tangent.shape
+    shapes = [(RADIUS, span_cols)] * 2 + [(span_rows, RADIUS)] * 2
+    vmem = pl.BlockSpec(memory_space=pltpu.VMEM)
+    return pl.pallas_call(
+        cut_kernel,
+        out_shape=[jax.ShapeDtypeStruct(s + (depth,), jnp.float32) for s in shapes],
+        in_specs=[vmem],
+        out_specs=[vmem] * 4,
+        compiler_params=pltpu.CompilerParams(vmem_limit_bytes=8 << 20),
+        cost_estimate=pl.CostEstimate(flops=0, bytes_accessed=3 << 20, transcendentals=0),
+        name="cut",
+    )(tangent)
+
+
 def shift(cells, axis, step):
     count = lax.axis_size(axis)
     return lax.ppermute(cells, axis, [(i, (i + step) % count) for i in range(count)])
@@ -329,16 +315,17 @@
     right = side_is_right()
 
     def side_cols(cells, place):
-        return lax.dynamic_slice_in_dim(cells, place * reach, reach, 1)
+        return jnp.where(place == 1, cells[:, reach:], cells[:, :reach])
 
     def joined(from_a, from_b):
         left, other = jnp.concatenate([from_a, from_b], 1), jnp.concatenate([from_b, from_a], 1)
         return jnp.where(right == 1, other, left)
 
-    north = shift(tangent[reach:], "gx", 1)
-    south = shift(tangent[:reach], "gx", -1)
-    side_b = swap_b(side_cols(tangent, 1 - right))
-    side_a = swap_a(side_cols(tangent, right))
+    last, first, cols_a, cols_b = cut(tangent)
+    north = shift(last, "gx", 1)
+    south = shift(first, "gx", -1)
+    side_b = swap_b(cols_b)
+    side_a = swap_a(cols_a)
 
     nh, nl, ch, cl, th, tl, bands, bands_t = build(kernel_rows, kernel_cols, kernel_depth, depth)
 

time: 69.9 us -> 58.9 us (0.84)
  the two profiles are of different devices: /device:TPU:1 before, /device:TPU:4 now
where the time goes in v4:
time: 58.9 us; the launch traced here: 58 us
  waiting for transfers between devices  18.4 us (31%)
  Pallas kernels  17.9 us (30%)
  starting transfers between devices  17.8 us (30%)
  other arithmetic  2.51 us (4%)
  local copies, waits for them, and re-layouts  1.14 us (2%)
    ppermute x4, waiting for transfers between devices, swap_b(): lax.ppermute(cells, 'gy', [(j, (j + (1 if j % 2 else -1)) % count) for j...  9.42 us
    ppermute x4, waiting for transfers between devices, shift(): lax.ppermute(cells, axis, [(i, (i + step) % count) for i in range(count)])  8.98 us
    ppermute x4, starting transfers between devices, swap_b(): lax.ppermute(cells, 'gy', [(j, (j + (1 if j % 2 else -1)) % count) for j...  8.96 us
    ppermute x4, starting transfers between devices, shift(): lax.ppermute(cells, axis, [(i, (i + step) % count) for i in range(count)])  8.59 us
    pallas_call x1, Pallas kernels, build(): pl.pallas_call(build_kernel, out_shape=[jax.ShapeDtypeStruct(s, jnp.bfloa...  5.64 us
    pallas_call x1, Pallas kernels, middle(): pl.pallas_call(middle_kernel, out_shape=[edge, edge, back, back], in_spec...  4.6 us
    pallas_call x1, Pallas kernels, near(): pl.pallas_call(near_kernel, out_shape=jax.ShapeDtypeStruct((DENSITIES * C...  4.11 us
    pallas_call x3, Pallas kernels, spread(): pl.pallas_call(functools.partial(spread_kernel, group), out_shape=[jax.Sh...  3.5 us
  transfers between devices with their start and end apart: 12, of which 5 were waited for; matrix products, arithmetic and copies ran while one was open for 3% of the time, Pallas kernels for 23%

profile of v4, /device:TPU:4, one launch (start us, length us, event | category | flops | bytes accessed | tf_op | source)
XLA Modules:
  0.0 58.0 jit_solution(5118156376954307033)
XLA Ops:
  0.0 0.0 copy-start
  0.0 1.0 %copy-done = f32[16,16,512]{2,1,0:T(8,128)S(1)} copy-done((f32[16,16,512]{2,1,0:T(8,128)S(1)}, f32[16,16,512]{2,1,0:T(8,128)}, u32[]{:S(2)}) %copy-start) | copy-done | bytes 524312
  1.0 0.0 copy-start.1
  1.0 0.1 cut.1
  1.1 2.0 %collective-permute-start = (f32[8,16,512]{2,1,0:T(8,128)S(1)}, f32[8,16,512]{2,1,0:T(8,128)S(1)}, u32[]{:S(2)}, u32[]{:S(2)}) collective-permute-start(f32[8,16,512]{2,1,0:T(8,128)S(1)} %get-tuple-element.27), channel_id=1, source_target_pairs={{0,16},{16,32},{32,48},{48,64},{64,80},{80,96},{96,112},{112,128},... | collective-permute-start | bytes 786440 | tf_op jit(solution)/shard_map/ppermute | solution.py:299
  3.1 4.0 %collective-permute-start.1 = (f32[8,16,512]{2,1,0:T(8,128)S(1)}, f32[8,16,512]{2,1,0:T(8,128)S(1)}, u32[]{:S(2)}, u32[]{:S(2)}) collective-permute-start(f32[8,16,512]{2,1,0:T(8,128)S(1)} %get-tuple-element.28), channel_id=1, source_target_pairs={{0,240},{16,0},{32,16},{48,32},{64,48},{80,64},{96,80},{112,96},{1... | collective-permute-start | bytes 786440 | tf_op jit(solution)/shard_map/ppermute | solution.py:299
  7.1 0.0 collective-permute-start.2
  7.1 4.7 %collective-permute-start.3 = (f32[16,8,512]{2,1,0:T(8,128)S(1)}, f32[16,8,512]{2,1,0:T(8,128)S(1)}, u32[]{:S(2)}, u32[]{:S(2)}) collective-permute-start(f32[16,8,512]{2,1,0:T(8,128)S(1)} %get-tuple-element.30), channel_id=1, source_target_pairs={{0,15},{1,2},{2,1},{3,4},{4,3},{5,6},{6,5},{7,8},{8,7},{9,10},{10,... | collective-permute-start | bytes 786440 | tf_op jit(solution)/shard_map/ppermute | solution.py:309
  11.7 0.7 %convert_element_type.3 = f32[5,17]{1,0:T(8,128)S(1)} convert(bf16[5,17]{1,0:T(8,128)(2,1)} %param.9) | non-fusion elementwise | flops 85 | bytes 510 | tf_op jit(solution)/shard_map/convert_element_type | solution.py:141
  12.4 0.7 %pad_maximum_fusion.weights = f32[15,17]{1,0:T(8,128)S(1)} fusion(f32[5,17]{1,0:T(8,128)S(1)} %convert_element_type.3, f32[5,17]{1,0:T(8,128)} %param.8, f32[5,17]{1,0:T(8,128)} %param.7), kind=kLoop, calls=%fused_computation.7 | loop fusion | flops 510 | bytes 2040 | tf_op jit(solution)/shard_map/concatenate | solution.py:141
  13.1 5.6 %build.1 = (bf16[1280,768]{1,0:T(8,128)(2,1)S(1)}, bf16[1280,768]{1,0:T(8,128)(2,1)S(1)}, bf16[1280,256]{1,0:T(8,128)(2,1)S(1)}, bf16[1280,256]{1,0:T(8,128)(2,1...) custom-call(f32[15,17]{1,0:T(8,128)S(1)} %pad_maximum_fusion.weights), custom_call_target="tpu_custom_call" | custom-call | flops 31457280 | bytes 16777216 | tf_op jit(solution)/shard_map/build/pallas_call | solution.py:133
  18.8 0.0 collective-permute-done.north
  18.8 0.0 collective-permute-done.1.south
  18.9 0.0 slice-start
  18.9 0.1 collective-permute-start.4
  19.0 0.1 collective-permute-start.5
  19.1 0.0 collective-permute-done.2.side_a
  19.1 2.9 %collective-permute-done.3.side_b = f32[16,8,512]{2,1,0:T(8,128)S(1)} collective-permute-done((f32[16,8,512]{2,1,0:T(8,128)S(1)}, f32[16,8,512]{2,1,0:T(8,128)S(1)}, u32[]{:S(2)}, u32[]{:S(2)}) %collective-permute-start.3) | collective-permute-done | bytes 262176 | tf_op jit(solution)/shard_map/ppermute | solution.py:309
  22.0 0.0 copy-done.1
  22.0 0.0 slice-start.1
  22.0 4.1 %near.1.partial = f32[1280,512]{1,0:T(8,128)S(1)} custom-call(f32[16,16,512]{2,1,0:T(8,128)S(1)} %copy-done.1, f32[8,16,512]{2,1,0:T(8,128)S(1)} %collective-permute-done.north, f32[8,16,512]{2,1,0:T(8,128)S(1)} %collective-permute-done.1.south, f32[16,8,512]{2,1,0:T(8,128)S(1)} %collective-permute-done.2.side_a, ...), custom_call_target="tpu_custom_call" | custom-call | flops 3019898880 | bytes 10485760 | tf_op jit(solution)/shard_map/near/pallas_call | solution.py:177
  26.2 0.0 collective-permute-done.4.corner_a
  26.2 2.3 %collective-permute-done.5.corner_b = f32[16,8,512]{2,1,0:T(8,128)S(1)} collective-permute-done((f32[16,8,512]{2,1,0:T(8,128)S(1)}, f32[16,8,512]{2,1,0:T(8,128)S(1)}, u32[]{:S(2)}, u32[]{:S(2)}) %collective-permute-start.5) | collective-permute-done | bytes 262176 | tf_op jit(solution)/shard_map/ppermute | solution.py:309
  28.5 0.0 slice-done
  28.5 0.0 slice-done.1
  28.5 4.6 %middle.1 = (f32[16,8,512]{2,1,0:T(8,128)S(1)}, f32[16,8,512]{2,1,0:T(8,128)S(1)}, bf16[1280,512]{1,0:T(8,128)(2,1)S(1)}, bf16[1280,512]{1,0:T(8,128)(2,1)S(1)}) custom-call(f32[1280,512]{1,0:T(8,128)S(1)} %near.1.partial, f32[16,8,512]{2,1,0:T(8,128)S(1)} %collective-permute-done.4.corner_a, f32[16,8,512]{2,1,0:T(8,128)S(1)} %collective-permute-done.5.corner_b, ...), custom_call_target="tpu_custom_call" | custom-call | flops 3355443200 | bytes 16777216 | tf_op jit(solution)/shard_map/middle/pallas_call | solution.py:228
  33.1 0.1 collective-permute-start.7
  33.2 1.2 %collective-permute-start.6 = (f32[16,8,512]{2,1,0:T(8,128)S(1)}, f32[16,8,512]{2,1,0:T(8,128)S(1)}, u32[]{:S(2)}, u32[]{:S(2)}) collective-permute-start(f32[16,8,512]{2,1,0:T(8,128)S(1)} %get-tuple-element.39), channel_id=1, source_target_pairs={{0,15},{1,2},{2,1},{3,4},{4,3},{5,6},{6,5},{7,8},{8,7},{9,10},{10,... | collective-permute-start | bytes 786440 | tf_op jit(solution)/shard_map/ppermute | solution.py:309
  34.4 1.2 %spread.5 = (f32[16,8,512]{2,1,0:T(8,128)S(1)}, f32[16,8,512]{2,1,0:T(8,128)S(1)}) custom-call(bf16[1024,1280]{1,0:T(8,128)(2,1)S(1)} %get-tuple-element.25.th, bf16[1024,1280]{1,0:T(8,128)(2,1)S(1)} %get-tuple-element.26.tl, bf16[1280,512]{1,0:T(8,128)(2,1)S(1)} %get-tuple-element.41.bh, bf16[1280,512]{1,0:T(8,128)(2,1)S(1)} %get-tuple-element.42.bl), custom_call_target="tpu_custom_call" | custom-call | flops 1006632960 | bytes 6291456 | tf_op jit(solution)/shard_map/spread/pallas_call | solution.py:260
  35.5 0.1 collective-permute-start.9
  35.6 3.1 %collective-permute-start.8 = (f32[16,8,512]{2,1,0:T(8,128)S(1)}, f32[16,8,512]{2,1,0:T(8,128)S(1)}, u32[]{:S(2)}, u32[]{:S(2)}) collective-permute-start(f32[16,8,512]{2,1,0:T(8,128)S(1)} %get-tuple-element.43), channel_id=1, source_target_pairs={{0,15},{1,2},{2,1},{3,4},{4,3},{5,6},{6,5},{7,8},{8,7},{9,10},{10,... | collective-permute-start | bytes 786440 | tf_op jit(solution)/shard_map/ppermute | solution.py:309
  38.7 1.2 %spread.3 = f32[16,16,512]{2,1,0:T(8,128)S(1)} custom-call(bf16[1024,1280]{1,0:T(8,128)(2,1)S(1)} %get-tuple-element.25.th, bf16[1024,1280]{1,0:T(8,128)(2,1)S(1)} %get-tuple-element.26.tl, bf16[1280,512]{1,0:T(8,128)(2,1)S(1)} %get-tuple-element.41.bh, bf16[1280,512]{1,0:T(8,128)(2,1)S(1)} %get-tuple-element.42.bl), custom_call_target="tpu_custom_call" | custom-call | flops 1006632960 | bytes 6291456 | tf_op jit(solution)/shard_map/spread/pallas_call | solution.py:260
  39.9 0.0 collective-permute-done.7
  39.9 4.2 %collective-permute-done.6 = f32[16,8,512]{2,1,0:T(8,128)S(1)} collective-permute-done((f32[16,8,512]{2,1,0:T(8,128)S(1)}, f32[16,8,512]{2,1,0:T(8,128)S(1)}, u32[]{:S(2)}, u32[]{:S(2)}) %collective-permute-start.6) | collective-permute-done | bytes 262176 | tf_op jit(solution)/shard_map/ppermute | solution.py:309
  44.1 0.1 fusion
  44.2 2.6 %collective-permute-start.11 = (f32[8,16,512]{2,1,0:T(8,128)S(1)}, f32[8,16,512]{2,1,0:T(8,128)S(1)}, u32[]{:S(2)}, u32[]{:S(2)}) collective-permute-start(f32[8,16,512]{2,1,0:T(8,128)S(1)} %get-tuple-element.46), channel_id=1, source_target_pairs={{0,240},{16,0},{32,16},{48,32},{64,48},{80,64},{96,80},{112,96},{1... | collective-permute-start | bytes 786440 | tf_op jit(solution)/shard_map/ppermute | solution.py:299
  46.8 0.0 collective-permute-start.10
  46.9 1.2 %spread.4 = f32[16,16,512]{2,1,0:T(8,128)S(1)} custom-call(bf16[1024,1280]{1,0:T(8,128)(2,1)S(1)} %get-tuple-element.25.th, bf16[1024,1280]{1,0:T(8,128)(2,1)S(1)} %get-tuple-element.26.tl, bf16[1280,512]{1,0:T(8,128)(2,1)S(1)} %get-tuple-element.41.bh, bf16[1280,512]{1,0:T(8,128)(2,1)S(1)} %get-tuple-element.42.bl), custom_call_target="tpu_custom_call" | custom-call | flops 1006632960 | bytes 6291456 | tf_op jit(solution)/shard_map/spread/pallas_call | solution.py:260
  48.0 0.0 collective-permute-done.9
  48.0 0.0 collective-permute-done.8
  48.0 0.1 fusion.1
  48.2 3.2 %collective-permute-done.11 = f32[8,16,512]{2,1,0:T(8,128)S(1)} collective-permute-done((f32[8,16,512]{2,1,0:T(8,128)S(1)}, f32[8,16,512]{2,1,0:T(8,128)S(1)}, u32[]{:S(2)}, u32[]{:S(2)}) %collective-permute-start.11) | collective-permute-done | bytes 262176 | tf_op jit(solution)/shard_map/ppermute | solution.py:299
  51.3 5.8 %collective-permute-done.10 = f32[8,16,512]{2,1,0:T(8,128)S(1)} collective-permute-done((f32[8,16,512]{2,1,0:T(8,128)S(1)}, f32[8,16,512]{2,1,0:T(8,128)S(1)}, u32[]{:S(2)}, u32[]{:S(2)}) %collective-permute-start.10) | collective-permute-done | bytes 262176 | tf_op jit(solution)/shard_map/ppermute | solution.py:299
  57.1 0.9 %maximum_add_fusion = f32[16,16,512]{2,1,0:T(8,128)} fusion(f32[16,16,512]{2,1,0:T(8,128)S(1)} %fusion.1, f32[8,16,512]{2,1,0:T(8,128)S(1)} %collective-permute-done.11, f32[8,16,512]{2,1,0:T(8,128)S(1)} %collective-permute-done.10), kind=kLoop, calls=%fused_computation.4 | loop fusion | flops 262144 | bytes 1572864 | tf_op jit(solution)/shard_map/add | solution.py:353
  (5 shorter events, 0.1 us)
Async XLA Ops:
  0.0 1.0 %copy-start = (f32[16,16,512]{2,1,0:T(8,128)S(1)}, f32[16,16,512]{2,1,0:T(8,128)}, u32[]{:S(2)}) copy-start(f32[16,16,512]{2,1,0:T(8,128)} %own.1) | copy-start | bytes 1572868
  1.0 21.0 %copy-start.1 = (f32[16,16,512]{2,1,0:T(8,128)S(1)}, f32[16,16,512]{2,1,0:T(8,128)}, u32[]{:S(2)}) copy-start(f32[16,16,512]{2,1,0:T(8,128)} %own.1) | copy-start | bytes 1572868
  1.1 17.7 %collective-permute-start = (f32[8,16,512]{2,1,0:T(8,128)S(1)}, f32[8,16,512]{2,1,0:T(8,128)S(1)}, u32[]{:S(2)}, u32[]{:S(2)}) collective-permute-start(f32[8,16,512]{2,1,0:T(8,128)S(1)} %get-tuple-element.27), channel_id=1, source_target_pairs={{0,16},{16,32},{32,48},{48,64},{64,80},{80,96},{96,112},{112,128},... | collective-permute-start | bytes 786440 | tf_op jit(solution)/shard_map/ppermute | solution.py:299
  3.1 15.7 %collective-permute-start.1 = (f32[8,16,512]{2,1,0:T(8,128)S(1)}, f32[8,16,512]{2,1,0:T(8,128)S(1)}, u32[]{:S(2)}, u32[]{:S(2)}) collective-permute-start(f32[8,16,512]{2,1,0:T(8,128)S(1)} %get-tuple-element.28), channel_id=1, source_target_pairs={{0,240},{16,0},{32,16},{48,32},{64,48},{80,64},{96,80},{112,96},{1... | collective-permute-start | bytes 786440 | tf_op jit(solution)/shard_map/ppermute | solution.py:299
  7.1 12.1 %collective-permute-start.2 = (f32[16,8,512]{2,1,0:T(8,128)S(1)}, f32[16,8,512]{2,1,0:T(8,128)S(1)}, u32[]{:S(2)}, u32[]{:S(2)}) collective-permute-start(f32[16,8,512]{2,1,0:T(8,128)S(1)} %get-tuple-element.29), channel_id=1, source_target_pairs={{0,1},{1,0},{2,3},{3,2},{4,5},{5,4},{6,7},{7,6},{8,9},{9,8},{10,11... | collective-permute-start | bytes 786440 | tf_op jit(solution)/shard_map/ppermute | solution.py:304
  7.1 15.0 %collective-permute-start.3 = (f32[16,8,512]{2,1,0:T(8,128)S(1)}, f32[16,8,512]{2,1,0:T(8,128)S(1)}, u32[]{:S(2)}, u32[]{:S(2)}) collective-permute-start(f32[16,8,512]{2,1,0:T(8,128)S(1)} %get-tuple-element.30), channel_id=1, source_target_pairs={{0,15},{1,2},{2,1},{3,4},{4,3},{5,6},{6,5},{7,8},{8,7},{9,10},{10,... | collective-permute-start | bytes 786440 | tf_op jit(solution)/shard_map/ppermute | solution.py:309
  18.9 9.6 %slice-start = ((s8[6553600]{0:T(1024)(128)(4,1)}), s8[4194304]{0:T(1024)(128)(4,1)S(1)}, s32[]{:S(2)}) async-start(s8[6553600]{0:T(1024)(128)(4,1)} %bitcast), calls=%async_computation | async-start | bytes 8388608
  18.9 7.2 %collective-permute-start.4 = (f32[16,8,512]{2,1,0:T(8,128)S(1)}, f32[16,8,512]{2,1,0:T(8,128)S(1)}, u32[]{:S(2)}, u32[]{:S(2)}) collective-permute-start(f32[16,8,512]{2,1,0:T(8,128)S(1)} %get-tuple-element.48), channel_id=1, source_target_pairs={{0,1},{1,0},{2,3},{3,2},{4,5},{5,4},{6,7},{7,6},{8,9},{9,8},{10,11... | collective-permute-start | bytes 786440 | tf_op jit(solution)/shard_map/ppermute | solution.py:304
  19.0 9.5 %collective-permute-start.5 = (f32[16,8,512]{2,1,0:T(8,128)S(1)}, f32[16,8,512]{2,1,0:T(8,128)S(1)}, u32[]{:S(2)}, u32[]{:S(2)}) collective-permute-start(f32[16,8,512]{2,1,0:T(8,128)S(1)} %get-tuple-element.47), channel_id=1, source_target_pairs={{0,15},{1,2},{2,1},{3,4},{4,3},{5,6},{6,5},{7,8},{8,7},{9,10},{10,... | collective-permute-start | bytes 786440 | tf_op jit(solution)/shard_map/ppermute | solution.py:309
  22.0 6.5 %slice-start.1 = ((s8[6553600]{0:T(1024)(128)(4,1)}), s8[2359296]{0:T(1024)(128)(4,1)S(1)}, s32[]{:S(2)}) async-start(s8[6553600]{0:T(1024)(128)(4,1)} %bitcast), calls=%async_computation.1 | async-start | bytes 4718592
  33.1 6.8 %collective-permute-start.7 = (f32[16,8,512]{2,1,0:T(8,128)S(1)}, f32[16,8,512]{2,1,0:T(8,128)S(1)}, u32[]{:S(2)}, u32[]{:S(2)}) collective-permute-start(f32[16,8,512]{2,1,0:T(8,128)S(1)} %get-tuple-element.40), channel_id=1, source_target_pairs={{0,1},{1,0},{2,3},{3,2},{4,5},{5,4},{6,7},{7,6},{8,9},{9,8},{10,11... | collective-permute-start | bytes 786440 | tf_op jit(solution)/shard_map/ppermute | solution.py:304
  33.2 10.9 %collective-permute-start.6 = (f32[16,8,512]{2,1,0:T(8,128)S(1)}, f32[16,8,512]{2,1,0:T(8,128)S(1)}, u32[]{:S(2)}, u32[]{:S(2)}) collective-permute-start(f32[16,8,512]{2,1,0:T(8,128)S(1)} %get-tuple-element.39), channel_id=1, source_target_pairs={{0,15},{1,2},{2,1},{3,4},{4,3},{5,6},{6,5},{7,8},{8,7},{9,10},{10,... | collective-permute-start | bytes 786440 | tf_op jit(solution)/shard_map/ppermute | solution.py:309
  35.5 12.5 %collective-permute-start.9 = (f32[16,8,512]{2,1,0:T(8,128)S(1)}, f32[16,8,512]{2,1,0:T(8,128)S(1)}, u32[]{:S(2)}, u32[]{:S(2)}) collective-permute-start(f32[16,8,512]{2,1,0:T(8,128)S(1)} %get-tuple-element.44), channel_id=1, source_target_pairs={{0,1},{1,0},{2,3},{3,2},{4,5},{5,4},{6,7},{7,6},{8,9},{9,8},{10,11... | collective-permute-start | bytes 786440 | tf_op jit(solution)/shard_map/ppermute | solution.py:304
  35.6 12.4 %collective-permute-start.8 = (f32[16,8,512]{2,1,0:T(8,128)S(1)}, f32[16,8,512]{2,1,0:T(8,128)S(1)}, u32[]{:S(2)}, u32[]{:S(2)}) collective-permute-start(f32[16,8,512]{2,1,0:T(8,128)S(1)} %get-tuple-element.43), channel_id=1, source_target_pairs={{0,15},{1,2},{2,1},{3,4},{4,3},{5,6},{6,5},{7,8},{8,7},{9,10},{10,... | collective-permute-start | bytes 786440 | tf_op jit(solution)/shard_map/ppermute | solution.py:309
  44.2 7.1 %collective-permute-start.11 = (f32[8,16,512]{2,1,0:T(8,128)S(1)}, f32[8,16,512]{2,1,0:T(8,128)S(1)}, u32[]{:S(2)}, u32[]{:S(2)}) collective-permute-start(f32[8,16,512]{2,1,0:T(8,128)S(1)} %get-tuple-element.46), channel_id=1, source_target_pairs={{0,240},{16,0},{32,16},{48,32},{64,48},{80,64},{96,80},{112,96},{1... | collective-permute-start | bytes 786440 | tf_op jit(solution)/shard_map/ppermute | solution.py:299
  46.8 10.3 %collective-permute-start.10 = (f32[8,16,512]{2,1,0:T(8,128)S(1)}, f32[8,16,512]{2,1,0:T(8,128)S(1)}, u32[]{:S(2)}, u32[]{:S(2)}) collective-permute-start(f32[8,16,512]{2,1,0:T(8,128)S(1)} %get-tuple-element.45), channel_id=1, source_target_pairs={{0,16},{16,32},{32,48},{48,64},{64,80},{80,96},{96,112},{112,128},... | collective-permute-start | bytes 786440 | tf_op jit(solution)/shard_map/ppermute | solution.py:299

commit v5 on v4

--- a/solution.py
+++ b/solution.py
@@ -22,27 +22,58 @@
     return 1 - lax.rem(lax.axis_index("gy"), 2)
 
 
-def taps_at(weights, first, density, offsets):
+def taps_at(weights, density, offsets):
     total = jnp.zeros(offsets.shape, jnp.float32)
     for tap in range(TAPS):
-        total = jnp.where(offsets == tap - RADIUS, weights[first + density, tap], total)
+        total = jnp.where(offsets == tap - RADIUS, weights[density, tap], total)
     return total
 
 
-def taps_of_all(weights, first, offsets):
+def taps_of_all(weights, offsets):
     totals = [jnp.zeros(offsets.shape, jnp.float32)] * DENSITIES
     for tap in range(TAPS):
         here = offsets == tap - RADIUS
-        totals = [jnp.where(here, weights[first + a, tap], totals[a]) for a in range(DENSITIES)]
+        totals = [jnp.where(here, weights[a, tap], totals[a]) for a in range(DENSITIES)]
     return totals
 
 
-ROWS, COLS, DEPTH = 0, DENSITIES, 2 * DENSITIES
-
-
-def build_kernel(weights, nh, nl, ch, cl, th, tl, bands, bands_t):
+def build_kernel(
+    kr_hbm, kc_hbm, kd_hbm, nh, nl, ch, cl, th, tl, bands, bands_t, kr, kc, depth_taps, depth_row, sems
+):
+    copies = [
+        pltpu.make_async_copy(kr_hbm, kr, sems.at[0]),
+        pltpu.make_async_copy(kc_hbm, kc, sems.at[1]),
+        pltpu.make_async_copy(kd_hbm, depth_taps, sems.at[2]),
+    ]
+    for copy in copies:
+        copy.start()
+    copies[2].wait()
     right = side_is_right()
     iota = lambda shape, dim: lax.broadcasted_iota(jnp.int32, shape, dim)
+
+    depth_row[...] = jnp.zeros(depth_row.shape, jnp.float32)
+    depth_row[:DENSITIES, :TAPS] = depth_taps[...].astype(jnp.float32)
+    depth = bands.shape[-1]
+    block = (LANES, LANES)
+    ahead = iota(block, 1) - iota(block, 0)
+
+    def band(density, carry):
+        row = jnp.broadcast_to(depth_row[pl.ds(density, 1)], block)
+        ring_t = pltpu.roll(row, LANES - RADIUS, 1, stride=1, stride_axis=0)
+        for ref, ring in ((bands_t, ring_t), (bands, ring_t.T)):
+            ref[density] = jnp.zeros((depth, depth), jnp.bfloat16)
+            for step in (-1, 0, 1):
+                here = jnp.abs(ahead + step * LANES) <= RADIUS
+                part = jnp.where(here, ring, 0.0).astype(jnp.bfloat16)
+                for start in range(0, depth, LANES):
+                    across = start + step * LANES
+                    if 0 <= across < depth:
+                        ref[density, start : start + LANES, across : across + LANES] = part
+        return carry
+
+    lax.fori_loop(0, DENSITIES, band, 0)
+    for copy in copies[:2]:
+        copy.wait()
 
     def put(high_ref, low_ref, start, lanes, values):
         high, low = halves(values)
@@ -60,8 +91,8 @@
             row = jnp.where(group == 0, wide + RADIUS * half, row)
             side = half + right - 2 * half * right
             col = jnp.where(group < 2, lane & 15, (lane & 7) - RADIUS + TURN * side)
-            by_row = taps_of_all(weights, ROWS, row - tile_place)
-            by_col = taps_of_all(weights, COLS, col - tile_place)
+            by_row = taps_of_all(kr, row - tile_place)
+            by_col = taps_of_all(kc, col - tile_place)
             for a in range(DENSITIES):
                 for r in range(TILE):
                     put(high_ref, low_ref, a * CELLS + r * TILE, lanes, by_row[a][r : r + 1] * by_col[a])
@@ -79,8 +110,8 @@
         place, lane = iota(shape, 0), iota(shape, 1)
         turn = TURN * right
         turned = place - RADIUS + jnp.where(place < RADIUS, turn, jnp.where(place < TILE + RADIUS, 0, -turn))
-        by_row = taps_at(weights, ROWS, density, place - RADIUS - (lane >> 4) - RADIUS * half)
-        by_col = taps_at(weights, COLS, density, turned - (lane & 15))
+        by_row = taps_at(kr, density, place - RADIUS - (lane >> 4) - RADIUS * half)
+        by_col = taps_at(kc, density, turned - (lane & 15))
         row = lambda r: by_row[r + RADIUS : r + RADIUS + 1]
         inner = list(range(TILE))
         outer = list(range(-RADIUS, 0)) + list(range(TILE, TILE + RADIUS))
@@ -96,49 +127,29 @@
 
     lax.fori_loop(0, DENSITIES * CELLS // LANES, transposes, 0)
 
-    depth = bands.shape[-1]
-    count = depth // LANES
-
-    def band(density, carry):
-        for ref, sign in ((bands, 1), (bands_t, -1)):
-            ref[density] = jnp.zeros((depth, depth), jnp.bfloat16)
-            for start in range(0, LANES, TILE):
-                shape = (TILE, LANES)
-                offsets = sign * (
-                    start + iota(shape, 0) - iota(shape, 1)
-                )
-                part = taps_at(weights, DEPTH, density, offsets).astype(jnp.bfloat16)
-                for block in range(count):
-                    base = block * LANES
-                    ref[density, base + start : base + start + TILE, base : base + LANES] = part
-                for step, near_edge in ((1, start == 0), (-1, start == LANES - TILE)):
-                    if near_edge:
-                        part = taps_at(weights, DEPTH, density, offsets + sign * step * LANES).astype(jnp.bfloat16)
-                        for block in range(count):
-                            if 0 <= block + step < count:
-                                base, across = (block + step) * LANES, block * LANES
-                                ref[density, base + start : base + start + TILE, across : across + LANES] = part
-        return carry
-
-    lax.fori_loop(0, DENSITIES, band, 0)
-
-
 def build(kernel_rows, kernel_cols, kernel_depth, depth):
     cells = DENSITIES * CELLS
     shapes = [(cells, 3 * CELLS)] * 2 + [(cells, CELLS)] * 2
     shapes += [(4 * CELLS, cells)] * 2
     shapes += [(DENSITIES, depth, depth)] * 2
     vmem = pl.BlockSpec(memory_space=pltpu.VMEM)
-    smem = pl.BlockSpec(memory_space=pltpu.SMEM)
+    hbm = pl.BlockSpec(memory_space=pltpu.HBM)
     return pl.pallas_call(
         build_kernel,
         out_shape=[jax.ShapeDtypeStruct(s, jnp.bfloat16) for s in shapes],
-        in_specs=[smem],
+        in_specs=[hbm] * 3,
         out_specs=[vmem] * len(shapes),
+        scratch_shapes=[
+            pltpu.SMEM(kernel_rows.shape, jnp.float32),
+            pltpu.SMEM(kernel_cols.shape, jnp.float32),
+            pltpu.VMEM(kernel_depth.shape, jnp.bfloat16),
+            pltpu.VMEM((RADIUS, LANES), jnp.float32),
+            pltpu.SemaphoreType.DMA((3,)),
+        ],
         compiler_params=pltpu.CompilerParams(vmem_limit_bytes=24 << 20),
         cost_estimate=pl.CostEstimate(flops=30 << 20, bytes_accessed=16 << 20, transcendentals=0),
         name="build",
-    )(jnp.concatenate([kernel_rows, kernel_cols, kernel_depth.astype(jnp.float32)], 0))
+    )(*[pltpu.with_memory_space_constraint(a, pltpu.HBM) for a in (kernel_rows, kernel_cols, kernel_depth)])
 
 
 def halves(values):
@@ -270,28 +281,36 @@
     )(th, tl, bh, bl)
 
 
-def cut_kernel(tangent, last, first, side_a, side_b):
+def cut_kernel(tangent, *refs):
+    outs, sems = refs[:-1], refs[-1]
     right = side_is_right()
-    cols = lambda place: pl.ds(pl.multiple_of(place * RADIUS, RADIUS), RADIUS)
-    last[...] = tangent[RADIUS:]
-    first[...] = tangent[:RADIUS]
-    side_a[...] = tangent[:, cols(right)]
-    side_b[...] = tangent[:, cols(1 - right)]
+    rows = lambda start: tangent.at[pl.ds(start, RADIUS)]
+    cols = lambda place: tangent.at[:, pl.ds(pl.multiple_of(place * RADIUS, RADIUS), RADIUS)]
+    sources = (rows(RADIUS), rows(0), cols(right), cols(1 - right), tangent)
+    copies = [
+        pltpu.make_async_copy(source, out, sems.at[index])
+        for index, (source, out) in enumerate(zip(sources, outs))
+    ]
+    for copy in copies:
+        copy.start()
+    for copy in copies:
+        copy.wait()
 
 
 def cut(tangent):
     span_rows, span_cols, depth = tangent.shape
-    shapes = [(RADIUS, span_cols)] * 2 + [(span_rows, RADIUS)] * 2
+    shapes = [(RADIUS, span_cols)] * 2 + [(span_rows, RADIUS)] * 2 + [(span_rows, span_cols)]
     vmem = pl.BlockSpec(memory_space=pltpu.VMEM)
     return pl.pallas_call(
         cut_kernel,
         out_shape=[jax.ShapeDtypeStruct(s + (depth,), jnp.float32) for s in shapes],
-        in_specs=[vmem],
-        out_specs=[vmem] * 4,
+        in_specs=[pl.BlockSpec(memory_space=pltpu.HBM)],
+        out_specs=[vmem] * 5,
+        scratch_shapes=[pltpu.SemaphoreType.DMA((5,))],
         compiler_params=pltpu.CompilerParams(vmem_limit_bytes=8 << 20),
         cost_estimate=pl.CostEstimate(flops=0, bytes_accessed=3 << 20, transcendentals=0),
         name="cut",
-    )(tangent)
+    )(pltpu.with_memory_space_constraint(tangent, pltpu.HBM))
 
 
 def shift(cells, axis, step):
@@ -321,7 +340,7 @@
         left, other = jnp.concatenate([from_a, from_b], 1), jnp.concatenate([from_b, from_a], 1)
         return jnp.where(right == 1, other, left)
 
-    last, first, cols_a, cols_b = cut(tangent)
+    last, first, cols_a, cols_b, tile = cut(tangent)
     north = shift(last, "gx", 1)
     south = shift(first, "gx", -1)
     side_b = swap_b(cols_b)
@@ -333,7 +352,7 @@
     corner_b = swap_b(side_cols(sides, 1 - right))
     corner_a = swap_a(side_cols(sides, right))
 
-    partial = near((tangent, north, south, side_a, side_b), nh, nl)
+    partial = near((tile, north, south, side_a, side_b), nh, nl)
     to_a, to_b, bh, bl = middle(partial, corner_a, corner_b, ch, cl, bands, bands_t, th, tl, hessian)
     from_b = swap_b(to_b)
     from_a = swap_a(to_a)
@@ -344,8 +363,10 @@
 
     (around,) = spread(1, th, tl, bh, bl, [(span_rows, span_cols)])
     around = around + joined(from_a, from_b)
-    side_from_s = shift(around[:reach], "gx", -1)
-    side_from_n = shift(around[reach:], "gx", 1)
+    above, below = around[:reach], around[reach:]
+    side_from_n = shift(below, "gx", 1)
+    above, below = lax.optimization_barrier((above, below))
+    side_from_s = shift(above, "gx", -1)
 
     around, bh, bl = lax.optimization_barrier((around, bh, bl))
     (own,) = spread(0, th, tl, bh, bl, [(span_rows, span_cols)])

time: 58.9 us -> 55.1 us (0.935); the launches traced: 58 us -> 55 us
  waiting for transfers between devices: 18.4 us -> 12.7 us
  starting transfers between devices: 17.8 us -> 21.8 us
  other arithmetic: 2.51 us -> 1.12 us
  Pallas kernels: 17.9 us -> 19.1 us
  local copies, waits for them, and re-layouts: 1.14 us -> 0.09 us
    ppermute x4, waiting for transfers between devices: 8.98 us -> 0.47 us  [shift(): lax.ppermute(cells, axis, [(i, (i + step) % count) for i in range(count)])]
    ppermute x4, starting transfers between devices: 8.59 us -> 11.7 us  [shift(): lax.ppermute(cells, axis, [(i, (i + step) % count) for i in range(count)])]
    ppermute x4, waiting for transfers between devices: 9.42 us -> 12.2 us  [swap_b(): lax.ppermute(cells, 'gy', [(j, (j + (1 if j % 2 else -1)) % count) for j...]
    pallas_call x1, Pallas kernels: 0.07 us -> 1.68 us  [cut(): pl.pallas_call(cut_kernel, out_shape=[jax.ShapeDtypeStruct(s + (depth,),...]
    unnamed x9 -> x5, local copies, waits for them, and re-layouts: 1.07 us -> 0.03 us
    ppermute x4, starting transfers between devices: 8.96 us -> 9.85 us  [swap_b(): lax.ppermute(cells, 'gy', [(j, (j + (1 if j % 2 else -1)) % count) for j...]
    concatenate x1 -> x0, other arithmetic: 0.71 us -> none  [build(): jnp.concatenate([kernel_rows, kernel_cols, kernel_depth.astype(jnp.float3...]
    convert_element_type x1 -> x0, other arithmetic: 0.68 us -> none  [build(): kernel_depth.astype(jnp.float32)]
  transfers between devices with their start and end apart: 12 -> 12, of which waited for: 5 -> 5; matrix products, arithmetic and copies ran while one was open for 3% -> 1% of each run, Pallas kernels for 23% -> 23%
where the time goes in v5:
time: 55.1 us; the launch traced here: 55 us
  starting transfers between devices  21.8 us (40%)
  Pallas kernels  19.1 us (35%)
  waiting for transfers between devices  12.7 us (23%)
  other arithmetic  1.12 us (2%)
    ppermute x4, waiting for transfers between devices, swap_b(): lax.ppermute(cells, 'gy', [(j, (j + (1 if j % 2 else -1)) % count) for j...  12.2 us
    ppermute x4, starting transfers between devices, shift(): lax.ppermute(cells, axis, [(i, (i + step) % count) for i in range(count)])  11.7 us
    ppermute x4, starting transfers between devices, swap_b(): lax.ppermute(cells, 'gy', [(j, (j + (1 if j % 2 else -1)) % count) for j...  9.85 us
    pallas_call x1, Pallas kernels, build(): pl.pallas_call(build_kernel, out_shape=[jax.ShapeDtypeStruct(s, jnp.bfloa...  5.3 us
    pallas_call x1, Pallas kernels, middle(): pl.pallas_call(middle_kernel, out_shape=[edge, edge, back, back], in_spec...  4.5 us
    pallas_call x1, Pallas kernels, near(): pl.pallas_call(near_kernel, out_shape=jax.ShapeDtypeStruct((DENSITIES * C...  4.11 us
    pallas_call x3, Pallas kernels, spread(): pl.pallas_call(functools.partial(spread_kernel, group), out_shape=[jax.Sh...  3.5 us
    pallas_call x1, Pallas kernels, cut(): pl.pallas_call(cut_kernel, out_shape=[jax.ShapeDtypeStruct(s + (depth,),...  1.68 us
  transfers between devices with their start and end apart: 12, of which 5 were waited for; matrix products, arithmetic and copies ran while one was open for 1% of the time, Pallas kernels for 23%

profile of v5, /device:TPU:4, one launch (start us, length us, event | category | flops | bytes accessed | tf_op | source)
XLA Modules:
  0.0 55.0 jit_solution(2963279678137392066)
XLA Ops:
  0.0 1.7 %cut.1 = (f32[8,16,512]{2,1,0:T(8,128)S(1)}, f32[8,16,512]{2,1,0:T(8,128)S(1)}, f32[16,8,512]{2,1,0:T(8,128)S(1)}, f32[16,8,512]{2,1,0:T(8,128)S(1)}, f32[16,16,512]{2,1,0:T(8,128)S(1)}) custom-call(f32[16,16,512]{2,1,0:T(8,128)} %tangent.1), custom_call_target="tpu_custom_call" | custom-call | bytes 3145728 | tf_op jit(solution)/shard_map/cut/pallas_call | solution.py:304
  1.7 2.0 %collective-permute-start = (f32[8,16,512]{2,1,0:T(8,128)S(1)}, f32[8,16,512]{2,1,0:T(8,128)S(1)}, u32[]{:S(2)}, u32[]{:S(2)}) collective-permute-start(f32[8,16,512]{2,1,0:T(8,128)S(1)} %get-tuple-element.30), channel_id=1, source_target_pairs={{0,16},{16,32},{32,48},{48,64},{64,80},{80,96},{96,112},{112,128},... | collective-permute-start | bytes 786440 | tf_op jit(solution)/shard_map/ppermute | solution.py:318
  3.7 4.0 %collective-permute-start.1 = (f32[8,16,512]{2,1,0:T(8,128)S(1)}, f32[8,16,512]{2,1,0:T(8,128)S(1)}, u32[]{:S(2)}, u32[]{:S(2)}) collective-permute-start(f32[8,16,512]{2,1,0:T(8,128)S(1)} %get-tuple-element.31), channel_id=1, source_target_pairs={{0,240},{16,0},{32,16},{48,32},{64,48},{80,64},{96,80},{112,96},{1... | collective-permute-start | bytes 786440 | tf_op jit(solution)/shard_map/ppermute | solution.py:318
  7.7 0.0 collective-permute-start.2
  7.7 4.7 %collective-permute-start.3 = (f32[16,8,512]{2,1,0:T(8,128)S(1)}, f32[16,8,512]{2,1,0:T(8,128)S(1)}, u32[]{:S(2)}, u32[]{:S(2)}) collective-permute-start(f32[16,8,512]{2,1,0:T(8,128)S(1)} %get-tuple-element.33), channel_id=1, source_target_pairs={{0,15},{1,2},{2,1},{3,4},{4,3},{5,6},{6,5},{7,8},{8,7},{9,10},{10,... | collective-permute-start | bytes 786440 | tf_op jit(solution)/shard_map/ppermute | solution.py:328
  12.3 5.3 %build.1 = (bf16[1280,768]{1,0:T(8,128)(2,1)S(1)}, bf16[1280,768]{1,0:T(8,128)(2,1)S(1)}, bf16[1280,256]{1,0:T(8,128)(2,1)S(1)}, bf16[1280,256]{1,0:T(8,128)(2,1...) custom-call(f32[5,17]{1,0:T(8,128)} %kr_hbm.1, ...), custom_call_target="tpu_custom_call" | custom-call | flops 31457280 | bytes 16777216 | tf_op jit(solution)/shard_map/build/pallas_call | solution.py:137
  17.6 0.0 collective-permute-done.north
  17.7 0.0 collective-permute-done.1.south
  17.7 0.0 slice-start
  17.8 0.1 collective-permute-start.4
  17.9 1.0 %collective-permute-start.5 = (f32[16,8,512]{2,1,0:T(8,128)S(1)}, f32[16,8,512]{2,1,0:T(8,128)S(1)}, u32[]{:S(2)}, u32[]{:S(2)}) collective-permute-start(f32[16,8,512]{2,1,0:T(8,128)S(1)} %get-tuple-element.51), channel_id=1, source_target_pairs={{0,15},{1,2},{2,1},{3,4},{4,3},{5,6},{6,5},{7,8},{8,7},{9,10},{10,... | collective-permute-start | bytes 786440 | tf_op jit(solution)/shard_map/ppermute | solution.py:328
  18.8 0.0 collective-permute-done.2.side_a
  18.8 3.8 %collective-permute-done.3.side_b = f32[16,8,512]{2,1,0:T(8,128)S(1)} collective-permute-done((f32[16,8,512]{2,1,0:T(8,128)S(1)}, f32[16,8,512]{2,1,0:T(8,128)S(1)}, u32[]{:S(2)}, u32[]{:S(2)}) %collective-permute-start.3) | collective-permute-done | bytes 262176 | tf_op jit(solution)/shard_map/ppermute | solution.py:328
  22.6 0.0 slice-start.1
  22.6 4.1 %near.1.partial = f32[1280,512]{1,0:T(8,128)S(1)} custom-call(f32[16,16,512]{2,1,0:T(8,128)S(1)} %get-tuple-element.29.own, f32[8,16,512]{2,1,0:T(8,128)S(1)} %collective-permute-done.north, f32[8,16,512]{2,1,0:T(8,128)S(1)} %collective-permute-done.1.south, f32[16,8,512]{2,1,0:T(8,128)S(1)} %collective-permute-done.2.side_a, ...), custom_call_target="tpu_custom_call" | custom-call | flops 3019898880 | bytes 10485760 | tf_op jit(solution)/shard_map/near/pallas_call | solution.py:188
  26.7 0.0 collective-permute-done.4.corner_a
  26.7 1.5 %collective-permute-done.5.corner_b = f32[16,8,512]{2,1,0:T(8,128)S(1)} collective-permute-done((f32[16,8,512]{2,1,0:T(8,128)S(1)}, f32[16,8,512]{2,1,0:T(8,128)S(1)}, u32[]{:S(2)}, u32[]{:S(2)}) %collective-permute-start.5) | collective-permute-done | bytes 262176 | tf_op jit(solution)/shard_map/ppermute | solution.py:328
  28.2 0.0 slice-done
  28.2 0.0 slice-done.1
  28.2 4.5 %middle.1 = (f32[16,8,512]{2,1,0:T(8,128)S(1)}, f32[16,8,512]{2,1,0:T(8,128)S(1)}, bf16[1280,512]{1,0:T(8,128)(2,1)S(1)}, bf16[1280,512]{1,0:T(8,128)(2,1)S(1)}) custom-call(f32[1280,512]{1,0:T(8,128)S(1)} %near.1.partial, f32[16,8,512]{2,1,0:T(8,128)S(1)} %collective-permute-done.4.corner_a, f32[16,8,512]{2,1,0:T(8,128)S(1)} %collective-permute-done.5.corner_b, ...), custom_call_target="tpu_custom_call" | custom-call | flops 3355443200 | bytes 16777216 | tf_op jit(solution)/shard_map/middle/pallas_call | solution.py:239
  32.8 0.1 collective-permute-start.7
  32.9 0.9 %collective-permute-start.6 = (f32[16,8,512]{2,1,0:T(8,128)S(1)}, f32[16,8,512]{2,1,0:T(8,128)S(1)}, u32[]{:S(2)}, u32[]{:S(2)}) collective-permute-start(f32[16,8,512]{2,1,0:T(8,128)S(1)} %get-tuple-element.42), channel_id=1, source_target_pairs={{0,15},{1,2},{2,1},{3,4},{4,3},{5,6},{6,5},{7,8},{8,7},{9,10},{10,... | collective-permute-start | bytes 786440 | tf_op jit(solution)/shard_map/ppermute | solution.py:328
  33.7 1.2 %spread.5 = (f32[16,8,512]{2,1,0:T(8,128)S(1)}, f32[16,8,512]{2,1,0:T(8,128)S(1)}) custom-call(bf16[1024,1280]{1,0:T(8,128)(2,1)S(1)} %get-tuple-element.27.th, bf16[1024,1280]{1,0:T(8,128)(2,1)S(1)} %get-tuple-element.28.tl, bf16[1280,512]{1,0:T(8,128)(2,1)S(1)} %get-tuple-element.44.bh, bf16[1280,512]{1,0:T(8,128)(2,1)S(1)} %get-tuple-element.45.bl), custom_call_target="tpu_custom_call" | custom-call | flops 1006632960 | bytes 6291456 | tf_op jit(solution)/shard_map/spread/pallas_call | solution.py:271
  34.9 0.1 collective-permute-start.9
  35.0 3.4 %collective-permute-start.8 = (f32[16,8,512]{2,1,0:T(8,128)S(1)}, f32[16,8,512]{2,1,0:T(8,128)S(1)}, u32[]{:S(2)}, u32[]{:S(2)}) collective-permute-start(f32[16,8,512]{2,1,0:T(8,128)S(1)} %get-tuple-element.46), channel_id=1, source_target_pairs={{0,15},{1,2},{2,1},{3,4},{4,3},{5,6},{6,5},{7,8},{8,7},{9,10},{10,... | collective-permute-start | bytes 786440 | tf_op jit(solution)/shard_map/ppermute | solution.py:328
  38.3 1.2 %spread.3 = f32[16,16,512]{2,1,0:T(8,128)S(1)} custom-call(bf16[1024,1280]{1,0:T(8,128)(2,1)S(1)} %get-tuple-element.27.th, bf16[1024,1280]{1,0:T(8,128)(2,1)S(1)} %get-tuple-element.28.tl, bf16[1280,512]{1,0:T(8,128)(2,1)S(1)} %get-tuple-element.44.bh, bf16[1280,512]{1,0:T(8,128)(2,1)S(1)} %get-tuple-element.45.bl), custom_call_target="tpu_custom_call" | custom-call | flops 1006632960 | bytes 6291456 | tf_op jit(solution)/shard_map/spread/pallas_call | solution.py:271
  39.5 0.0 collective-permute-done.7
  39.5 4.2 %collective-permute-done.6 = f32[16,8,512]{2,1,0:T(8,128)S(1)} collective-permute-done((f32[16,8,512]{2,1,0:T(8,128)S(1)}, f32[16,8,512]{2,1,0:T(8,128)S(1)}, u32[]{:S(2)}, u32[]{:S(2)}) %collective-permute-start.6) | collective-permute-done | bytes 262176 | tf_op jit(solution)/shard_map/ppermute | solution.py:328
  43.7 0.1 fusion
  43.9 0.1 collective-permute-start.10
  43.9 5.6 %collective-permute-start.11 = (f32[8,16,512]{2,1,0:T(8,128)S(1)}, f32[8,16,512]{2,1,0:T(8,128)S(1)}, u32[]{:S(2)}, u32[]{:S(2)}) collective-permute-start(f32[8,16,512]{2,1,0:T(8,128)S(1)} %get-tuple-element.48), channel_id=1, source_target_pairs={{0,240},{16,0},{32,16},{48,32},{64,48},{80,64},{96,80},{112,96},{1... | collective-permute-start | bytes 786440 | tf_op jit(solution)/shard_map/ppermute | solution.py:318
  49.6 1.2 %spread.4 = f32[16,16,512]{2,1,0:T(8,128)S(1)} custom-call(bf16[1024,1280]{1,0:T(8,128)(2,1)S(1)} %get-tuple-element.27.th, bf16[1024,1280]{1,0:T(8,128)(2,1)S(1)} %get-tuple-element.28.tl, bf16[1280,512]{1,0:T(8,128)(2,1)S(1)} %get-tuple-element.44.bh, bf16[1280,512]{1,0:T(8,128)(2,1)S(1)} %get-tuple-element.45.bl), custom_call_target="tpu_custom_call" | custom-call | flops 1006632960 | bytes 6291456 | tf_op jit(solution)/shard_map/spread/pallas_call | solution.py:271
  50.8 0.0 collective-permute-done.9
  50.8 2.8 %collective-permute-done.8 = f32[16,8,512]{2,1,0:T(8,128)S(1)} collective-permute-done((f32[16,8,512]{2,1,0:T(8,128)S(1)}, f32[16,8,512]{2,1,0:T(8,128)S(1)}, u32[]{:S(2)}, u32[]{:S(2)}) %collective-permute-start.8) | collective-permute-done | bytes 262176 | tf_op jit(solution)/shard_map/ppermute | solution.py:328
  53.5 0.1 fusion.1
  53.6 0.0 collective-permute-done.11
  53.6 0.5 collective-permute-done.10
  54.1 0.9 %maximum_add_fusion = f32[16,16,512]{2,1,0:T(8,128)} fusion(f32[16,16,512]{2,1,0:T(8,128)S(1)} %fusion.1, f32[8,16,512]{2,1,0:T(8,128)S(1)} %collective-permute-done.11, f32[8,16,512]{2,1,0:T(8,128)S(1)} %collective-permute-done.10), kind=kLoop, calls=%fused_computation.4 | loop fusion | flops 262144 | bytes 1572864 | tf_op jit(solution)/shard_map/add | solution.py:374
  (5 shorter events, 0.1 us)
Async XLA Ops:
  1.7 15.9 %collective-permute-start = (f32[8,16,512]{2,1,0:T(8,128)S(1)}, f32[8,16,512]{2,1,0:T(8,128)S(1)}, u32[]{:S(2)}, u32[]{:S(2)}) collective-permute-start(f32[8,16,512]{2,1,0:T(8,128)S(1)} %get-tuple-element.30), channel_id=1, source_target_pairs={{0,16},{16,32},{32,48},{48,64},{64,80},{80,96},{96,112},{112,128},... | collective-permute-start | bytes 786440 | tf_op jit(solution)/shard_map/ppermute | solution.py:318
  3.7 14.0 %collective-permute-start.1 = (f32[8,16,512]{2,1,0:T(8,128)S(1)}, f32[8,16,512]{2,1,0:T(8,128)S(1)}, u32[]{:S(2)}, u32[]{:S(2)}) collective-permute-start(f32[8,16,512]{2,1,0:T(8,128)S(1)} %get-tuple-element.31), channel_id=1, source_target_pairs={{0,240},{16,0},{32,16},{48,32},{64,48},{80,64},{96,80},{112,96},{1... | collective-permute-start | bytes 786440 | tf_op jit(solution)/shard_map/ppermute | solution.py:318
  7.7 11.2 %collective-permute-start.2 = (f32[16,8,512]{2,1,0:T(8,128)S(1)}, f32[16,8,512]{2,1,0:T(8,128)S(1)}, u32[]{:S(2)}, u32[]{:S(2)}) collective-permute-start(f32[16,8,512]{2,1,0:T(8,128)S(1)} %get-tuple-element.32), channel_id=1, source_target_pairs={{0,1},{1,0},{2,3},{3,2},{4,5},{5,4},{6,7},{7,6},{8,9},{9,8},{10,11... | collective-permute-start | bytes 786440 | tf_op jit(solution)/shard_map/ppermute | solution.py:323
  7.7 15.0 %collective-permute-start.3 = (f32[16,8,512]{2,1,0:T(8,128)S(1)}, f32[16,8,512]{2,1,0:T(8,128)S(1)}, u32[]{:S(2)}, u32[]{:S(2)}) collective-permute-start(f32[16,8,512]{2,1,0:T(8,128)S(1)} %get-tuple-element.33), channel_id=1, source_target_pairs={{0,15},{1,2},{2,1},{3,4},{4,3},{5,6},{6,5},{7,8},{8,7},{9,10},{10,... | collective-permute-start | bytes 786440 | tf_op jit(solution)/shard_map/ppermute | solution.py:328
  17.7 10.6 %slice-start = ((s8[6553600]{0:T(1024)(128)(4,1)}), s8[4194304]{0:T(1024)(128)(4,1)S(1)}, s32[]{:S(2)}) async-start(s8[6553600]{0:T(1024)(128)(4,1)} %bitcast), calls=%async_computation | async-start | bytes 8388608
  17.8 9.0 %collective-permute-start.4 = (f32[16,8,512]{2,1,0:T(8,128)S(1)}, f32[16,8,512]{2,1,0:T(8,128)S(1)}, u32[]{:S(2)}, u32[]{:S(2)}) collective-permute-start(f32[16,8,512]{2,1,0:T(8,128)S(1)} %get-tuple-element.52), channel_id=1, source_target_pairs={{0,1},{1,0},{2,3},{3,2},{4,5},{5,4},{6,7},{7,6},{8,9},{9,8},{10,11... | collective-permute-start | bytes 786440 | tf_op jit(solution)/shard_map/ppermute | solution.py:323
  17.9 10.4 %collective-permute-start.5 = (f32[16,8,512]{2,1,0:T(8,128)S(1)}, f32[16,8,512]{2,1,0:T(8,128)S(1)}, u32[]{:S(2)}, u32[]{:S(2)}) collective-permute-start(f32[16,8,512]{2,1,0:T(8,128)S(1)} %get-tuple-element.51), channel_id=1, source_target_pairs={{0,15},{1,2},{2,1},{3,4},{4,3},{5,6},{6,5},{7,8},{8,7},{9,10},{10,... | collective-permute-start | bytes 786440 | tf_op jit(solution)/shard_map/ppermute | solution.py:328
  22.6 5.6 %slice-start.1 = ((s8[6553600]{0:T(1024)(128)(4,1)}), s8[2359296]{0:T(1024)(128)(4,1)S(1)}, s32[]{:S(2)}) async-start(s8[6553600]{0:T(1024)(128)(4,1)} %bitcast), calls=%async_computation.1 | async-start | bytes 4718592
  32.8 6.8 %collective-permute-start.7 = (f32[16,8,512]{2,1,0:T(8,128)S(1)}, f32[16,8,512]{2,1,0:T(8,128)S(1)}, u32[]{:S(2)}, u32[]{:S(2)}) collective-permute-start(f32[16,8,512]{2,1,0:T(8,128)S(1)} %get-tuple-element.43), channel_id=1, source_target_pairs={{0,1},{1,0},{2,3},{3,2},{4,5},{5,4},{6,7},{7,6},{8,9},{9,8},{10,11... | collective-permute-start | bytes 786440 | tf_op jit(solution)/shard_map/ppermute | solution.py:323
  32.9 10.9 %collective-permute-start.6 = (f32[16,8,512]{2,1,0:T(8,128)S(1)}, f32[16,8,512]{2,1,0:T(8,128)S(1)}, u32[]{:S(2)}, u32[]{:S(2)}) collective-permute-start(f32[16,8,512]{2,1,0:T(8,128)S(1)} %get-tuple-element.42), channel_id=1, source_target_pairs={{0,15},{1,2},{2,1},{3,4},{4,3},{5,6},{6,5},{7,8},{8,7},{9,10},{10,... | collective-permute-start | bytes 786440 | tf_op jit(solution)/shard_map/ppermute | solution.py:328
  34.9 15.9 %collective-permute-start.9 = (f32[16,8,512]{2,1,0:T(8,128)S(1)}, f32[16,8,512]{2,1,0:T(8,128)S(1)}, u32[]{:S(2)}, u32[]{:S(2)}) collective-permute-start(f32[16,8,512]{2,1,0:T(8,128)S(1)} %get-tuple-element.47), channel_id=1, source_target_pairs={{0,1},{1,0},{2,3},{3,2},{4,5},{5,4},{6,7},{7,6},{8,9},{9,8},{10,11... | collective-permute-start | bytes 786440 | tf_op jit(solution)/shard_map/ppermute | solution.py:323
  35.0 18.6 %collective-permute-start.8 = (f32[16,8,512]{2,1,0:T(8,128)S(1)}, f32[16,8,512]{2,1,0:T(8,128)S(1)}, u32[]{:S(2)}, u32[]{:S(2)}) collective-permute-start(f32[16,8,512]{2,1,0:T(8,128)S(1)} %get-tuple-element.46), channel_id=1, source_target_pairs={{0,15},{1,2},{2,1},{3,4},{4,3},{5,6},{6,5},{7,8},{8,7},{9,10},{10,... | collective-permute-start | bytes 786440 | tf_op jit(solution)/shard_map/ppermute | solution.py:328
  43.9 10.3 %collective-permute-start.10 = (f32[8,16,512]{2,1,0:T(8,128)S(1)}, f32[8,16,512]{2,1,0:T(8,128)S(1)}, u32[]{:S(2)}, u32[]{:S(2)}) collective-permute-start(f32[8,16,512]{2,1,0:T(8,128)S(1)} %get-tuple-element.49), channel_id=1, source_target_pairs={{0,16},{16,32},{32,48},{48,64},{64,80},{80,96},{96,112},{112,128},... | collective-permute-start | bytes 786440 | tf_op jit(solution)/shard_map/ppermute | solution.py:318
  43.9 9.7 %collective-permute-start.11 = (f32[8,16,512]{2,1,0:T(8,128)S(1)}, f32[8,16,512]{2,1,0:T(8,128)S(1)}, u32[]{:S(2)}, u32[]{:S(2)}) collective-permute-start(f32[8,16,512]{2,1,0:T(8,128)S(1)} %get-tuple-element.48), channel_id=1, source_target_pairs={{0,240},{16,0},{32,16},{48,32},{64,48},{80,64},{96,80},{112,96},{1... | collective-permute-start | bytes 786440 | tf_op jit(solution)/shard_map/ppermute | solution.py:318

commit v6 on v5

--- a/solution.py
+++ b/solution.py
@@ -281,20 +281,25 @@
     )(th, tl, bh, bl)
 
 
-def cut_kernel(tangent, *refs):
-    outs, sems = refs[:-1], refs[-1]
+PIECES = 8
+
+
+def cut_kernel(tangent, last, first, side_a, side_b, tile, sems):
     right = side_is_right()
-    rows = lambda start: tangent.at[pl.ds(start, RADIUS)]
-    cols = lambda place: tangent.at[:, pl.ds(pl.multiple_of(place * RADIUS, RADIUS), RADIUS)]
-    sources = (rows(RADIUS), rows(0), cols(right), cols(1 - right), tangent)
+    step = TILE // PIECES
     copies = [
-        pltpu.make_async_copy(source, out, sems.at[index])
-        for index, (source, out) in enumerate(zip(sources, outs))
+        pltpu.make_async_copy(tangent.at[pl.ds(step * i, step)], tile.at[pl.ds(step * i, step)], sems.at[i])
+        for i in range(PIECES)
     ]
     for copy in copies:
         copy.start()
     for copy in copies:
         copy.wait()
+    cols = lambda place: pl.ds(pl.multiple_of(place * RADIUS, RADIUS), RADIUS)
+    last[...] = tile[RADIUS:]
+    first[...] = tile[:RADIUS]
+    side_a[...] = tile[:, cols(right)]
+    side_b[...] = tile[:, cols(1 - right)]
 
 
 def cut(tangent):
@@ -306,7 +311,7 @@
         out_shape=[jax.ShapeDtypeStruct(s + (depth,), jnp.float32) for s in shapes],
         in_specs=[pl.BlockSpec(memory_space=pltpu.HBM)],
         out_specs=[vmem] * 5,
-        scratch_shapes=[pltpu.SemaphoreType.DMA((5,))],
+        scratch_shapes=[pltpu.SemaphoreType.DMA((PIECES,))],
         compiler_params=pltpu.CompilerParams(vmem_limit_bytes=8 << 20),
         cost_estimate=pl.CostEstimate(flops=0, bytes_accessed=3 << 20, transcendentals=0),
         name="cut",
@@ -328,6 +333,12 @@
     return lax.ppermute(cells, "gy", [(j, (j + (1 if j % 2 else -1)) % count) for j in range(count)])
 
 
+def swapped(for_b, for_a):
+    from_b = swap_b(for_b)
+    for_b, for_a = lax.optimization_barrier((for_b, for_a))
+    return from_b, swap_a(for_a)
+
+
 def per_device(tangent, hessian, kernel_rows, kernel_cols, kernel_depth):
     span_rows, span_cols, depth = tangent.shape
     reach = RADIUS
@@ -343,23 +354,19 @@
     last, first, cols_a, cols_b, tile = cut(tangent)
     north = shift(last, "gx", 1)
     south = shift(first, "gx", -1)
-    side_b = swap_b(cols_b)
-    side_a = swap_a(cols_a)
+    side_b, side_a = swapped(cols_b, cols_a)
 
     nh, nl, ch, cl, th, tl, bands, bands_t = build(kernel_rows, kernel_cols, kernel_depth, depth)
 
     sides = jnp.concatenate([north, south], 0)
-    corner_b = swap_b(side_cols(sides, 1 - right))
-    corner_a = swap_a(side_cols(sides, right))
+    corner_b, corner_a = swapped(side_cols(sides, 1 - right), side_cols(sides, right))
 
     partial = near((tile, north, south, side_a, side_b), nh, nl)
     to_a, to_b, bh, bl = middle(partial, corner_a, corner_b, ch, cl, bands, bands_t, th, tl, hessian)
-    from_b = swap_b(to_b)
-    from_a = swap_a(to_a)
+    from_b, from_a = swapped(to_b, to_a)
 
     edge_a, edge_b = spread(2, th, tl, bh, bl, [(span_rows, reach)] * 2)
-    edge_from_b = swap_b(edge_b)
-    edge_from_a = swap_a(edge_a)
+    edge_from_b, edge_from_a = swapped(edge_b, edge_a)
 
     (around,) = spread(1, th, tl, bh, bl, [(span_rows, span_cols)])
     around = around + joined(from_a, from_b)

time: 55.1 us -> 54.8 us (level)
  waiting for transfers between devices: 12.7 us -> 14.1 us
  starting transfers between devices: 21.8 us -> 20.6 us
    ppermute x4, waiting for transfers between devices: 12.2 us -> 13.5 us  [swap_b(): lax.ppermute(cells, 'gy', [(j, (j + (1 if j % 2 else -1)) % count) for j...]
    ppermute x4, starting transfers between devices: 9.85 us -> 8.78 us  [swap_b(): lax.ppermute(cells, 'gy', [(j, (j + (1 if j % 2 else -1)) % count) for j...]
  transfers between devices with their start and end apart: 12 -> 12, of which waited for: 5 -> 5; matrix products, arithmetic and copies ran while one was open for 1% -> 1% of each run, Pallas kernels for 23% -> 24%
where the time goes in v6:
time: 54.8 us; the launch traced here: 54.7 us
  starting transfers between devices  20.6 us (38%)
  Pallas kernels  18.6 us (34%)
  waiting for transfers between devices  14.1 us (26%)
  other arithmetic  1.12 us (2%)
    ppermute x4, waiting for transfers between devices, swap_b(): lax.ppermute(cells, 'gy', [(j, (j + (1 if j % 2 else -1)) % count) for j...  13.5 us
    ppermute x4, starting transfers between devices, shift(): lax.ppermute(cells, axis, [(i, (i + step) % count) for i in range(count)])  11.7 us
    ppermute x4, starting transfers between devices, swap_b(): lax.ppermute(cells, 'gy', [(j, (j + (1 if j % 2 else -1)) % count) for j...  8.78 us
    pallas_call x1, Pallas kernels, build(): pl.pallas_call(build_kernel, out_shape=[jax.ShapeDtypeStruct(s, jnp.bfloa...  5.3 us
    pallas_call x1, Pallas kernels, middle(): pl.pallas_call(middle_kernel, out_shape=[edge, edge, back, back], in_spec...  4.49 us
    pallas_call x1, Pallas kernels, near(): pl.pallas_call(near_kernel, out_shape=jax.ShapeDtypeStruct((DENSITIES * C...  4.11 us
    pallas_call x3, Pallas kernels, spread(): pl.pallas_call(functools.partial(spread_kernel, group), out_shape=[jax.Sh...  3.5 us
    pallas_call x1, Pallas kernels, cut(): pl.pallas_call(cut_kernel, out_shape=[jax.ShapeDtypeStruct(s + (depth,),...  1.19 us
  transfers between devices with their start and end apart: 12, of which 5 were waited for; matrix products, arithmetic and copies ran while one was open for 1% of the time, Pallas kernels for 24%

profile of v6, /device:TPU:4, one launch (start us, length us, event | category | flops | bytes accessed | tf_op | source)
XLA Modules:
  0.0 54.7 jit_solution(2179316730322564061)
XLA Ops:
  0.0 1.2 %cut.1 = (f32[8,16,512]{2,1,0:T(8,128)S(1)}, f32[8,16,512]{2,1,0:T(8,128)S(1)}, f32[16,8,512]{2,1,0:T(8,128)S(1)}, f32[16,8,512]{2,1,0:T(8,128)S(1)}, f32[16,16,512]{2,1,0:T(8,128)S(1)}) custom-call(f32[16,16,512]{2,1,0:T(8,128)} %tangent.1), custom_call_target="tpu_custom_call" | custom-call | bytes 3145728 | tf_op jit(solution)/shard_map/cut/pallas_call | solution.py:309
  1.2 2.0 %collective-permute-start = (f32[8,16,512]{2,1,0:T(8,128)S(1)}, f32[8,16,512]{2,1,0:T(8,128)S(1)}, u32[]{:S(2)}, u32[]{:S(2)}) collective-permute-start(f32[8,16,512]{2,1,0:T(8,128)S(1)} %get-tuple-element.34), channel_id=1, source_target_pairs={{0,16},{16,32},{32,48},{48,64},{64,80},{80,96},{96,112},{112,128},... | collective-permute-start | bytes 786440 | tf_op jit(solution)/shard_map/ppermute | solution.py:323
  3.2 4.0 %collective-permute-start.1 = (f32[8,16,512]{2,1,0:T(8,128)S(1)}, f32[8,16,512]{2,1,0:T(8,128)S(1)}, u32[]{:S(2)}, u32[]{:S(2)}) collective-permute-start(f32[8,16,512]{2,1,0:T(8,128)S(1)} %get-tuple-element.35), channel_id=1, source_target_pairs={{0,240},{16,0},{32,16},{48,32},{64,48},{80,64},{96,80},{112,96},{1... | collective-permute-start | bytes 786440 | tf_op jit(solution)/shard_map/ppermute | solution.py:323
  7.2 3.7 %collective-permute-start.3 = (f32[16,8,512]{2,1,0:T(8,128)S(1)}, f32[16,8,512]{2,1,0:T(8,128)S(1)}, u32[]{:S(2)}, u32[]{:S(2)}) collective-permute-start(f32[16,8,512]{2,1,0:T(8,128)S(1)} %get-tuple-element.36), channel_id=1, source_target_pairs={{0,15},{1,2},{2,1},{3,4},{4,3},{5,6},{6,5},{7,8},{8,7},{9,10},{10,... | collective-permute-start | bytes 786440 | tf_op jit(solution)/shard_map/ppermute | solution.py:333
  10.9 0.0 collective-permute-start.2
  10.9 5.3 %build.1 = (bf16[1280,768]{1,0:T(8,128)(2,1)S(1)}, bf16[1280,768]{1,0:T(8,128)(2,1)S(1)}, bf16[1280,256]{1,0:T(8,128)(2,1)S(1)}, bf16[1280,256]{1,0:T(8,128)(2,1...) custom-call(f32[5,17]{1,0:T(8,128)} %kr_hbm.1, ...), custom_call_target="tpu_custom_call" | custom-call | flops 31457280 | bytes 16777216 | tf_op jit(solution)/shard_map/build/pallas_call | solution.py:137
  16.2 0.0 collective-permute-done.north
  16.2 0.0 collective-permute-done.1.south
  16.3 0.0 slice-start
  16.3 1.0 %collective-permute-start.5 = (f32[16,8,512]{2,1,0:T(8,128)S(1)}, f32[16,8,512]{2,1,0:T(8,128)S(1)}, u32[]{:S(2)}, u32[]{:S(2)}) collective-permute-start(f32[16,8,512]{2,1,0:T(8,128)S(1)} %get-tuple-element.60), channel_id=1, source_target_pairs={{0,15},{1,2},{2,1},{3,4},{4,3},{5,6},{6,5},{7,8},{8,7},{9,10},{10,... | collective-permute-start | bytes 786440 | tf_op jit(solution)/shard_map/ppermute | solution.py:333
  17.4 0.0 collective-permute-start.4
  17.4 0.0 collective-permute-done.2.side_a
  17.4 4.7 %collective-permute-done.3.side_b = f32[16,8,512]{2,1,0:T(8,128)S(1)} collective-permute-done((f32[16,8,512]{2,1,0:T(8,128)S(1)}, f32[16,8,512]{2,1,0:T(8,128)S(1)}, u32[]{:S(2)}, u32[]{:S(2)}) %collective-permute-start.3) | collective-permute-done | bytes 262176 | tf_op jit(solution)/shard_map/ppermute | solution.py:333
  22.0 0.0 slice-start.1
  22.0 4.1 %near.1.partial = f32[1280,512]{1,0:T(8,128)S(1)} custom-call(f32[16,16,512]{2,1,0:T(8,128)S(1)} %get-tuple-element.33.own, f32[8,16,512]{2,1,0:T(8,128)S(1)} %collective-permute-done.north, f32[8,16,512]{2,1,0:T(8,128)S(1)} %collective-permute-done.1.south, f32[16,8,512]{2,1,0:T(8,128)S(1)} %collective-permute-done.2.side_a, ...), custom_call_target="tpu_custom_call" | custom-call | flops 3019898880 | bytes 10485760 | tf_op jit(solution)/shard_map/near/pallas_call | solution.py:188
  26.2 0.0 collective-permute-done.4.corner_a
  26.2 1.5 %collective-permute-done.5.corner_b = f32[16,8,512]{2,1,0:T(8,128)S(1)} collective-permute-done((f32[16,8,512]{2,1,0:T(8,128)S(1)}, f32[16,8,512]{2,1,0:T(8,128)S(1)}, u32[]{:S(2)}, u32[]{:S(2)}) %collective-permute-start.5) | collective-permute-done | bytes 262176 | tf_op jit(solution)/shard_map/ppermute | solution.py:333
  27.7 0.0 slice-done
  27.7 0.0 slice-done.1
  27.7 4.5 %middle.1 = (f32[16,8,512]{2,1,0:T(8,128)S(1)}, f32[16,8,512]{2,1,0:T(8,128)S(1)}, bf16[1280,512]{1,0:T(8,128)(2,1)S(1)}, bf16[1280,512]{1,0:T(8,128)(2,1)S(1)}) custom-call(f32[1280,512]{1,0:T(8,128)S(1)} %near.1.partial, f32[16,8,512]{2,1,0:T(8,128)S(1)} %collective-permute-done.4.corner_a, f32[16,8,512]{2,1,0:T(8,128)S(1)} %collective-permute-done.5.corner_b, ...), custom_call_target="tpu_custom_call" | custom-call | flops 3355443200 | bytes 16777216 | tf_op jit(solution)/shard_map/middle/pallas_call | solution.py:239
  32.2 0.1 collective-permute-start.7
  32.3 1.0 %collective-permute-start.6 = (f32[16,8,512]{2,1,0:T(8,128)S(1)}, f32[16,8,512]{2,1,0:T(8,128)S(1)}, u32[]{:S(2)}, u32[]{:S(2)}) collective-permute-start(f32[16,8,512]{2,1,0:T(8,128)S(1)} %get-tuple-element.48), channel_id=1, source_target_pairs={{0,15},{1,2},{2,1},{3,4},{4,3},{5,6},{6,5},{7,8},{8,7},{9,10},{10,... | collective-permute-start | bytes 786440 | tf_op jit(solution)/shard_map/ppermute | solution.py:333
  33.3 1.2 %spread.5 = (f32[16,8,512]{2,1,0:T(8,128)S(1)}, f32[16,8,512]{2,1,0:T(8,128)S(1)}) custom-call(bf16[1024,1280]{1,0:T(8,128)(2,1)S(1)} %get-tuple-element.31.th, bf16[1024,1280]{1,0:T(8,128)(2,1)S(1)} %get-tuple-element.32.tl, bf16[1280,512]{1,0:T(8,128)(2,1)S(1)} %get-tuple-element.51.bh, bf16[1280,512]{1,0:T(8,128)(2,1)S(1)} %get-tuple-element.52.bl), custom_call_target="tpu_custom_call" | custom-call | flops 1006632960 | bytes 6291456 | tf_op jit(solution)/shard_map/spread/pallas_call | solution.py:271
  34.5 3.0 %collective-permute-start.8 = (f32[16,8,512]{2,1,0:T(8,128)S(1)}, f32[16,8,512]{2,1,0:T(8,128)S(1)}, u32[]{:S(2)}, u32[]{:S(2)}) collective-permute-start(f32[16,8,512]{2,1,0:T(8,128)S(1)} %get-tuple-element.53), channel_id=1, source_target_pairs={{0,15},{1,2},{2,1},{3,4},{4,3},{5,6},{6,5},{7,8},{8,7},{9,10},{10,... | collective-permute-start | bytes 786440 | tf_op jit(solution)/shard_map/ppermute | solution.py:333
  37.5 0.0 collective-permute-start.9
  37.5 1.2 %spread.3 = f32[16,16,512]{2,1,0:T(8,128)S(1)} custom-call(bf16[1024,1280]{1,0:T(8,128)(2,1)S(1)} %get-tuple-element.31.th, bf16[1024,1280]{1,0:T(8,128)(2,1)S(1)} %get-tuple-element.32.tl, bf16[1280,512]{1,0:T(8,128)(2,1)S(1)} %get-tuple-element.51.bh, bf16[1280,512]{1,0:T(8,128)(2,1)S(1)} %get-tuple-element.52.bl), custom_call_target="tpu_custom_call" | custom-call | flops 1006632960 | bytes 6291456 | tf_op jit(solution)/shard_map/spread/pallas_call | solution.py:271
  38.7 0.0 collective-permute-done.7
  38.7 4.4 %collective-permute-done.6 = f32[16,8,512]{2,1,0:T(8,128)S(1)} collective-permute-done((f32[16,8,512]{2,1,0:T(8,128)S(1)}, f32[16,8,512]{2,1,0:T(8,128)S(1)}, u32[]{:S(2)}, u32[]{:S(2)}) %collective-permute-start.6) | collective-permute-done | bytes 262176 | tf_op jit(solution)/shard_map/ppermute | solution.py:333
  43.1 0.1 fusion
  43.3 0.1 collective-permute-start.10
  43.4 5.6 %collective-permute-start.11 = (f32[8,16,512]{2,1,0:T(8,128)S(1)}, f32[8,16,512]{2,1,0:T(8,128)S(1)}, u32[]{:S(2)}, u32[]{:S(2)}) collective-permute-start(f32[8,16,512]{2,1,0:T(8,128)S(1)} %get-tuple-element.56), channel_id=1, source_target_pairs={{0,240},{16,0},{32,16},{48,32},{64,48},{80,64},{96,80},{112,96},{1... | collective-permute-start | bytes 786440 | tf_op jit(solution)/shard_map/ppermute | solution.py:323
  49.0 1.2 %spread.4 = f32[16,16,512]{2,1,0:T(8,128)S(1)} custom-call(bf16[1024,1280]{1,0:T(8,128)(2,1)S(1)} %get-tuple-element.31.th, bf16[1024,1280]{1,0:T(8,128)(2,1)S(1)} %get-tuple-element.32.tl, bf16[1280,512]{1,0:T(8,128)(2,1)S(1)} %get-tuple-element.51.bh, bf16[1280,512]{1,0:T(8,128)(2,1)S(1)} %get-tuple-element.52.bl), custom_call_target="tpu_custom_call" | custom-call | flops 1006632960 | bytes 6291456 | tf_op jit(solution)/shard_map/spread/pallas_call | solution.py:271
  50.2 0.0 collective-permute-done.9
  50.2 2.9 %collective-permute-done.8 = f32[16,8,512]{2,1,0:T(8,128)S(1)} collective-permute-done((f32[16,8,512]{2,1,0:T(8,128)S(1)}, f32[16,8,512]{2,1,0:T(8,128)S(1)}, u32[]{:S(2)}, u32[]{:S(2)}) %collective-permute-start.8) | collective-permute-done | bytes 262176 | tf_op jit(solution)/shard_map/ppermute | solution.py:333
  53.1 0.1 fusion.1
  53.2 0.0 collective-permute-done.11
  53.2 0.6 %collective-permute-done.10 = f32[8,16,512]{2,1,0:T(8,128)S(1)} collective-permute-done((f32[8,16,512]{2,1,0:T(8,128)S(1)}, f32[8,16,512]{2,1,0:T(8,128)S(1)}, u32[]{:S(2)}, u32[]{:S(2)}) %collective-permute-start.10) | collective-permute-done | bytes 262176 | tf_op jit(solution)/shard_map/ppermute | solution.py:323
  53.8 0.9 %maximum_add_fusion = f32[16,16,512]{2,1,0:T(8,128)} fusion(f32[16,16,512]{2,1,0:T(8,128)S(1)} %fusion.1, f32[8,16,512]{2,1,0:T(8,128)S(1)} %collective-permute-done.11, f32[8,16,512]{2,1,0:T(8,128)S(1)} %collective-permute-done.10), kind=kLoop, calls=%fused_computation.4 | loop fusion | flops 262144 | bytes 1572864 | tf_op jit(solution)/shard_map/add | solution.py:381
  (5 shorter events, 0.1 us)
Async XLA Ops:
  1.2 15.0 %collective-permute-start = (f32[8,16,512]{2,1,0:T(8,128)S(1)}, f32[8,16,512]{2,1,0:T(8,128)S(1)}, u32[]{:S(2)}, u32[]{:S(2)}) collective-permute-start(f32[8,16,512]{2,1,0:T(8,128)S(1)} %get-tuple-element.34), channel_id=1, source_target_pairs={{0,16},{16,32},{32,48},{48,64},{64,80},{80,96},{96,112},{112,128},... | collective-permute-start | bytes 786440 | tf_op jit(solution)/shard_map/ppermute | solution.py:323
  3.2 13.0 %collective-permute-start.1 = (f32[8,16,512]{2,1,0:T(8,128)S(1)}, f32[8,16,512]{2,1,0:T(8,128)S(1)}, u32[]{:S(2)}, u32[]{:S(2)}) collective-permute-start(f32[8,16,512]{2,1,0:T(8,128)S(1)} %get-tuple-element.35), channel_id=1, source_target_pairs={{0,240},{16,0},{32,16},{48,32},{64,48},{80,64},{96,80},{112,96},{1... | collective-permute-start | bytes 786440 | tf_op jit(solution)/shard_map/ppermute | solution.py:323
  7.2 14.9 %collective-permute-start.3 = (f32[16,8,512]{2,1,0:T(8,128)S(1)}, f32[16,8,512]{2,1,0:T(8,128)S(1)}, u32[]{:S(2)}, u32[]{:S(2)}) collective-permute-start(f32[16,8,512]{2,1,0:T(8,128)S(1)} %get-tuple-element.36), channel_id=1, source_target_pairs={{0,15},{1,2},{2,1},{3,4},{4,3},{5,6},{6,5},{7,8},{8,7},{9,10},{10,... | collective-permute-start | bytes 786440 | tf_op jit(solution)/shard_map/ppermute | solution.py:333
  10.9 6.5 %collective-permute-start.2 = (f32[16,8,512]{2,1,0:T(8,128)S(1)}, f32[16,8,512]{2,1,0:T(8,128)S(1)}, u32[]{:S(2)}, u32[]{:S(2)}) collective-permute-start(f32[16,8,512]{2,1,0:T(8,128)S(1)} %get-tuple-element.38), channel_id=1, source_target_pairs={{0,1},{1,0},{2,3},{3,2},{4,5},{5,4},{6,7},{7,6},{8,9},{9,8},{10,11... | collective-permute-start | bytes 786440 | tf_op jit(solution)/shard_map/ppermute | solution.py:328
  16.3 11.4 %slice-start = ((s8[6553600]{0:T(1024)(128)(4,1)}), s8[4194304]{0:T(1024)(128)(4,1)S(1)}, s32[]{:S(2)}) async-start(s8[6553600]{0:T(1024)(128)(4,1)} %bitcast), calls=%async_computation | async-start | bytes 8388608
  16.3 11.3 %collective-permute-start.5 = (f32[16,8,512]{2,1,0:T(8,128)S(1)}, f32[16,8,512]{2,1,0:T(8,128)S(1)}, u32[]{:S(2)}, u32[]{:S(2)}) collective-permute-start(f32[16,8,512]{2,1,0:T(8,128)S(1)} %get-tuple-element.60), channel_id=1, source_target_pairs={{0,15},{1,2},{2,1},{3,4},{4,3},{5,6},{6,5},{7,8},{8,7},{9,10},{10,... | collective-permute-start | bytes 786440 | tf_op jit(solution)/shard_map/ppermute | solution.py:333
  17.4 8.8 %collective-permute-start.4 = (f32[16,8,512]{2,1,0:T(8,128)S(1)}, f32[16,8,512]{2,1,0:T(8,128)S(1)}, u32[]{:S(2)}, u32[]{:S(2)}) collective-permute-start(f32[16,8,512]{2,1,0:T(8,128)S(1)} %get-tuple-element.41), channel_id=1, source_target_pairs={{0,1},{1,0},{2,3},{3,2},{4,5},{5,4},{6,7},{7,6},{8,9},{9,8},{10,11... | collective-permute-start | bytes 786440 | tf_op jit(solution)/shard_map/ppermute | solution.py:328
  22.0 5.6 %slice-start.1 = ((s8[6553600]{0:T(1024)(128)(4,1)}), s8[2359296]{0:T(1024)(128)(4,1)S(1)}, s32[]{:S(2)}) async-start(s8[6553600]{0:T(1024)(128)(4,1)} %bitcast), calls=%async_computation.1 | async-start | bytes 4718592
  32.2 6.5 %collective-permute-start.7 = (f32[16,8,512]{2,1,0:T(8,128)S(1)}, f32[16,8,512]{2,1,0:T(8,128)S(1)}, u32[]{:S(2)}, u32[]{:S(2)}) collective-permute-start(f32[16,8,512]{2,1,0:T(8,128)S(1)} %get-tuple-element.50), channel_id=1, source_target_pairs={{0,1},{1,0},{2,3},{3,2},{4,5},{5,4},{6,7},{7,6},{8,9},{9,8},{10,11... | collective-permute-start | bytes 786440 | tf_op jit(solution)/shard_map/ppermute | solution.py:328
  32.3 10.8 %collective-permute-start.6 = (f32[16,8,512]{2,1,0:T(8,128)S(1)}, f32[16,8,512]{2,1,0:T(8,128)S(1)}, u32[]{:S(2)}, u32[]{:S(2)}) collective-permute-start(f32[16,8,512]{2,1,0:T(8,128)S(1)} %get-tuple-element.48), channel_id=1, source_target_pairs={{0,15},{1,2},{2,1},{3,4},{4,3},{5,6},{6,5},{7,8},{8,7},{9,10},{10,... | collective-permute-start | bytes 786440 | tf_op jit(solution)/shard_map/ppermute | solution.py:333
  34.5 18.6 %collective-permute-start.8 = (f32[16,8,512]{2,1,0:T(8,128)S(1)}, f32[16,8,512]{2,1,0:T(8,128)S(1)}, u32[]{:S(2)}, u32[]{:S(2)}) collective-permute-start(f32[16,8,512]{2,1,0:T(8,128)S(1)} %get-tuple-element.53), channel_id=1, source_target_pairs={{0,15},{1,2},{2,1},{3,4},{4,3},{5,6},{6,5},{7,8},{8,7},{9,10},{10,... | collective-permute-start | bytes 786440 | tf_op jit(solution)/shard_map/ppermute | solution.py:333
  37.5 12.7 %collective-permute-start.9 = (f32[16,8,512]{2,1,0:T(8,128)S(1)}, f32[16,8,512]{2,1,0:T(8,128)S(1)}, u32[]{:S(2)}, u32[]{:S(2)}) collective-permute-start(f32[16,8,512]{2,1,0:T(8,128)S(1)} %get-tuple-element.55), channel_id=1, source_target_pairs={{0,1},{1,0},{2,3},{3,2},{4,5},{5,4},{6,7},{7,6},{8,9},{9,8},{10,11... | collective-permute-start | bytes 786440 | tf_op jit(solution)/shard_map/ppermute | solution.py:328
  43.3 10.5 %collective-permute-start.10 = (f32[8,16,512]{2,1,0:T(8,128)S(1)}, f32[8,16,512]{2,1,0:T(8,128)S(1)}, u32[]{:S(2)}, u32[]{:S(2)}) collective-permute-start(f32[8,16,512]{2,1,0:T(8,128)S(1)} %get-tuple-element.57), channel_id=1, source_target_pairs={{0,16},{16,32},{32,48},{48,64},{64,80},{80,96},{96,112},{112,128},... | collective-permute-start | bytes 786440 | tf_op jit(solution)/shard_map/ppermute | solution.py:323
  43.4 9.8 %collective-permute-start.11 = (f32[8,16,512]{2,1,0:T(8,128)S(1)}, f32[8,16,512]{2,1,0:T(8,128)S(1)}, u32[]{:S(2)}, u32[]{:S(2)}) collective-permute-start(f32[8,16,512]{2,1,0:T(8,128)S(1)} %get-tuple-element.56), channel_id=1, source_target_pairs={{0,240},{16,0},{32,16},{48,32},{64,48},{80,64},{96,80},{112,96},{1... | collective-permute-start | bytes 786440 | tf_op jit(solution)/shard_map/ppermute | solution.py:323

commit v7 on v6

--- a/solution.py
+++ b/solution.py
@@ -333,6 +333,40 @@
     return lax.ppermute(cells, "gy", [(j, (j + (1 if j % 2 else -1)) % count) for j in range(count)])
 
 
+RUN = 8
+
+
+def b_place(j, count):
+    return (j + (1 if j % 2 else -1)) % count
+
+
+def over_both(cells, chosen):
+    rows, cols = lax.axis_size("gx"), lax.axis_size("gy")
+    pairs = [
+        (i * cols + j, (i + chosen(i)) % rows * cols + b_place(j, cols))
+        for i in range(rows)
+        for j in range(cols)
+        if chosen(i) is not None
+    ]
+    return lax.ppermute(cells, ("gx", "gy"), pairs)
+
+
+def swap_b_within(cells):
+    return over_both(cells, lambda i: None if i % RUN in (0, RUN - 1) else 0)
+
+
+def over_wrap(cells):
+    return over_both(cells, lambda i: {0: -1, RUN - 1: 1}.get(i % RUN))
+
+
+def to_ends(cells):
+    return over_both(cells, lambda i: {1: -1, RUN - 2: 1}.get(i % RUN))
+
+
+def from_ends(cells):
+    return over_both(cells, lambda i: {0: 1, RUN - 1: -1}.get(i % RUN))
+
+
 def swapped(for_b, for_a):
     from_b = swap_b(for_b)
     for_b, for_a = lax.optimization_barrier((for_b, for_a))
@@ -355,18 +389,26 @@
     north = shift(last, "gx", 1)
     south = shift(first, "gx", -1)
     side_b, side_a = swapped(cols_b, cols_a)
+    lower = lax.rem(lax.axis_index("gx"), RUN) >= RUN // 2
+    facing = jnp.where(lower, cols_b[reach:], cols_b[:reach])
+    beyond, within = over_wrap(facing), to_ends(facing)
 
     nh, nl, ch, cl, th, tl, bands, bands_t = build(kernel_rows, kernel_cols, kernel_depth, depth)
 
     sides = jnp.concatenate([north, south], 0)
-    corner_b, corner_a = swapped(side_cols(sides, 1 - right), side_cols(sides, right))
+    corner_b = swap_b_within(side_cols(sides, 1 - right))
+    corner_a = swap_a(side_cols(sides, right))
+    direct = jnp.where(lower, jnp.concatenate([within, beyond], 0), jnp.concatenate([beyond, within], 0))
+    corner_b = corner_b + direct
 
     partial = near((tile, north, south, side_a, side_b), nh, nl)
     to_a, to_b, bh, bl = middle(partial, corner_a, corner_b, ch, cl, bands, bands_t, th, tl, hessian)
-    from_b, from_a = swapped(to_b, to_a)
+    from_b, from_a = swap_b_within(to_b), swap_a(to_a)
 
     edge_a, edge_b = spread(2, th, tl, bh, bl, [(span_rows, reach)] * 2)
     edge_from_b, edge_from_a = swapped(edge_b, edge_a)
+    beyond = over_wrap(jnp.where(lower, to_b[reach:], to_b[:reach]))
+    within = from_ends(jnp.where(lower, to_b[:reach], to_b[reach:]))
 
     (around,) = spread(1, th, tl, bh, bl, [(span_rows, span_cols)])
     around = around + joined(from_a, from_b)
@@ -377,7 +419,10 @@
 
     around, bh, bl = lax.optimization_barrier((around, bh, bl))
     (own,) = spread(0, th, tl, bh, bl, [(span_rows, span_cols)])
-    own = lax.optimization_barrier(own + joined(edge_from_a, edge_from_b))
+    direct = beyond + within
+    blank = jnp.zeros_like(direct)
+    direct = jnp.where(lower, jnp.concatenate([blank, direct], 0), jnp.concatenate([direct, blank], 0))
+    own = lax.optimization_barrier(own + joined(edge_from_a, edge_from_b + direct))
     return own + jnp.concatenate([side_from_n, side_from_s], 0)
 
 

time: 54.8 us -> 69.9 us (1.28)
  the two profiles are of different devices: /device:TPU:4 before, /device:TPU:1 now
where the time goes in v7:
time: 69.9 us; the launch traced here: 69.7 us
  starting transfers between devices  43.3 us (62%)
  Pallas kernels  18.6 us (27%)
  waiting for transfers between devices  6.1 us (9%)
  other arithmetic  1.24 us (2%)
    ppermute x6, starting transfers between devices, over_both(): return lax.ppermute(cells, ('gx', 'gy'), pairs)  20.7 us
    ppermute x4, starting transfers between devices, shift(): lax.ppermute(cells, axis, [(i, (i + step) % count) for i in range(count)])  14.2 us
    ppermute x4, starting transfers between devices, swap_a(): return lax.ppermute(cells, 'gy', [(j, j ^ 1) for j in range(count)])  7.13 us
    pallas_call x1, Pallas kernels, build(): pl.pallas_call(build_kernel, out_shape=[jax.ShapeDtypeStruct(s, jnp.bfloa...  5.3 us
    pallas_call x1, Pallas kernels, middle(): pl.pallas_call(middle_kernel, out_shape=[edge, edge, back, back], in_spec...  4.5 us
    pallas_call x1, Pallas kernels, near(): pl.pallas_call(near_kernel, out_shape=jax.ShapeDtypeStruct((DENSITIES * C...  4.11 us
    pallas_call x3, Pallas kernels, spread(): pl.pallas_call(functools.partial(spread_kernel, group), out_shape=[jax.Sh...  3.51 us
    ppermute x2, waiting for transfers between devices, swap_b(): lax.ppermute(cells, 'gy', [(j, (j + (1 if j % 2 else -1)) % count) for j...  2.96 us
  transfers between devices with their start and end apart: 16, of which 4 were waited for; matrix products, arithmetic and copies ran while one was open for 1% of the time, Pallas kernels for 19%

profile of v7, /device:TPU:1, one launch (start us, length us, event | category | flops | bytes accessed | tf_op | source)
XLA Modules:
  0.0 69.7 jit_solution(18140362126743265386)
XLA Ops:
  0.0 1.2 %cut.1 = (f32[8,16,512]{2,1,0:T(8,128)S(1)}, f32[8,16,512]{2,1,0:T(8,128)S(1)}, f32[16,8,512]{2,1,0:T(8,128)S(1)}, f32[16,8,512]{2,1,0:T(8,128)S(1)}, f32[16,16,512]{2,1,0:T(8,128)S(1)}) custom-call(f32[16,16,512]{2,1,0:T(8,128)} %tangent.1), custom_call_target="tpu_custom_call" | custom-call | bytes 3145728 | tf_op jit(solution)/shard_map/cut/pallas_call | solution.py:309
  1.2 2.5 %collective-permute-start = (f32[8,16,512]{2,1,0:T(8,128)S(1)}, f32[8,16,512]{2,1,0:T(8,128)S(1)}, u32[]{:S(2)}, u32[]{:S(2)}) collective-permute-start(f32[8,16,512]{2,1,0:T(8,128)S(1)} %get-tuple-element.32), channel_id=1, source_target_pairs={{0,16},{16,32},{32,48},{48,64},{64,80},{80,96},{96,112},{112,128},... | collective-permute-start | bytes 786440 | tf_op jit(solution)/shard_map/ppermute | solution.py:323
  3.7 6.5 %collective-permute-start.1 = (f32[8,16,512]{2,1,0:T(8,128)S(1)}, f32[8,16,512]{2,1,0:T(8,128)S(1)}, u32[]{:S(2)}, u32[]{:S(2)}) collective-permute-start(f32[8,16,512]{2,1,0:T(8,128)S(1)} %get-tuple-element.33), channel_id=1, source_target_pairs={{0,240},{16,0},{32,16},{48,32},{64,48},{80,64},{96,80},{112,96},{1... | collective-permute-start | bytes 786440 | tf_op jit(solution)/shard_map/ppermute | solution.py:323
  10.2 1.2 %collective-permute-start.3 = (f32[16,8,512]{2,1,0:T(8,128)S(1)}, f32[16,8,512]{2,1,0:T(8,128)S(1)}, u32[]{:S(2)}, u32[]{:S(2)}) collective-permute-start(f32[16,8,512]{2,1,0:T(8,128)S(1)} %get-tuple-element.34), channel_id=1, source_target_pairs={{0,15},{1,2},{2,1},{3,4},{4,3},{5,6},{6,5},{7,8},{8,7},{9,10},{10,... | collective-permute-start | bytes 786440 | tf_op jit(solution)/shard_map/ppermute | solution.py:333
  11.4 3.0 %collective-permute-start.7 = (f32[8,8,512]{2,1,0:T(8,128)S(1)}, f32[8,8,512]{2,1,0:T(8,128)S(1)}, u32[]{:S(2)}, u32[]{:S(2)}) collective-permute-start(f32[8,8,512]{2,1,0:T(8,128)S(1)} %slice_select_fusion.2), channel_id=1, source_target_pairs={{0,255},{1,242},{2,241},{3,244},{4,243},{5,246},{6,245},{7,248},{8... | collective-permute-start | bytes 393224 | tf_op jit(solution)/shard_map/ppermute | solution.py:351
  14.4 1.3 %collective-permute-start.6 = (f32[8,8,512]{2,1,0:T(8,128)S(1)}, f32[8,8,512]{2,1,0:T(8,128)S(1)}, u32[]{:S(2)}, u32[]{:S(2)}) collective-permute-start(f32[8,8,512]{2,1,0:T(8,128)S(1)} %slice_select_fusion.2), channel_id=1, source_target_pairs={{16,15},{17,2},{18,1},{19,4},{20,3},{21,6},{22,5},{23,8},{24,7},{2... | collective-permute-start | bytes 393224 | tf_op jit(solution)/shard_map/ppermute | solution.py:351
  15.7 5.3 %build.1 = (bf16[1280,768]{1,0:T(8,128)(2,1)S(1)}, bf16[1280,768]{1,0:T(8,128)(2,1)S(1)}, bf16[1280,256]{1,0:T(8,128)(2,1)S(1)}, bf16[1280,256]{1,0:T(8,128)(2,1...) custom-call(f32[5,17]{1,0:T(8,128)} %kr_hbm.1, ...), custom_call_target="tpu_custom_call" | custom-call | flops 31457280 | bytes 16777216 | tf_op jit(solution)/shard_map/build/pallas_call | solution.py:137
  21.0 0.0 collective-permute-done.north
  21.0 3.1 %collective-permute-start.2 = (f32[16,8,512]{2,1,0:T(8,128)S(1)}, f32[16,8,512]{2,1,0:T(8,128)S(1)}, u32[]{:S(2)}, u32[]{:S(2)}) collective-permute-start(f32[16,8,512]{2,1,0:T(8,128)S(1)} %get-tuple-element.36), channel_id=1, source_target_pairs={{0,1},{1,0},{2,3},{3,2},{4,5},{5,4},{6,7},{7,6},{8,9},{9,8},{10,11... | collective-permute-start | bytes 786440 | tf_op jit(solution)/shard_map/ppermute | solution.py:328
  24.2 0.0 collective-permute-done.1.south
  24.3 0.1 collective-permute-start.4
  24.4 0.9 %collective-permute-done.2.side_a = f32[16,8,512]{2,1,0:T(8,128)S(1)} collective-permute-done((f32[16,8,512]{2,1,0:T(8,128)S(1)}, f32[16,8,512]{2,1,0:T(8,128)S(1)}, u32[]{:S(2)}, u32[]{:S(2)}) %collective-permute-start.2) | collective-permute-done | bytes 262176 | tf_op jit(solution)/shard_map/ppermute | solution.py:328
  25.3 0.7 collective-permute-start.5
  26.0 0.0 collective-permute-done.3.side_b
  26.0 0.0 slice-start
  26.0 0.0 slice-start.1
  26.0 4.1 %near.1.partial = f32[1280,512]{1,0:T(8,128)S(1)} custom-call(f32[16,16,512]{2,1,0:T(8,128)S(1)} %get-tuple-element.31.own, f32[8,16,512]{2,1,0:T(8,128)S(1)} %collective-permute-done.north, f32[8,16,512]{2,1,0:T(8,128)S(1)} %collective-permute-done.1.south, f32[16,8,512]{2,1,0:T(8,128)S(1)} %collective-permute-done.2.side_a, ...), custom_call_target="tpu_custom_call" | custom-call | flops 3019898880 | bytes 10485760 | tf_op jit(solution)/shard_map/near/pallas_call | solution.py:188
  30.2 0.0 collective-permute-done.7
  30.2 0.0 collective-permute-done.6
  30.2 0.0 collective-permute-done.5
  30.2 0.0 collective-permute-done.4.corner_a
  30.3 0.0 slice-done
  30.3 0.0 slice-done.1
  30.3 4.5 %middle.1 = (f32[16,8,512]{2,1,0:T(8,128)S(1)}, f32[16,8,512]{2,1,0:T(8,128)S(1)}, bf16[1280,512]{1,0:T(8,128)(2,1)S(1)}, bf16[1280,512]{1,0:T(8,128)(2,1)S(1)}) custom-call(f32[1280,512]{1,0:T(8,128)S(1)} %near.1.partial, f32[16,8,512]{2,1,0:T(8,128)S(1)} %collective-permute-done.4.corner_a, f32[16,8,512]{2,1,0:T(8,128)S(1)} %fusion.2.corner_b, ...), custom_call_target="tpu_custom_call" | custom-call | flops 3355443200 | bytes 16777216 | tf_op jit(solution)/shard_map/middle/pallas_call | solution.py:239
  34.8 0.5 collective-permute-start.9
  35.3 0.7 collective-permute-start.8
  36.0 4.7 %collective-permute-start.11 = (f32[8,8,512]{2,1,0:T(8,128)S(1)}, f32[8,8,512]{2,1,0:T(8,128)S(1)}, u32[]{:S(2)}, u32[]{:S(2)}) collective-permute-start(f32[8,8,512]{2,1,0:T(8,128)S(1)} %get-tuple-element.58), channel_id=1, source_target_pairs={{0,255},{1,242},{2,241},{3,244},{4,243},{5,246},{6,245},{7,248},{8... | collective-permute-start | bytes 393224 | tf_op jit(solution)/shard_map/ppermute | solution.py:351
  40.6 10.5 %collective-permute-start.12 = (f32[8,8,512]{2,1,0:T(8,128)S(1)}, f32[8,8,512]{2,1,0:T(8,128)S(1)}, u32[]{:S(2)}, u32[]{:S(2)}) collective-permute-start(f32[8,8,512]{2,1,0:T(8,128)S(1)} %get-tuple-element.57), channel_id=1, source_target_pairs={{0,31},{1,18},{2,17},{3,20},{4,19},{5,22},{6,21},{7,24},{8,23},{9,... | collective-permute-start | bytes 393224 | tf_op jit(solution)/shard_map/ppermute | solution.py:351
  51.1 1.2 %spread.5 = (f32[16,8,512]{2,1,0:T(8,128)S(1)}, f32[16,8,512]{2,1,0:T(8,128)S(1)}) custom-call(bf16[1024,1280]{1,0:T(8,128)(2,1)S(1)} %get-tuple-element.29.th, bf16[1024,1280]{1,0:T(8,128)(2,1)S(1)} %get-tuple-element.30.tl, bf16[1280,512]{1,0:T(8,128)(2,1)S(1)} %get-tuple-element.47.bh, bf16[1280,512]{1,0:T(8,128)(2,1)S(1)} %get-tuple-element.48.bl), custom_call_target="tpu_custom_call" | custom-call | flops 1006632960 | bytes 6291456 | tf_op jit(solution)/shard_map/spread/pallas_call | solution.py:271
  52.3 0.1 collective-permute-start.10
  52.4 1.2 %spread.3 = f32[16,16,512]{2,1,0:T(8,128)S(1)} custom-call(bf16[1024,1280]{1,0:T(8,128)(2,1)S(1)} %get-tuple-element.29.th, bf16[1024,1280]{1,0:T(8,128)(2,1)S(1)} %get-tuple-element.30.tl, bf16[1280,512]{1,0:T(8,128)(2,1)S(1)} %get-tuple-element.47.bh, bf16[1280,512]{1,0:T(8,128)(2,1)S(1)} %get-tuple-element.48.bl), custom_call_target="tpu_custom_call" | custom-call | flops 1006632960 | bytes 6291456 | tf_op jit(solution)/shard_map/spread/pallas_call | solution.py:271
  53.5 0.0 collective-permute-done.11
  53.6 3.4 %collective-permute-start.13 = (f32[16,8,512]{2,1,0:T(8,128)S(1)}, f32[16,8,512]{2,1,0:T(8,128)S(1)}, u32[]{:S(2)}, u32[]{:S(2)}) collective-permute-start(f32[16,8,512]{2,1,0:T(8,128)S(1)} %get-tuple-element.51), channel_id=1, source_target_pairs={{0,1},{1,0},{2,3},{3,2},{4,5},{5,4},{6,7},{7,6},{8,9},{9,8},{10,11... | collective-permute-start | bytes 786440 | tf_op jit(solution)/shard_map/ppermute | solution.py:328
  57.0 0.0 collective-permute-done.12
  57.0 0.0 collective-permute-done.9
  57.0 0.0 collective-permute-done.8
  57.0 0.1 fusion
  57.2 0.1 collective-permute-start.14
  57.3 5.1 %collective-permute-start.15 = (f32[8,16,512]{2,1,0:T(8,128)S(1)}, f32[8,16,512]{2,1,0:T(8,128)S(1)}, u32[]{:S(2)}, u32[]{:S(2)}) collective-permute-start(f32[8,16,512]{2,1,0:T(8,128)S(1)} %get-tuple-element.52), channel_id=1, source_target_pairs={{0,240},{16,0},{32,16},{48,32},{64,48},{80,64},{96,80},{112,96},{1... | collective-permute-start | bytes 786440 | tf_op jit(solution)/shard_map/ppermute | solution.py:323
  62.4 3.0 %collective-permute-done.10 = f32[16,8,512]{2,1,0:T(8,128)S(1)} collective-permute-done((f32[16,8,512]{2,1,0:T(8,128)S(1)}, f32[16,8,512]{2,1,0:T(8,128)S(1)}, u32[]{:S(2)}, u32[]{:S(2)}) %collective-permute-start.10) | collective-permute-done | bytes 262176 | tf_op jit(solution)/shard_map/ppermute | solution.py:333
  65.3 1.2 %spread.4 = f32[16,16,512]{2,1,0:T(8,128)S(1)} custom-call(bf16[1024,1280]{1,0:T(8,128)(2,1)S(1)} %get-tuple-element.29.th, bf16[1024,1280]{1,0:T(8,128)(2,1)S(1)} %get-tuple-element.30.tl, bf16[1280,512]{1,0:T(8,128)(2,1)S(1)} %get-tuple-element.47.bh, bf16[1280,512]{1,0:T(8,128)(2,1)S(1)} %get-tuple-element.48.bl), custom_call_target="tpu_custom_call" | custom-call | flops 1006632960 | bytes 6291456 | tf_op jit(solution)/shard_map/spread/pallas_call | solution.py:271
  66.5 0.0 collective-permute-done.13
  66.5 0.1 fusion.1
  66.6 1.1 %collective-permute-done.15 = f32[8,16,512]{2,1,0:T(8,128)S(1)} collective-permute-done((f32[8,16,512]{2,1,0:T(8,128)S(1)}, f32[8,16,512]{2,1,0:T(8,128)S(1)}, u32[]{:S(2)}, u32[]{:S(2)}) %collective-permute-start.15) | collective-permute-done | bytes 262176 | tf_op jit(solution)/shard_map/ppermute | solution.py:323
  67.7 1.1 %collective-permute-done.14 = f32[8,16,512]{2,1,0:T(8,128)S(1)} collective-permute-done((f32[8,16,512]{2,1,0:T(8,128)S(1)}, f32[8,16,512]{2,1,0:T(8,128)S(1)}, u32[]{:S(2)}, u32[]{:S(2)}) %collective-permute-start.14) | collective-permute-done | bytes 262176 | tf_op jit(solution)/shard_map/ppermute | solution.py:323
  68.8 0.9 %maximum_add_fusion = f32[16,16,512]{2,1,0:T(8,128)} fusion(f32[16,16,512]{2,1,0:T(8,128)S(1)} %fusion.1, f32[8,16,512]{2,1,0:T(8,128)S(1)} %collective-permute-done.15, f32[8,16,512]{2,1,0:T(8,128)S(1)} %collective-permute-done.14), kind=kLoop, calls=%fused_computation.4 | loop fusion | flops 262144 | bytes 1572864 | tf_op jit(solution)/shard_map/add | solution.py:426
  (10 shorter events, 0.2 us)
Async XLA Ops:
  1.2 19.8 %collective-permute-start = (f32[8,16,512]{2,1,0:T(8,128)S(1)}, f32[8,16,512]{2,1,0:T(8,128)S(1)}, u32[]{:S(2)}, u32[]{:S(2)}) collective-permute-start(f32[8,16,512]{2,1,0:T(8,128)S(1)} %get-tuple-element.32), channel_id=1, source_target_pairs={{0,16},{16,32},{32,48},{48,64},{64,80},{80,96},{96,112},{112,128},... | collective-permute-start | bytes 786440 | tf_op jit(solution)/shard_map/ppermute | solution.py:323
  3.7 20.5 %collective-permute-start.1 = (f32[8,16,512]{2,1,0:T(8,128)S(1)}, f32[8,16,512]{2,1,0:T(8,128)S(1)}, u32[]{:S(2)}, u32[]{:S(2)}) collective-permute-start(f32[8,16,512]{2,1,0:T(8,128)S(1)} %get-tuple-element.33), channel_id=1, source_target_pairs={{0,240},{16,0},{32,16},{48,32},{64,48},{80,64},{96,80},{112,96},{1... | collective-permute-start | bytes 786440 | tf_op jit(solution)/shard_map/ppermute | solution.py:323
  10.2 15.8 %collective-permute-start.3 = (f32[16,8,512]{2,1,0:T(8,128)S(1)}, f32[16,8,512]{2,1,0:T(8,128)S(1)}, u32[]{:S(2)}, u32[]{:S(2)}) collective-permute-start(f32[16,8,512]{2,1,0:T(8,128)S(1)} %get-tuple-element.34), channel_id=1, source_target_pairs={{0,15},{1,2},{2,1},{3,4},{4,3},{5,6},{6,5},{7,8},{8,7},{9,10},{10,... | collective-permute-start | bytes 786440 | tf_op jit(solution)/shard_map/ppermute | solution.py:333
  11.4 18.8 %collective-permute-start.7 = (f32[8,8,512]{2,1,0:T(8,128)S(1)}, f32[8,8,512]{2,1,0:T(8,128)S(1)}, u32[]{:S(2)}, u32[]{:S(2)}) collective-permute-start(f32[8,8,512]{2,1,0:T(8,128)S(1)} %slice_select_fusion.2), channel_id=1, source_target_pairs={{0,255},{1,242},{2,241},{3,244},{4,243},{5,246},{6,245},{7,248},{8... | collective-permute-start | bytes 393224 | tf_op jit(solution)/shard_map/ppermute | solution.py:351
  14.4 15.8 %collective-permute-start.6 = (f32[8,8,512]{2,1,0:T(8,128)S(1)}, f32[8,8,512]{2,1,0:T(8,128)S(1)}, u32[]{:S(2)}, u32[]{:S(2)}) collective-permute-start(f32[8,8,512]{2,1,0:T(8,128)S(1)} %slice_select_fusion.2), channel_id=1, source_target_pairs={{16,15},{17,2},{18,1},{19,4},{20,3},{21,6},{22,5},{23,8},{24,7},{2... | collective-permute-start | bytes 393224 | tf_op jit(solution)/shard_map/ppermute | solution.py:351
  21.0 4.3 %collective-permute-start.2 = (f32[16,8,512]{2,1,0:T(8,128)S(1)}, f32[16,8,512]{2,1,0:T(8,128)S(1)}, u32[]{:S(2)}, u32[]{:S(2)}) collective-permute-start(f32[16,8,512]{2,1,0:T(8,128)S(1)} %get-tuple-element.36), channel_id=1, source_target_pairs={{0,1},{1,0},{2,3},{3,2},{4,5},{5,4},{6,7},{7,6},{8,9},{9,8},{10,11... | collective-permute-start | bytes 786440 | tf_op jit(solution)/shard_map/ppermute | solution.py:328
  24.3 6.0 %collective-permute-start.4 = (f32[16,8,512]{2,1,0:T(8,128)S(1)}, f32[16,8,512]{2,1,0:T(8,128)S(1)}, u32[]{:S(2)}, u32[]{:S(2)}) collective-permute-start(f32[16,8,512]{2,1,0:T(8,128)S(1)} %get-tuple-element.56), channel_id=1, source_target_pairs={{0,1},{1,0},{2,3},{3,2},{4,5},{5,4},{6,7},{7,6},{8,9},{9,8},{10,11... | collective-permute-start | bytes 786440 | tf_op jit(solution)/shard_map/ppermute | solution.py:328
  25.3 4.8 %collective-permute-start.5 = (f32[16,8,512]{2,1,0:T(8,128)S(1)}, f32[16,8,512]{2,1,0:T(8,128)S(1)}, u32[]{:S(2)}, u32[]{:S(2)}) collective-permute-start(f32[16,8,512]{2,1,0:T(8,128)S(1)} %get-tuple-element.55), channel_id=1, source_target_pairs={{16,31},{17,18},{18,17},{19,20},{20,19},{21,22},{22,21},{23,24},{2... | collective-permute-start | bytes 786440 | tf_op jit(solution)/shard_map/ppermute | solution.py:351
  26.0 4.2 %slice-start = ((s8[6553600]{0:T(1024)(128)(4,1)}), s8[4194304]{0:T(1024)(128)(4,1)S(1)}, s32[]{:S(2)}) async-start(s8[6553600]{0:T(1024)(128)(4,1)} %bitcast), calls=%async_computation | async-start | bytes 8388608
  26.0 4.2 %slice-start.1 = ((s8[6553600]{0:T(1024)(128)(4,1)}), s8[2359296]{0:T(1024)(128)(4,1)S(1)}, s32[]{:S(2)}) async-start(s8[6553600]{0:T(1024)(128)(4,1)} %bitcast), calls=%async_computation.1 | async-start | bytes 4718592
  34.8 22.2 %collective-permute-start.9 = (f32[16,8,512]{2,1,0:T(8,128)S(1)}, f32[16,8,512]{2,1,0:T(8,128)S(1)}, u32[]{:S(2)}, u32[]{:S(2)}) collective-permute-start(f32[16,8,512]{2,1,0:T(8,128)S(1)} %get-tuple-element.46), channel_id=1, source_target_pairs={{0,1},{1,0},{2,3},{3,2},{4,5},{5,4},{6,7},{7,6},{8,9},{9,8},{10,11... | collective-permute-start | bytes 786440 | tf_op jit(solution)/shard_map/ppermute | solution.py:328
  35.3 21.8 %collective-permute-start.8 = (f32[16,8,512]{2,1,0:T(8,128)S(1)}, f32[16,8,512]{2,1,0:T(8,128)S(1)}, u32[]{:S(2)}, u32[]{:S(2)}) collective-permute-start(f32[16,8,512]{2,1,0:T(8,128)S(1)} %get-tuple-element.45), channel_id=1, source_target_pairs={{16,31},{17,18},{18,17},{19,20},{20,19},{21,22},{22,21},{23,24},{2... | collective-permute-start | bytes 786440 | tf_op jit(solution)/shard_map/ppermute | solution.py:351
  36.0 17.6 %collective-permute-start.11 = (f32[8,8,512]{2,1,0:T(8,128)S(1)}, f32[8,8,512]{2,1,0:T(8,128)S(1)}, u32[]{:S(2)}, u32[]{:S(2)}) collective-permute-start(f32[8,8,512]{2,1,0:T(8,128)S(1)} %get-tuple-element.58), channel_id=1, source_target_pairs={{0,255},{1,242},{2,241},{3,244},{4,243},{5,246},{6,245},{7,248},{8... | collective-permute-start | bytes 393224 | tf_op jit(solution)/shard_map/ppermute | solution.py:351
  40.6 16.4 %collective-permute-start.12 = (f32[8,8,512]{2,1,0:T(8,128)S(1)}, f32[8,8,512]{2,1,0:T(8,128)S(1)}, u32[]{:S(2)}, u32[]{:S(2)}) collective-permute-start(f32[8,8,512]{2,1,0:T(8,128)S(1)} %get-tuple-element.57), channel_id=1, source_target_pairs={{0,31},{1,18},{2,17},{3,20},{4,19},{5,22},{6,21},{7,24},{8,23},{9,... | collective-permute-start | bytes 393224 | tf_op jit(solution)/shard_map/ppermute | solution.py:351
  52.3 13.0 %collective-permute-start.10 = (f32[16,8,512]{2,1,0:T(8,128)S(1)}, f32[16,8,512]{2,1,0:T(8,128)S(1)}, u32[]{:S(2)}, u32[]{:S(2)}) collective-permute-start(f32[16,8,512]{2,1,0:T(8,128)S(1)} %get-tuple-element.49), channel_id=1, source_target_pairs={{0,15},{1,2},{2,1},{3,4},{4,3},{5,6},{6,5},{7,8},{8,7},{9,10},{10,... | collective-permute-start | bytes 786440 | tf_op jit(solution)/shard_map/ppermute | solution.py:333
  53.6 13.0 %collective-permute-start.13 = (f32[16,8,512]{2,1,0:T(8,128)S(1)}, f32[16,8,512]{2,1,0:T(8,128)S(1)}, u32[]{:S(2)}, u32[]{:S(2)}) collective-permute-start(f32[16,8,512]{2,1,0:T(8,128)S(1)} %get-tuple-element.51), channel_id=1, source_target_pairs={{0,1},{1,0},{2,3},{3,2},{4,5},{5,4},{6,7},{7,6},{8,9},{9,8},{10,11... | collective-permute-start | bytes 786440 | tf_op jit(solution)/shard_map/ppermute | solution.py:328
  57.2 11.6 %collective-permute-start.14 = (f32[8,16,512]{2,1,0:T(8,128)S(1)}, f32[8,16,512]{2,1,0:T(8,128)S(1)}, u32[]{:S(2)}, u32[]{:S(2)}) collective-permute-start(f32[8,16,512]{2,1,0:T(8,128)S(1)} %get-tuple-element.53), channel_id=1, source_target_pairs={{0,16},{16,32},{32,48},{48,64},{64,80},{80,96},{96,112},{112,128},... | collective-permute-start | bytes 786440 | tf_op jit(solution)/shard_map/ppermute | solution.py:323
  57.3 10.5 %collective-permute-start.15 = (f32[8,16,512]{2,1,0:T(8,128)S(1)}, f32[8,16,512]{2,1,0:T(8,128)S(1)}, u32[]{:S(2)}, u32[]{:S(2)}) collective-permute-start(f32[8,16,512]{2,1,0:T(8,128)S(1)} %get-tuple-element.52), channel_id=1, source_target_pairs={{0,240},{16,0},{32,16},{48,32},{64,48},{80,64},{96,80},{112,96},{1... | collective-permute-start | bytes 786440 | tf_op jit(solution)/shard_map/ppermute | solution.py:323

commit v8 on v6

--- a/solution.py
+++ b/solution.py
@@ -86,10 +86,11 @@
             group, half = (first + index) // 2, (first + index) % 2
             lane, tile_place = iota((TILE, LANES), 1), iota((TILE, LANES), 0)
             wide, slim = lane >> 4, lane >> 3
-            row = jnp.where(group == 2, slim, jnp.where(slim < RADIUS, slim - RADIUS, slim + RADIUS))
-            row = jnp.where(group == 1, wide - RADIUS + TURN * half, row)
+            row = jnp.where(group == 1, wide - RADIUS + TURN * half, slim)
             row = jnp.where(group == 0, wide + RADIUS * half, row)
-            side = half + right - 2 * half * right
+            row = jnp.where(group == 3, (slim & 7) - RADIUS + TURN * half, row)
+            side = jnp.where(group == 3, lane >> 6, half)
+            side = side + right - 2 * side * right
             col = jnp.where(group < 2, lane & 15, (lane & 7) - RADIUS + TURN * side)
             by_row = taps_of_all(kr, row - tile_place)
             by_col = taps_of_all(kc, col - tile_place)
@@ -201,17 +202,22 @@
 
 def middle_kernel(
     partial, corner_a, corner_b, wh, wl, bands, bands_t, th, tl, hessian, out_a, out_b, bh, bl,
-    xh, xl, dens, low
+    dens, low
 ):
     depth = partial.shape[-1]
     half = CELLS // 2
-    for start, ref in ((0, corner_a), (half, corner_b)):
-        high, rest = halves(ref[...].reshape(half, depth))
-        xh[start : start + half] = high
-        xl[start : start + half] = rest
+    terms = []
+    for part in range(2):
+        pieces = [ref[part * RADIUS : (part + 1) * RADIUS].reshape(half // 2, depth) for ref in (corner_a, corner_b)]
+        high, rest = halves(jnp.concatenate(pieces, 0))
+        lanes = slice(part * half, (part + 1) * half)
+        tile_rows = [slice(b * CELLS + part * half, b * CELLS + (part + 1) * half) for b in range(DENSITIES)]
+        of_all = lambda ref: jnp.concatenate([ref[rows, lanes] for rows in tile_rows], 0)
+        terms.append(dot3(of_all(wh), of_all(wl), high, rest))
     for b in range(DENSITIES):
         rows = slice(b * CELLS, (b + 1) * CELLS)
-        lateral = partial[rows] + dot3(wh[rows], wl[rows], xh[...], xl[...])
+        own = slice(b * half, (b + 1) * half)
+        lateral = partial[rows] + jnp.concatenate([terms[0][own], terms[1][own]], 0)
         dens[b] = jnp.dot(lateral.astype(jnp.bfloat16), bands[b], preferred_element_type=jnp.float32)
     for a in range(DENSITIES):
         for r in range(TILE):
@@ -242,8 +248,6 @@
         in_specs=[vmem] * 10,
         out_specs=[vmem] * 4,
         scratch_shapes=[
-            pltpu.VMEM((CELLS, depth), jnp.bfloat16),
-            pltpu.VMEM((CELLS, depth), jnp.bfloat16),
             pltpu.VMEM((DENSITIES, CELLS, depth), jnp.float32),
             pltpu.VMEM((DENSITIES, CELLS, depth), jnp.bfloat16),
         ],
@@ -256,13 +260,14 @@
 
 
 def spread_kernel(group, th, tl, bh, bl, *outs):
-    rows = slice(group * CELLS, (group + 1) * CELLS)
-    total = dot3(th[rows], tl[rows], bh[...], bl[...])
-    start = 0
-    for out in outs:
-        size = out.shape[0] * out.shape[1]
-        out[...] = total[start : start + size].reshape(out.shape)
-        start += size
+    start = group * CELLS
+    for first in range(0, len(outs), 2):
+        pair = outs[first : first + 2]
+        sizes = [out.shape[0] * out.shape[1] for out in pair]
+        total = dot3(th[start : start + sum(sizes)], tl[start : start + sum(sizes)], bh[...], bl[...])
+        start += sum(sizes)
+        for out, size, offset in zip(pair, sizes, (0, sizes[0])):
+            out[...] = total[offset : offset + size].reshape(out.shape)
 
 
 def spread(group, th, tl, bh, bl, shapes):
@@ -275,7 +280,7 @@
         out_specs=[vmem] * len(shapes),
         compiler_params=pltpu.CompilerParams(vmem_limit_bytes=16 << 20),
         cost_estimate=pl.CostEstimate(
-            flops=6 * CELLS * th.shape[1] * depth, bytes_accessed=6 << 20, transcendentals=0
+            flops=6 * sum(r * c for r, c in shapes) * th.shape[1] * depth, bytes_accessed=6 << 20, transcendentals=0
         ),
         name="spread",
     )(th, tl, bh, bl)
@@ -365,11 +370,12 @@
     to_a, to_b, bh, bl = middle(partial, corner_a, corner_b, ch, cl, bands, bands_t, th, tl, hessian)
     from_b, from_a = swapped(to_b, to_a)
 
-    edge_a, edge_b = spread(2, th, tl, bh, bl, [(span_rows, reach)] * 2)
+    above, below, edge_a, edge_b = spread(
+        1, th, tl, bh, bl, [(reach, span_cols)] * 2 + [(span_rows, reach)] * 2
+    )
     edge_from_b, edge_from_a = swapped(edge_b, edge_a)
 
-    (around,) = spread(1, th, tl, bh, bl, [(span_rows, span_cols)])
-    around = around + joined(from_a, from_b)
+    around = jnp.concatenate([above, below], 0) + joined(from_a, from_b)
     above, below = around[:reach], around[reach:]
     side_from_n = shift(below, "gx", 1)
     above, below = lax.optimization_barrier((above, below))

time: 54.8 us -> 53.8 us (0.982)
  Pallas kernels: 18.6 us -> 17.9 us
    pallas_call x1, Pallas kernels: 4.49 us -> 3.91 us  [middle(): pl.pallas_call(middle_kernel, out_shape=[edge, edge, back, back], in_spec...]
    pallas_call x3 -> x2, Pallas kernels: 3.5 us -> 3.35 us  [spread(): pl.pallas_call(functools.partial(spread_kernel, group), out_shape=[jax.Sh...]
where the time goes in v8:
time: 53.8 us; the launch traced here: 53.6 us
  starting transfers between devices  20.6 us (38%)
  Pallas kernels  17.9 us (33%)
  waiting for transfers between devices  13.8 us (26%)
  other arithmetic  1.12 us (2%)
    ppermute x4, waiting for transfers between devices, swap_b(): lax.ppermute(cells, 'gy', [(j, (j + (1 if j % 2 else -1)) % count) for j...  13.7 us
    ppermute x4, starting transfers between devices, shift(): lax.ppermute(cells, axis, [(i, (i + step) % count) for i in range(count)])  11.7 us
    ppermute x4, starting transfers between devices, swap_b(): lax.ppermute(cells, 'gy', [(j, (j + (1 if j % 2 else -1)) % count) for j...  8.78 us
    pallas_call x1, Pallas kernels, build(): pl.pallas_call(build_kernel, out_shape=[jax.ShapeDtypeStruct(s, jnp.bfloa...  5.3 us
    pallas_call x1, Pallas kernels, near(): pl.pallas_call(near_kernel, out_shape=jax.ShapeDtypeStruct((DENSITIES * C...  4.11 us
    pallas_call x1, Pallas kernels, middle(): pl.pallas_call(middle_kernel, out_shape=[edge, edge, back, back], in_spec...  3.91 us
    pallas_call x2, Pallas kernels, spread(): pl.pallas_call(functools.partial(spread_kernel, group), out_shape=[jax.Sh...  3.35 us
    pallas_call x1, Pallas kernels, cut(): pl.pallas_call(cut_kernel, out_shape=[jax.ShapeDtypeStruct(s + (depth,),...  1.19 us
  transfers between devices with their start and end apart: 12, of which 5 were waited for; matrix products, arithmetic and copies ran while one was open for 1% of the time, Pallas kernels for 24%

profile of v8, /device:TPU:4, one launch (start us, length us, event | category | flops | bytes accessed | tf_op | source)
XLA Modules:
  0.0 53.6 jit_solution(14382522680118012268)
XLA Ops:
  0.0 1.2 %cut.1 = (f32[8,16,512]{2,1,0:T(8,128)S(1)}, f32[8,16,512]{2,1,0:T(8,128)S(1)}, f32[16,8,512]{2,1,0:T(8,128)S(1)}, f32[16,8,512]{2,1,0:T(8,128)S(1)}, f32[16,16,512]{2,1,0:T(8,128)S(1)}) custom-call(f32[16,16,512]{2,1,0:T(8,128)} %tangent.1), custom_call_target="tpu_custom_call" | custom-call | bytes 3145728 | tf_op jit(solution)/shard_map/cut/pallas_call | solution.py:314
  1.2 2.0 %collective-permute-start = (f32[8,16,512]{2,1,0:T(8,128)S(1)}, f32[8,16,512]{2,1,0:T(8,128)S(1)}, u32[]{:S(2)}, u32[]{:S(2)}) collective-permute-start(f32[8,16,512]{2,1,0:T(8,128)S(1)} %get-tuple-element.36), channel_id=1, source_target_pairs={{0,16},{16,32},{32,48},{48,64},{64,80},{80,96},{96,112},{112,128},... | collective-permute-start | bytes 786440 | tf_op jit(solution)/shard_map/ppermute | solution.py:328
  3.2 4.0 %collective-permute-start.1 = (f32[8,16,512]{2,1,0:T(8,128)S(1)}, f32[8,16,512]{2,1,0:T(8,128)S(1)}, u32[]{:S(2)}, u32[]{:S(2)}) collective-permute-start(f32[8,16,512]{2,1,0:T(8,128)S(1)} %get-tuple-element.37), channel_id=1, source_target_pairs={{0,240},{16,0},{32,16},{48,32},{64,48},{80,64},{96,80},{112,96},{1... | collective-permute-start | bytes 786440 | tf_op jit(solution)/shard_map/ppermute | solution.py:328
  7.2 3.7 %collective-permute-start.3 = (f32[16,8,512]{2,1,0:T(8,128)S(1)}, f32[16,8,512]{2,1,0:T(8,128)S(1)}, u32[]{:S(2)}, u32[]{:S(2)}) collective-permute-start(f32[16,8,512]{2,1,0:T(8,128)S(1)} %get-tuple-element.38), channel_id=1, source_target_pairs={{0,15},{1,2},{2,1},{3,4},{4,3},{5,6},{6,5},{7,8},{8,7},{9,10},{10,... | collective-permute-start | bytes 786440 | tf_op jit(solution)/shard_map/ppermute | solution.py:338
  10.9 0.0 collective-permute-start.2
  10.9 5.3 %build.1 = (bf16[1280,768]{1,0:T(8,128)(2,1)S(1)}, bf16[1280,768]{1,0:T(8,128)(2,1)S(1)}, bf16[1280,256]{1,0:T(8,128)(2,1)S(1)}, bf16[1280,256]{1,0:T(8,128)(2,1...) custom-call(f32[5,17]{1,0:T(8,128)} %kr_hbm.1, ...), custom_call_target="tpu_custom_call" | custom-call | flops 31457280 | bytes 16777216 | tf_op jit(solution)/shard_map/build/pallas_call | solution.py:138
  16.2 0.0 collective-permute-done.north
  16.2 0.0 collective-permute-done.1.south
  16.3 0.0 slice-start
  16.3 1.0 %collective-permute-start.5 = (f32[16,8,512]{2,1,0:T(8,128)S(1)}, f32[16,8,512]{2,1,0:T(8,128)S(1)}, u32[]{:S(2)}, u32[]{:S(2)}) collective-permute-start(f32[16,8,512]{2,1,0:T(8,128)S(1)} %get-tuple-element.64), channel_id=1, source_target_pairs={{0,15},{1,2},{2,1},{3,4},{4,3},{5,6},{6,5},{7,8},{8,7},{9,10},{10,... | collective-permute-start | bytes 786440 | tf_op jit(solution)/shard_map/ppermute | solution.py:338
  17.4 0.0 collective-permute-start.4
  17.4 0.0 collective-permute-done.2.side_a
  17.4 4.7 %collective-permute-done.3.side_b = f32[16,8,512]{2,1,0:T(8,128)S(1)} collective-permute-done((f32[16,8,512]{2,1,0:T(8,128)S(1)}, f32[16,8,512]{2,1,0:T(8,128)S(1)}, u32[]{:S(2)}, u32[]{:S(2)}) %collective-permute-start.3) | collective-permute-done | bytes 262176 | tf_op jit(solution)/shard_map/ppermute | solution.py:338
  22.0 0.0 slice-start.1
  22.0 4.1 %near.1.partial = f32[1280,512]{1,0:T(8,128)S(1)} custom-call(f32[16,16,512]{2,1,0:T(8,128)S(1)} %get-tuple-element.35.own, f32[8,16,512]{2,1,0:T(8,128)S(1)} %collective-permute-done.north, f32[8,16,512]{2,1,0:T(8,128)S(1)} %collective-permute-done.1.south, f32[16,8,512]{2,1,0:T(8,128)S(1)} %collective-permute-done.2.side_a, ...), custom_call_target="tpu_custom_call" | custom-call | flops 3019898880 | bytes 10485760 | tf_op jit(solution)/shard_map/near/pallas_call | solution.py:189
  26.2 0.0 collective-permute-done.4.corner_a
  26.2 1.5 %collective-permute-done.5.corner_b = f32[16,8,512]{2,1,0:T(8,128)S(1)} collective-permute-done((f32[16,8,512]{2,1,0:T(8,128)S(1)}, f32[16,8,512]{2,1,0:T(8,128)S(1)}, u32[]{:S(2)}, u32[]{:S(2)}) %collective-permute-start.5) | collective-permute-done | bytes 262176 | tf_op jit(solution)/shard_map/ppermute | solution.py:338
  27.7 0.0 slice-done
  27.7 0.0 slice-done.1
  27.7 3.9 %middle.1 = (f32[16,8,512]{2,1,0:T(8,128)S(1)}, f32[16,8,512]{2,1,0:T(8,128)S(1)}, bf16[1280,512]{1,0:T(8,128)(2,1)S(1)}, bf16[1280,512]{1,0:T(8,128)(2,1)S(1)}) custom-call(f32[1280,512]{1,0:T(8,128)S(1)} %near.1.partial, f32[16,8,512]{2,1,0:T(8,128)S(1)} %collective-permute-done.4.corner_a, f32[16,8,512]{2,1,0:T(8,128)S(1)} %collective-permute-done.5.corner_b, ...), custom_call_target="tpu_custom_call" | custom-call | flops 3355443200 | bytes 16777216 | tf_op jit(solution)/shard_map/middle/pallas_call | solution.py:245
  31.6 0.1 collective-permute-start.7
  31.7 1.0 %collective-permute-start.6 = (f32[16,8,512]{2,1,0:T(8,128)S(1)}, f32[16,8,512]{2,1,0:T(8,128)S(1)}, u32[]{:S(2)}, u32[]{:S(2)}) collective-permute-start(f32[16,8,512]{2,1,0:T(8,128)S(1)} %get-tuple-element.52), channel_id=1, source_target_pairs={{0,15},{1,2},{2,1},{3,4},{4,3},{5,6},{6,5},{7,8},{8,7},{9,10},{10,... | collective-permute-start | bytes 786440 | tf_op jit(solution)/shard_map/ppermute | solution.py:338
  32.7 2.2 %spread.2 = (f32[8,16,512]{2,1,0:T(8,128)S(1)}, f32[8,16,512]{2,1,0:T(8,128)S(1)}, f32[16,8,512]{2,1,0:T(8,128)S(1)}, f32[16,8,512]{2,1,0:T(8,128)S(1)}) custom-call(bf16[1024,1280]{1,0:T(8,128)(2,1)S(1)} %get-tuple-element.33.th, bf16[1024,1280]{1,0:T(8,128)(2,1)S(1)} %get-tuple-element.34.tl, bf16[1280,512]{1,0:T(8,128)(2,1)S(1)} %get-tuple-element.55.bh, ...), custom_call_target="tpu_custom_call" | custom-call | flops 2013265920 | bytes 6291456 | tf_op jit(solution)/shard_map/spread/pallas_call | solution.py:276
  34.9 3.0 %collective-permute-start.8 = (f32[16,8,512]{2,1,0:T(8,128)S(1)}, f32[16,8,512]{2,1,0:T(8,128)S(1)}, u32[]{:S(2)}, u32[]{:S(2)}) collective-permute-start(f32[16,8,512]{2,1,0:T(8,128)S(1)} %get-tuple-element.57), channel_id=1, source_target_pairs={{0,15},{1,2},{2,1},{3,4},{4,3},{5,6},{6,5},{7,8},{8,7},{9,10},{10,... | collective-permute-start | bytes 786440 | tf_op jit(solution)/shard_map/ppermute | solution.py:338
  37.9 0.0 collective-permute-start.9
  37.9 0.0 collective-permute-done.7
  37.9 4.6 %collective-permute-done.6 = f32[16,8,512]{2,1,0:T(8,128)S(1)} collective-permute-done((f32[16,8,512]{2,1,0:T(8,128)S(1)}, f32[16,8,512]{2,1,0:T(8,128)S(1)}, u32[]{:S(2)}, u32[]{:S(2)}) %collective-permute-start.6) | collective-permute-done | bytes 262176 | tf_op jit(solution)/shard_map/ppermute | solution.py:338
  42.5 0.1 maximum_add_fusion
  42.7 0.1 collective-permute-start.10
  42.8 5.6 %collective-permute-start.11 = (f32[8,16,512]{2,1,0:T(8,128)S(1)}, f32[8,16,512]{2,1,0:T(8,128)S(1)}, u32[]{:S(2)}, u32[]{:S(2)}) collective-permute-start(f32[8,16,512]{2,1,0:T(8,128)S(1)} %get-tuple-element.60), channel_id=1, source_target_pairs={{0,240},{16,0},{32,16},{48,32},{64,48},{80,64},{96,80},{112,96},{1... | collective-permute-start | bytes 786440 | tf_op jit(solution)/shard_map/ppermute | solution.py:328
  48.4 1.2 %spread.3 = f32[16,16,512]{2,1,0:T(8,128)S(1)} custom-call(bf16[1024,1280]{1,0:T(8,128)(2,1)S(1)} %get-tuple-element.33.th, bf16[1024,1280]{1,0:T(8,128)(2,1)S(1)} %get-tuple-element.34.tl, bf16[1280,512]{1,0:T(8,128)(2,1)S(1)} %get-tuple-element.55.bh, bf16[1280,512]{1,0:T(8,128)(2,1)S(1)} %get-tuple-element.56.bl), custom_call_target="tpu_custom_call" | custom-call | flops 1006632960 | bytes 6291456 | tf_op jit(solution)/shard_map/spread/pallas_call | solution.py:276
  49.6 0.0 collective-permute-done.9
  49.6 2.9 %collective-permute-done.8 = f32[16,8,512]{2,1,0:T(8,128)S(1)} collective-permute-done((f32[16,8,512]{2,1,0:T(8,128)S(1)}, f32[16,8,512]{2,1,0:T(8,128)S(1)}, u32[]{:S(2)}, u32[]{:S(2)}) %collective-permute-start.8) | collective-permute-done | bytes 262176 | tf_op jit(solution)/shard_map/ppermute | solution.py:338
  52.5 0.1 fusion
  52.6 0.0 collective-permute-done.11
  52.6 0.2 collective-permute-done.10
  52.8 0.9 %maximum_add_fusion.1 = f32[16,16,512]{2,1,0:T(8,128)} fusion(f32[16,16,512]{2,1,0:T(8,128)S(1)} %fusion, f32[8,16,512]{2,1,0:T(8,128)S(1)} %collective-permute-done.11, f32[8,16,512]{2,1,0:T(8,128)S(1)} %collective-permute-done.10), kind=kLoop, calls=%fused_computation.4 | loop fusion | flops 262144 | bytes 1572864 | tf_op jit(solution)/shard_map/add | solution.py:387
  (5 shorter events, 0.1 us)
Async XLA Ops:
  1.2 15.0 %collective-permute-start = (f32[8,16,512]{2,1,0:T(8,128)S(1)}, f32[8,16,512]{2,1,0:T(8,128)S(1)}, u32[]{:S(2)}, u32[]{:S(2)}) collective-permute-start(f32[8,16,512]{2,1,0:T(8,128)S(1)} %get-tuple-element.36), channel_id=1, source_target_pairs={{0,16},{16,32},{32,48},{48,64},{64,80},{80,96},{96,112},{112,128},... | collective-permute-start | bytes 786440 | tf_op jit(solution)/shard_map/ppermute | solution.py:328
  3.2 13.0 %collective-permute-start.1 = (f32[8,16,512]{2,1,0:T(8,128)S(1)}, f32[8,16,512]{2,1,0:T(8,128)S(1)}, u32[]{:S(2)}, u32[]{:S(2)}) collective-permute-start(f32[8,16,512]{2,1,0:T(8,128)S(1)} %get-tuple-element.37), channel_id=1, source_target_pairs={{0,240},{16,0},{32,16},{48,32},{64,48},{80,64},{96,80},{112,96},{1... | collective-permute-start | bytes 786440 | tf_op jit(solution)/shard_map/ppermute | solution.py:328
  7.2 14.9 %collective-permute-start.3 = (f32[16,8,512]{2,1,0:T(8,128)S(1)}, f32[16,8,512]{2,1,0:T(8,128)S(1)}, u32[]{:S(2)}, u32[]{:S(2)}) collective-permute-start(f32[16,8,512]{2,1,0:T(8,128)S(1)} %get-tuple-element.38), channel_id=1, source_target_pairs={{0,15},{1,2},{2,1},{3,4},{4,3},{5,6},{6,5},{7,8},{8,7},{9,10},{10,... | collective-permute-start | bytes 786440 | tf_op jit(solution)/shard_map/ppermute | solution.py:338
  10.9 6.5 %collective-permute-start.2 = (f32[16,8,512]{2,1,0:T(8,128)S(1)}, f32[16,8,512]{2,1,0:T(8,128)S(1)}, u32[]{:S(2)}, u32[]{:S(2)}) collective-permute-start(f32[16,8,512]{2,1,0:T(8,128)S(1)} %get-tuple-element.40), channel_id=1, source_target_pairs={{0,1},{1,0},{2,3},{3,2},{4,5},{5,4},{6,7},{7,6},{8,9},{9,8},{10,11... | collective-permute-start | bytes 786440 | tf_op jit(solution)/shard_map/ppermute | solution.py:333
  16.3 11.4 %slice-start = ((s8[6553600]{0:T(1024)(128)(4,1)}), s8[4194304]{0:T(1024)(128)(4,1)S(1)}, s32[]{:S(2)}) async-start(s8[6553600]{0:T(1024)(128)(4,1)} %bitcast), calls=%async_computation | async-start | bytes 8388608
  16.3 11.3 %collective-permute-start.5 = (f32[16,8,512]{2,1,0:T(8,128)S(1)}, f32[16,8,512]{2,1,0:T(8,128)S(1)}, u32[]{:S(2)}, u32[]{:S(2)}) collective-permute-start(f32[16,8,512]{2,1,0:T(8,128)S(1)} %get-tuple-element.64), channel_id=1, source_target_pairs={{0,15},{1,2},{2,1},{3,4},{4,3},{5,6},{6,5},{7,8},{8,7},{9,10},{10,... | collective-permute-start | bytes 786440 | tf_op jit(solution)/shard_map/ppermute | solution.py:338
  17.4 8.8 %collective-permute-start.4 = (f32[16,8,512]{2,1,0:T(8,128)S(1)}, f32[16,8,512]{2,1,0:T(8,128)S(1)}, u32[]{:S(2)}, u32[]{:S(2)}) collective-permute-start(f32[16,8,512]{2,1,0:T(8,128)S(1)} %get-tuple-element.43), channel_id=1, source_target_pairs={{0,1},{1,0},{2,3},{3,2},{4,5},{5,4},{6,7},{7,6},{8,9},{9,8},{10,11... | collective-permute-start | bytes 786440 | tf_op jit(solution)/shard_map/ppermute | solution.py:333
  22.0 5.6 %slice-start.1 = ((s8[6553600]{0:T(1024)(128)(4,1)}), s8[2359296]{0:T(1024)(128)(4,1)S(1)}, s32[]{:S(2)}) async-start(s8[6553600]{0:T(1024)(128)(4,1)} %bitcast), calls=%async_computation.1 | async-start | bytes 4718592
  31.6 6.3 %collective-permute-start.7 = (f32[16,8,512]{2,1,0:T(8,128)S(1)}, f32[16,8,512]{2,1,0:T(8,128)S(1)}, u32[]{:S(2)}, u32[]{:S(2)}) collective-permute-start(f32[16,8,512]{2,1,0:T(8,128)S(1)} %get-tuple-element.54), channel_id=1, source_target_pairs={{0,1},{1,0},{2,3},{3,2},{4,5},{5,4},{6,7},{7,6},{8,9},{9,8},{10,11... | collective-permute-start | bytes 786440 | tf_op jit(solution)/shard_map/ppermute | solution.py:333
  31.7 10.8 %collective-permute-start.6 = (f32[16,8,512]{2,1,0:T(8,128)S(1)}, f32[16,8,512]{2,1,0:T(8,128)S(1)}, u32[]{:S(2)}, u32[]{:S(2)}) collective-permute-start(f32[16,8,512]{2,1,0:T(8,128)S(1)} %get-tuple-element.52), channel_id=1, source_target_pairs={{0,15},{1,2},{2,1},{3,4},{4,3},{5,6},{6,5},{7,8},{8,7},{9,10},{10,... | collective-permute-start | bytes 786440 | tf_op jit(solution)/shard_map/ppermute | solution.py:338
  34.9 17.6 %collective-permute-start.8 = (f32[16,8,512]{2,1,0:T(8,128)S(1)}, f32[16,8,512]{2,1,0:T(8,128)S(1)}, u32[]{:S(2)}, u32[]{:S(2)}) collective-permute-start(f32[16,8,512]{2,1,0:T(8,128)S(1)} %get-tuple-element.57), channel_id=1, source_target_pairs={{0,15},{1,2},{2,1},{3,4},{4,3},{5,6},{6,5},{7,8},{8,7},{9,10},{10,... | collective-permute-start | bytes 786440 | tf_op jit(solution)/shard_map/ppermute | solution.py:338
  37.9 11.7 %collective-permute-start.9 = (f32[16,8,512]{2,1,0:T(8,128)S(1)}, f32[16,8,512]{2,1,0:T(8,128)S(1)}, u32[]{:S(2)}, u32[]{:S(2)}) collective-permute-start(f32[16,8,512]{2,1,0:T(8,128)S(1)} %get-tuple-element.59), channel_id=1, source_target_pairs={{0,1},{1,0},{2,3},{3,2},{4,5},{5,4},{6,7},{7,6},{8,9},{9,8},{10,11... | collective-permute-start | bytes 786440 | tf_op jit(solution)/shard_map/ppermute | solution.py:333
  42.7 10.1 %collective-permute-start.10 = (f32[8,16,512]{2,1,0:T(8,128)S(1)}, f32[8,16,512]{2,1,0:T(8,128)S(1)}, u32[]{:S(2)}, u32[]{:S(2)}) collective-permute-start(f32[8,16,512]{2,1,0:T(8,128)S(1)} %get-tuple-element.61), channel_id=1, source_target_pairs={{0,16},{16,32},{32,48},{48,64},{64,80},{80,96},{96,112},{112,128},... | collective-permute-start | bytes 786440 | tf_op jit(solution)/shard_map/ppermute | solution.py:328
  42.8 9.8 %collective-permute-start.11 = (f32[8,16,512]{2,1,0:T(8,128)S(1)}, f32[8,16,512]{2,1,0:T(8,128)S(1)}, u32[]{:S(2)}, u32[]{:S(2)}) collective-permute-start(f32[8,16,512]{2,1,0:T(8,128)S(1)} %get-tuple-element.60), channel_id=1, source_target_pairs={{0,240},{16,0},{32,16},{48,32},{64,48},{80,64},{96,80},{112,96},{1... | collective-permute-start | bytes 786440 | tf_op jit(solution)/shard_map/ppermute | solution.py:328

commit v9 on v8

--- a/solution.py
+++ b/solution.py
@@ -375,7 +375,9 @@
     )
     edge_from_b, edge_from_a = swapped(edge_b, edge_a)
 
-    around = jnp.concatenate([above, below], 0) + joined(from_a, from_b)
+    blank = jnp.zeros_like(from_a)
+    around = jnp.concatenate([above, below], 0) + joined(blank, from_b)
+    around = lax.optimization_barrier(around) + joined(from_a, blank)
     above, below = around[:reach], around[reach:]
     side_from_n = shift(below, "gx", 1)
     above, below = lax.optimization_barrier((above, below))

time: 53.8 us -> 53.1 us (0.987)
  waiting for transfers between devices: 13.8 us -> 13.1 us
  transfers between devices with their start and end apart: 12 -> 12, of which waited for: 5 -> 4; matrix products, arithmetic and copies ran while one was open for 1% -> 1% of each run, Pallas kernels for 24% -> 24%
where the time goes in v9:
time: 53.1 us; the launch traced here: 52.9 us
  starting transfers between devices  20.4 us (38%)
  Pallas kernels  17.9 us (34%)
  waiting for transfers between devices  13.1 us (25%)
  other arithmetic  1.17 us (2%)
    ppermute x4, waiting for transfers between devices, swap_b(): lax.ppermute(cells, 'gy', [(j, (j + (1 if j % 2 else -1)) % count) for j...  13.1 us
    ppermute x4, starting transfers between devices, shift(): lax.ppermute(cells, axis, [(i, (i + step) % count) for i in range(count)])  11.7 us
    ppermute x4, starting transfers between devices, swap_b(): lax.ppermute(cells, 'gy', [(j, (j + (1 if j % 2 else -1)) % count) for j...  8.67 us
    pallas_call x1, Pallas kernels, build(): pl.pallas_call(build_kernel, out_shape=[jax.ShapeDtypeStruct(s, jnp.bfloa...  5.3 us
    pallas_call x1, Pallas kernels, near(): pl.pallas_call(near_kernel, out_shape=jax.ShapeDtypeStruct((DENSITIES * C...  4.11 us
    pallas_call x1, Pallas kernels, middle(): pl.pallas_call(middle_kernel, out_shape=[edge, edge, back, back], in_spec...  3.91 us
    pallas_call x2, Pallas kernels, spread(): pl.pallas_call(functools.partial(spread_kernel, group), out_shape=[jax.Sh...  3.35 us
    pallas_call x1, Pallas kernels, cut(): pl.pallas_call(cut_kernel, out_shape=[jax.ShapeDtypeStruct(s + (depth,),...  1.19 us
  transfers between devices with their start and end apart: 12, of which 4 were waited for; matrix products, arithmetic and copies ran while one was open for 1% of the time, Pallas kernels for 24%

profile of v9, /device:TPU:4, one launch (start us, length us, event | category | flops | bytes accessed | tf_op | source)
XLA Modules:
  0.0 52.9 jit_solution(15623635414616765737)
XLA Ops:
  0.0 1.2 %cut.1 = (f32[8,16,512]{2,1,0:T(8,128)S(1)}, f32[8,16,512]{2,1,0:T(8,128)S(1)}, f32[16,8,512]{2,1,0:T(8,128)S(1)}, f32[16,8,512]{2,1,0:T(8,128)S(1)}, f32[16,16,512]{2,1,0:T(8,128)S(1)}) custom-call(f32[16,16,512]{2,1,0:T(8,128)} %tangent.1), custom_call_target="tpu_custom_call" | custom-call | bytes 3145728 | tf_op jit(solution)/shard_map/cut/pallas_call | solution.py:314
  1.2 2.0 %collective-permute-start = (f32[8,16,512]{2,1,0:T(8,128)S(1)}, f32[8,16,512]{2,1,0:T(8,128)S(1)}, u32[]{:S(2)}, u32[]{:S(2)}) collective-permute-start(f32[8,16,512]{2,1,0:T(8,128)S(1)} %get-tuple-element.36), channel_id=1, source_target_pairs={{0,16},{16,32},{32,48},{48,64},{64,80},{80,96},{96,112},{112,128},... | collective-permute-start | bytes 786440 | tf_op jit(solution)/shard_map/ppermute | solution.py:328
  3.2 4.0 %collective-permute-start.1 = (f32[8,16,512]{2,1,0:T(8,128)S(1)}, f32[8,16,512]{2,1,0:T(8,128)S(1)}, u32[]{:S(2)}, u32[]{:S(2)}) collective-permute-start(f32[8,16,512]{2,1,0:T(8,128)S(1)} %get-tuple-element.37), channel_id=1, source_target_pairs={{0,240},{16,0},{32,16},{48,32},{64,48},{80,64},{96,80},{112,96},{1... | collective-permute-start | bytes 786440 | tf_op jit(solution)/shard_map/ppermute | solution.py:328
  7.2 3.7 %collective-permute-start.3 = (f32[16,8,512]{2,1,0:T(8,128)S(1)}, f32[16,8,512]{2,1,0:T(8,128)S(1)}, u32[]{:S(2)}, u32[]{:S(2)}) collective-permute-start(f32[16,8,512]{2,1,0:T(8,128)S(1)} %get-tuple-element.38), channel_id=1, source_target_pairs={{0,15},{1,2},{2,1},{3,4},{4,3},{5,6},{6,5},{7,8},{8,7},{9,10},{10,... | collective-permute-start | bytes 786440 | tf_op jit(solution)/shard_map/ppermute | solution.py:338
  10.9 0.0 collective-permute-start.2
  10.9 5.3 %build.1 = (bf16[1280,768]{1,0:T(8,128)(2,1)S(1)}, bf16[1280,768]{1,0:T(8,128)(2,1)S(1)}, bf16[1280,256]{1,0:T(8,128)(2,1)S(1)}, bf16[1280,256]{1,0:T(8,128)(2,1...) custom-call(f32[5,17]{1,0:T(8,128)} %kr_hbm.1, ...), custom_call_target="tpu_custom_call" | custom-call | flops 31457280 | bytes 16777216 | tf_op jit(solution)/shard_map/build/pallas_call | solution.py:138
  16.2 0.0 collective-permute-done.north
  16.2 0.0 collective-permute-done.1.south
  16.3 0.0 slice-start
  16.3 1.0 %collective-permute-start.5 = (f32[16,8,512]{2,1,0:T(8,128)S(1)}, f32[16,8,512]{2,1,0:T(8,128)S(1)}, u32[]{:S(2)}, u32[]{:S(2)}) collective-permute-start(f32[16,8,512]{2,1,0:T(8,128)S(1)} %get-tuple-element.64), channel_id=1, source_target_pairs={{0,15},{1,2},{2,1},{3,4},{4,3},{5,6},{6,5},{7,8},{8,7},{9,10},{10,... | collective-permute-start | bytes 786440 | tf_op jit(solution)/shard_map/ppermute | solution.py:338
  17.4 0.0 collective-permute-start.4
  17.4 0.0 collective-permute-done.2.side_a
  17.4 4.7 %collective-permute-done.3.side_b = f32[16,8,512]{2,1,0:T(8,128)S(1)} collective-permute-done((f32[16,8,512]{2,1,0:T(8,128)S(1)}, f32[16,8,512]{2,1,0:T(8,128)S(1)}, u32[]{:S(2)}, u32[]{:S(2)}) %collective-permute-start.3) | collective-permute-done | bytes 262176 | tf_op jit(solution)/shard_map/ppermute | solution.py:338
  22.0 0.0 slice-start.1
  22.0 4.1 %near.1.partial = f32[1280,512]{1,0:T(8,128)S(1)} custom-call(f32[16,16,512]{2,1,0:T(8,128)S(1)} %get-tuple-element.35.own, f32[8,16,512]{2,1,0:T(8,128)S(1)} %collective-permute-done.north, f32[8,16,512]{2,1,0:T(8,128)S(1)} %collective-permute-done.1.south, f32[16,8,512]{2,1,0:T(8,128)S(1)} %collective-permute-done.2.side_a, ...), custom_call_target="tpu_custom_call" | custom-call | flops 3019898880 | bytes 10485760 | tf_op jit(solution)/shard_map/near/pallas_call | solution.py:189
  26.2 0.0 collective-permute-done.4.corner_a
  26.2 1.5 %collective-permute-done.5.corner_b = f32[16,8,512]{2,1,0:T(8,128)S(1)} collective-permute-done((f32[16,8,512]{2,1,0:T(8,128)S(1)}, f32[16,8,512]{2,1,0:T(8,128)S(1)}, u32[]{:S(2)}, u32[]{:S(2)}) %collective-permute-start.5) | collective-permute-done | bytes 262176 | tf_op jit(solution)/shard_map/ppermute | solution.py:338
  27.7 0.0 slice-done
  27.7 0.0 slice-done.1
  27.7 3.9 %middle.1 = (f32[16,8,512]{2,1,0:T(8,128)S(1)}, f32[16,8,512]{2,1,0:T(8,128)S(1)}, bf16[1280,512]{1,0:T(8,128)(2,1)S(1)}, bf16[1280,512]{1,0:T(8,128)(2,1)S(1)}) custom-call(f32[1280,512]{1,0:T(8,128)S(1)} %near.1.partial, f32[16,8,512]{2,1,0:T(8,128)S(1)} %collective-permute-done.4.corner_a, f32[16,8,512]{2,1,0:T(8,128)S(1)} %collective-permute-done.5.corner_b, ...), custom_call_target="tpu_custom_call" | custom-call | flops 3355443200 | bytes 16777216 | tf_op jit(solution)/shard_map/middle/pallas_call | solution.py:245
  31.6 0.1 collective-permute-start.6
  31.7 0.1 collective-permute-start.7
  31.8 2.2 %spread.2 = (f32[8,16,512]{2,1,0:T(8,128)S(1)}, f32[8,16,512]{2,1,0:T(8,128)S(1)}, f32[16,8,512]{2,1,0:T(8,128)S(1)}, f32[16,8,512]{2,1,0:T(8,128)S(1)}) custom-call(bf16[1024,1280]{1,0:T(8,128)(2,1)S(1)} %get-tuple-element.33.th, bf16[1024,1280]{1,0:T(8,128)(2,1)S(1)} %get-tuple-element.34.tl, bf16[1280,512]{1,0:T(8,128)(2,1)S(1)} %get-tuple-element.55.bh, ...), custom_call_target="tpu_custom_call" | custom-call | flops 2013265920 | bytes 6291456 | tf_op jit(solution)/shard_map/spread/pallas_call | solution.py:276
  34.0 3.8 %collective-permute-start.8 = (f32[16,8,512]{2,1,0:T(8,128)S(1)}, f32[16,8,512]{2,1,0:T(8,128)S(1)}, u32[]{:S(2)}, u32[]{:S(2)}) collective-permute-start(f32[16,8,512]{2,1,0:T(8,128)S(1)} %get-tuple-element.57), channel_id=1, source_target_pairs={{0,15},{1,2},{2,1},{3,4},{4,3},{5,6},{6,5},{7,8},{8,7},{9,10},{10,... | collective-permute-start | bytes 786440 | tf_op jit(solution)/shard_map/ppermute | solution.py:338
  37.8 0.0 collective-permute-start.9
  37.8 3.7 %collective-permute-done.6 = f32[16,8,512]{2,1,0:T(8,128)S(1)} collective-permute-done((f32[16,8,512]{2,1,0:T(8,128)S(1)}, f32[16,8,512]{2,1,0:T(8,128)S(1)}, u32[]{:S(2)}, u32[]{:S(2)}) %collective-permute-start.6) | collective-permute-done | bytes 262176 | tf_op jit(solution)/shard_map/ppermute | solution.py:338
  41.5 0.1 maximum_add_fusion
  41.6 0.0 collective-permute-done.7
  41.6 0.1 select_add_fusion
  41.7 0.1 collective-permute-start.10
  41.8 5.6 %collective-permute-start.11 = (f32[8,16,512]{2,1,0:T(8,128)S(1)}, f32[8,16,512]{2,1,0:T(8,128)S(1)}, u32[]{:S(2)}, u32[]{:S(2)}) collective-permute-start(f32[8,16,512]{2,1,0:T(8,128)S(1)} %get-tuple-element.60), channel_id=1, source_target_pairs={{0,240},{16,0},{32,16},{48,32},{64,48},{80,64},{96,80},{112,96},{1... | collective-permute-start | bytes 786440 | tf_op jit(solution)/shard_map/ppermute | solution.py:328
  47.4 1.2 %spread.3 = f32[16,16,512]{2,1,0:T(8,128)S(1)} custom-call(bf16[1024,1280]{1,0:T(8,128)(2,1)S(1)} %get-tuple-element.33.th, bf16[1024,1280]{1,0:T(8,128)(2,1)S(1)} %get-tuple-element.34.tl, bf16[1280,512]{1,0:T(8,128)(2,1)S(1)} %get-tuple-element.55.bh, bf16[1280,512]{1,0:T(8,128)(2,1)S(1)} %get-tuple-element.56.bl), custom_call_target="tpu_custom_call" | custom-call | flops 1006632960 | bytes 6291456 | tf_op jit(solution)/shard_map/spread/pallas_call | solution.py:276
  48.6 0.0 collective-permute-done.9
  48.6 3.3 %collective-permute-done.8 = f32[16,8,512]{2,1,0:T(8,128)S(1)} collective-permute-done((f32[16,8,512]{2,1,0:T(8,128)S(1)}, f32[16,8,512]{2,1,0:T(8,128)S(1)}, u32[]{:S(2)}, u32[]{:S(2)}) %collective-permute-start.8) | collective-permute-done | bytes 262176 | tf_op jit(solution)/shard_map/ppermute | solution.py:338
  51.9 0.1 fusion
  52.0 0.0 collective-permute-done.11
  52.0 0.0 collective-permute-done.10
  52.0 0.9 %maximum_add_fusion.1 = f32[16,16,512]{2,1,0:T(8,128)} fusion(f32[16,16,512]{2,1,0:T(8,128)S(1)} %fusion, f32[8,16,512]{2,1,0:T(8,128)S(1)} %collective-permute-done.11, f32[8,16,512]{2,1,0:T(8,128)S(1)} %collective-permute-done.10), kind=kLoop, calls=%fused_computation.3 | loop fusion | flops 262144 | bytes 1572864 | tf_op jit(solution)/shard_map/add | solution.py:389
  (5 shorter events, 0.1 us)
Async XLA Ops:
  1.2 15.0 %collective-permute-start = (f32[8,16,512]{2,1,0:T(8,128)S(1)}, f32[8,16,512]{2,1,0:T(8,128)S(1)}, u32[]{:S(2)}, u32[]{:S(2)}) collective-permute-start(f32[8,16,512]{2,1,0:T(8,128)S(1)} %get-tuple-element.36), channel_id=1, source_target_pairs={{0,16},{16,32},{32,48},{48,64},{64,80},{80,96},{96,112},{112,128},... | collective-permute-start | bytes 786440 | tf_op jit(solution)/shard_map/ppermute | solution.py:328
  3.2 13.0 %collective-permute-start.1 = (f32[8,16,512]{2,1,0:T(8,128)S(1)}, f32[8,16,512]{2,1,0:T(8,128)S(1)}, u32[]{:S(2)}, u32[]{:S(2)}) collective-permute-start(f32[8,16,512]{2,1,0:T(8,128)S(1)} %get-tuple-element.37), channel_id=1, source_target_pairs={{0,240},{16,0},{32,16},{48,32},{64,48},{80,64},{96,80},{112,96},{1... | collective-permute-start | bytes 786440 | tf_op jit(solution)/shard_map/ppermute | solution.py:328
  7.2 14.9 %collective-permute-start.3 = (f32[16,8,512]{2,1,0:T(8,128)S(1)}, f32[16,8,512]{2,1,0:T(8,128)S(1)}, u32[]{:S(2)}, u32[]{:S(2)}) collective-permute-start(f32[16,8,512]{2,1,0:T(8,128)S(1)} %get-tuple-element.38), channel_id=1, source_target_pairs={{0,15},{1,2},{2,1},{3,4},{4,3},{5,6},{6,5},{7,8},{8,7},{9,10},{10,... | collective-permute-start | bytes 786440 | tf_op jit(solution)/shard_map/ppermute | solution.py:338
  10.9 6.5 %collective-permute-start.2 = (f32[16,8,512]{2,1,0:T(8,128)S(1)}, f32[16,8,512]{2,1,0:T(8,128)S(1)}, u32[]{:S(2)}, u32[]{:S(2)}) collective-permute-start(f32[16,8,512]{2,1,0:T(8,128)S(1)} %get-tuple-element.40), channel_id=1, source_target_pairs={{0,1},{1,0},{2,3},{3,2},{4,5},{5,4},{6,7},{7,6},{8,9},{9,8},{10,11... | collective-permute-start | bytes 786440 | tf_op jit(solution)/shard_map/ppermute | solution.py:333
  16.3 11.4 %slice-start = ((s8[6553600]{0:T(1024)(128)(4,1)}), s8[4194304]{0:T(1024)(128)(4,1)S(1)}, s32[]{:S(2)}) async-start(s8[6553600]{0:T(1024)(128)(4,1)} %bitcast), calls=%async_computation | async-start | bytes 8388608
  16.3 11.3 %collective-permute-start.5 = (f32[16,8,512]{2,1,0:T(8,128)S(1)}, f32[16,8,512]{2,1,0:T(8,128)S(1)}, u32[]{:S(2)}, u32[]{:S(2)}) collective-permute-start(f32[16,8,512]{2,1,0:T(8,128)S(1)} %get-tuple-element.64), channel_id=1, source_target_pairs={{0,15},{1,2},{2,1},{3,4},{4,3},{5,6},{6,5},{7,8},{8,7},{9,10},{10,... | collective-permute-start | bytes 786440 | tf_op jit(solution)/shard_map/ppermute | solution.py:338
  17.4 8.8 %collective-permute-start.4 = (f32[16,8,512]{2,1,0:T(8,128)S(1)}, f32[16,8,512]{2,1,0:T(8,128)S(1)}, u32[]{:S(2)}, u32[]{:S(2)}) collective-permute-start(f32[16,8,512]{2,1,0:T(8,128)S(1)} %get-tuple-element.43), channel_id=1, source_target_pairs={{0,1},{1,0},{2,3},{3,2},{4,5},{5,4},{6,7},{7,6},{8,9},{9,8},{10,11... | collective-permute-start | bytes 786440 | tf_op jit(solution)/shard_map/ppermute | solution.py:333
  22.0 5.6 %slice-start.1 = ((s8[6553600]{0:T(1024)(128)(4,1)}), s8[2359296]{0:T(1024)(128)(4,1)S(1)}, s32[]{:S(2)}) async-start(s8[6553600]{0:T(1024)(128)(4,1)} %bitcast), calls=%async_computation.1 | async-start | bytes 4718592
  31.6 9.9 %collective-permute-start.6 = (f32[16,8,512]{2,1,0:T(8,128)S(1)}, f32[16,8,512]{2,1,0:T(8,128)S(1)}, u32[]{:S(2)}, u32[]{:S(2)}) collective-permute-start(f32[16,8,512]{2,1,0:T(8,128)S(1)} %get-tuple-element.52), channel_id=1, source_target_pairs={{0,15},{1,2},{2,1},{3,4},{4,3},{5,6},{6,5},{7,8},{8,7},{9,10},{10,... | collective-permute-start | bytes 786440 | tf_op jit(solution)/shard_map/ppermute | solution.py:338
  31.7 9.9 %collective-permute-start.7 = (f32[16,8,512]{2,1,0:T(8,128)S(1)}, f32[16,8,512]{2,1,0:T(8,128)S(1)}, u32[]{:S(2)}, u32[]{:S(2)}) collective-permute-start(f32[16,8,512]{2,1,0:T(8,128)S(1)} %get-tuple-element.54), channel_id=1, source_target_pairs={{0,1},{1,0},{2,3},{3,2},{4,5},{5,4},{6,7},{7,6},{8,9},{9,8},{10,11... | collective-permute-start | bytes 786440 | tf_op jit(solution)/shard_map/ppermute | solution.py:333
  34.0 17.9 %collective-permute-start.8 = (f32[16,8,512]{2,1,0:T(8,128)S(1)}, f32[16,8,512]{2,1,0:T(8,128)S(1)}, u32[]{:S(2)}, u32[]{:S(2)}) collective-permute-start(f32[16,8,512]{2,1,0:T(8,128)S(1)} %get-tuple-element.57), channel_id=1, source_target_pairs={{0,15},{1,2},{2,1},{3,4},{4,3},{5,6},{6,5},{7,8},{8,7},{9,10},{10,... | collective-permute-start | bytes 786440 | tf_op jit(solution)/shard_map/ppermute | solution.py:338
  37.8 10.8 %collective-permute-start.9 = (f32[16,8,512]{2,1,0:T(8,128)S(1)}, f32[16,8,512]{2,1,0:T(8,128)S(1)}, u32[]{:S(2)}, u32[]{:S(2)}) collective-permute-start(f32[16,8,512]{2,1,0:T(8,128)S(1)} %get-tuple-element.59), channel_id=1, source_target_pairs={{0,1},{1,0},{2,3},{3,2},{4,5},{5,4},{6,7},{7,6},{8,9},{9,8},{10,11... | collective-permute-start | bytes 786440 | tf_op jit(solution)/shard_map/ppermute | solution.py:333
  41.7 10.3 %collective-permute-start.10 = (f32[8,16,512]{2,1,0:T(8,128)S(1)}, f32[8,16,512]{2,1,0:T(8,128)S(1)}, u32[]{:S(2)}, u32[]{:S(2)}) collective-permute-start(f32[8,16,512]{2,1,0:T(8,128)S(1)} %get-tuple-element.61), channel_id=1, source_target_pairs={{0,16},{16,32},{32,48},{48,64},{64,80},{80,96},{96,112},{112,128},... | collective-permute-start | bytes 786440 | tf_op jit(solution)/shard_map/ppermute | solution.py:328
  41.8 10.2 %collective-permute-start.11 = (f32[8,16,512]{2,1,0:T(8,128)S(1)}, f32[8,16,512]{2,1,0:T(8,128)S(1)}, u32[]{:S(2)}, u32[]{:S(2)}) collective-permute-start(f32[8,16,512]{2,1,0:T(8,128)S(1)} %get-tuple-element.60), channel_id=1, source_target_pairs={{0,240},{16,0},{32,16},{48,32},{64,48},{80,64},{96,80},{112,96},{1... | collective-permute-start | bytes 786440 | tf_op jit(solution)/shard_map/ppermute | solution.py:328

commit v10 on v9

--- a/solution.py
+++ b/solution.py
@@ -53,7 +53,7 @@
 
     depth_row[...] = jnp.zeros(depth_row.shape, jnp.float32)
     depth_row[:DENSITIES, :TAPS] = depth_taps[...].astype(jnp.float32)
-    depth = bands.shape[-1]
+    mid = bands.shape[-1]
     block = (LANES, LANES)
     ahead = iota(block, 1) - iota(block, 0)
 
@@ -61,14 +61,16 @@
         row = jnp.broadcast_to(depth_row[pl.ds(density, 1)], block)
         ring_t = pltpu.roll(row, LANES - RADIUS, 1, stride=1, stride_axis=0)
         for ref, ring in ((bands_t, ring_t), (bands, ring_t.T)):
-            ref[density] = jnp.zeros((depth, depth), jnp.bfloat16)
+            ref[density] = jnp.zeros(ref.shape[1:], jnp.bfloat16)
             for step in (-1, 0, 1):
                 here = jnp.abs(ahead + step * LANES) <= RADIUS
                 part = jnp.where(here, ring, 0.0).astype(jnp.bfloat16)
-                for start in range(0, depth, LANES):
+                for start in range(0, mid, LANES):
                     across = start + step * LANES
-                    if 0 <= across < depth:
-                        ref[density, start : start + LANES, across : across + LANES] = part
+                    if 0 <= across < mid:
+                        ref[density, 0, start : start + LANES, across : across + LANES] = part
+                        if step:
+                            ref[density, 1, start : start + LANES, across : across + LANES] = part
         return carry
 
     lax.fori_loop(0, DENSITIES, band, 0)
@@ -132,7 +134,7 @@
     cells = DENSITIES * CELLS
     shapes = [(cells, 3 * CELLS)] * 2 + [(cells, CELLS)] * 2
     shapes += [(4 * CELLS, cells)] * 2
-    shapes += [(DENSITIES, depth, depth)] * 2
+    shapes += [(DENSITIES, 2, depth // 2, depth // 2)] * 2
     vmem = pl.BlockSpec(memory_space=pltpu.VMEM)
     hbm = pl.BlockSpec(memory_space=pltpu.HBM)
     return pl.pallas_call(
@@ -200,6 +202,22 @@
     )(*pieces, wh, wl)
 
 
+def along_depth(values, bands):
+    mid, count = bands.shape[-1], values.shape[0]
+    quarter = mid // 2
+    stacked = jnp.concatenate([values[:, :mid], values[:, mid:]], 0)
+    main = jnp.dot(stacked, bands[0], preferred_element_type=jnp.float32)
+    cross = jnp.dot(values[:, quarter : quarter + mid], bands[1], preferred_element_type=jnp.float32)
+    first, second = main[:count], main[count:]
+    parts = [
+        first[:, :quarter],
+        first[:, quarter:] + cross[:, :quarter],
+        second[:, :quarter] + cross[:, quarter:],
+        second[:, quarter:],
+    ]
+    return jnp.concatenate(parts, 1)
+
+
 def middle_kernel(
     partial, corner_a, corner_b, wh, wl, bands, bands_t, th, tl, hessian, out_a, out_b, bh, bl,
     dens, low
@@ -218,7 +236,7 @@
         rows = slice(b * CELLS, (b + 1) * CELLS)
         own = slice(b * half, (b + 1) * half)
         lateral = partial[rows] + jnp.concatenate([terms[0][own], terms[1][own]], 0)
-        dens[b] = jnp.dot(lateral.astype(jnp.bfloat16), bands[b], preferred_element_type=jnp.float32)
+        dens[b] = along_depth(lateral.astype(jnp.bfloat16), bands[b])
     for a in range(DENSITIES):
         for r in range(TILE):
             cells = slice(r * TILE, (r + 1) * TILE)
@@ -226,7 +244,7 @@
             for b in range(1, DENSITIES):
                 grad = grad + hessian[a, b, r].astype(jnp.float32) * dens[b, cells]
             low[a, cells] = grad.astype(jnp.bfloat16)
-        back = jnp.dot(low[a], bands_t[a], preferred_element_type=jnp.float32)
+        back = along_depth(low[a], bands_t[a])
         rows = slice(a * CELLS, (a + 1) * CELLS)
         high, rest = halves(back)
         bh[rows] = high

time: 53.1 us -> 53 us (level)
  no operation moved by 1% of the time
where the time goes in v10:
time: 53 us; the launch traced here: 52.8 us
  starting transfers between devices  20.5 us (39%)
  Pallas kernels  17.6 us (33%)
  waiting for transfers between devices  13.3 us (25%)
  other arithmetic  1.17 us (2%)
    ppermute x4, waiting for transfers between devices, swap_b(): lax.ppermute(cells, 'gy', [(j, (j + (1 if j % 2 else -1)) % count) for j...  13.3 us
    ppermute x4, starting transfers between devices, shift(): lax.ppermute(cells, axis, [(i, (i + step) % count) for i in range(count)])  11.7 us
    ppermute x4, starting transfers between devices, swap_b(): lax.ppermute(cells, 'gy', [(j, (j + (1 if j % 2 else -1)) % count) for j...  8.68 us
    pallas_call x1, Pallas kernels, build(): pl.pallas_call(build_kernel, out_shape=[jax.ShapeDtypeStruct(s, jnp.bfloa...  5.17 us
    pallas_call x1, Pallas kernels, near(): pl.pallas_call(near_kernel, out_shape=jax.ShapeDtypeStruct((DENSITIES * C...  4.11 us
    pallas_call x1, Pallas kernels, middle(): pl.pallas_call(middle_kernel, out_shape=[edge, edge, back, back], in_spec...  3.8 us
    pallas_call x2, Pallas kernels, spread(): pl.pallas_call(functools.partial(spread_kernel, group), out_shape=[jax.Sh...  3.35 us
    pallas_call x1, Pallas kernels, cut(): pl.pallas_call(cut_kernel, out_shape=[jax.ShapeDtypeStruct(s + (depth,),...  1.19 us
  transfers between devices with their start and end apart: 12, of which 4 were waited for; matrix products, arithmetic and copies ran while one was open for 1% of the time, Pallas kernels for 24%

profile of v10, /device:TPU:4, one launch (start us, length us, event | category | flops | bytes accessed | tf_op | source)
XLA Modules:
  0.0 52.8 jit_solution(1922271472285470354)
XLA Ops:
  0.0 1.2 %cut.1 = (f32[8,16,512]{2,1,0:T(8,128)S(1)}, f32[8,16,512]{2,1,0:T(8,128)S(1)}, f32[16,8,512]{2,1,0:T(8,128)S(1)}, f32[16,8,512]{2,1,0:T(8,128)S(1)}, f32[16,16,512]{2,1,0:T(8,128)S(1)}) custom-call(f32[16,16,512]{2,1,0:T(8,128)} %tangent.1), custom_call_target="tpu_custom_call" | custom-call | bytes 3145728 | tf_op jit(solution)/shard_map/cut/pallas_call | solution.py:332
  1.2 2.0 %collective-permute-start = (f32[8,16,512]{2,1,0:T(8,128)S(1)}, f32[8,16,512]{2,1,0:T(8,128)S(1)}, u32[]{:S(2)}, u32[]{:S(2)}) collective-permute-start(f32[8,16,512]{2,1,0:T(8,128)S(1)} %get-tuple-element.36), channel_id=1, source_target_pairs={{0,16},{16,32},{32,48},{48,64},{64,80},{80,96},{96,112},{112,128},... | collective-permute-start | bytes 786440 | tf_op jit(solution)/shard_map/ppermute | solution.py:346
  3.2 4.0 %collective-permute-start.1 = (f32[8,16,512]{2,1,0:T(8,128)S(1)}, f32[8,16,512]{2,1,0:T(8,128)S(1)}, u32[]{:S(2)}, u32[]{:S(2)}) collective-permute-start(f32[8,16,512]{2,1,0:T(8,128)S(1)} %get-tuple-element.37), channel_id=1, source_target_pairs={{0,240},{16,0},{32,16},{48,32},{64,48},{80,64},{96,80},{112,96},{1... | collective-permute-start | bytes 786440 | tf_op jit(solution)/shard_map/ppermute | solution.py:346
  7.2 3.7 %collective-permute-start.3 = (f32[16,8,512]{2,1,0:T(8,128)S(1)}, f32[16,8,512]{2,1,0:T(8,128)S(1)}, u32[]{:S(2)}, u32[]{:S(2)}) collective-permute-start(f32[16,8,512]{2,1,0:T(8,128)S(1)} %get-tuple-element.38), channel_id=1, source_target_pairs={{0,15},{1,2},{2,1},{3,4},{4,3},{5,6},{6,5},{7,8},{8,7},{9,10},{10,... | collective-permute-start | bytes 786440 | tf_op jit(solution)/shard_map/ppermute | solution.py:356
  10.9 0.0 collective-permute-start.2
  10.9 5.2 %build.1 = (bf16[1280,768]{1,0:T(8,128)(2,1)S(1)}, bf16[1280,768]{1,0:T(8,128)(2,1)S(1)}, bf16[1280,256]{1,0:T(8,128)(2,1)S(1)}, bf16[1280,256]{1,0:T(8,128)(2,1...) custom-call(f32[5,17]{1,0:T(8,128)} %kr_hbm.1, ...), custom_call_target="tpu_custom_call" | custom-call | flops 31457280 | bytes 16777216 | tf_op jit(solution)/shard_map/build/pallas_call | solution.py:140
  16.1 0.0 collective-permute-done.north
  16.1 0.0 collective-permute-done.1.south
  16.1 0.0 slice-start
  16.2 1.0 %collective-permute-start.5 = (f32[16,8,512]{2,1,0:T(8,128)S(1)}, f32[16,8,512]{2,1,0:T(8,128)S(1)}, u32[]{:S(2)}, u32[]{:S(2)}) collective-permute-start(f32[16,8,512]{2,1,0:T(8,128)S(1)} %get-tuple-element.64), channel_id=1, source_target_pairs={{0,15},{1,2},{2,1},{3,4},{4,3},{5,6},{6,5},{7,8},{8,7},{9,10},{10,... | collective-permute-start | bytes 786440 | tf_op jit(solution)/shard_map/ppermute | solution.py:356
  17.2 0.0 collective-permute-start.4
  17.2 0.0 collective-permute-done.2.side_a
  17.2 4.8 %collective-permute-done.3.side_b = f32[16,8,512]{2,1,0:T(8,128)S(1)} collective-permute-done((f32[16,8,512]{2,1,0:T(8,128)S(1)}, f32[16,8,512]{2,1,0:T(8,128)S(1)}, u32[]{:S(2)}, u32[]{:S(2)}) %collective-permute-start.3) | collective-permute-done | bytes 262176 | tf_op jit(solution)/shard_map/ppermute | solution.py:356
  22.0 0.0 slice-start.1
  22.0 4.1 %near.1.partial = f32[1280,512]{1,0:T(8,128)S(1)} custom-call(f32[16,16,512]{2,1,0:T(8,128)S(1)} %get-tuple-element.35.own, f32[8,16,512]{2,1,0:T(8,128)S(1)} %collective-permute-done.north, f32[8,16,512]{2,1,0:T(8,128)S(1)} %collective-permute-done.1.south, f32[16,8,512]{2,1,0:T(8,128)S(1)} %collective-permute-done.2.side_a, ...), custom_call_target="tpu_custom_call" | custom-call | flops 3019898880 | bytes 10485760 | tf_op jit(solution)/shard_map/near/pallas_call | solution.py:191
  26.2 0.0 collective-permute-done.4.corner_a
  26.2 1.5 %collective-permute-done.5.corner_b = f32[16,8,512]{2,1,0:T(8,128)S(1)} collective-permute-done((f32[16,8,512]{2,1,0:T(8,128)S(1)}, f32[16,8,512]{2,1,0:T(8,128)S(1)}, u32[]{:S(2)}, u32[]{:S(2)}) %collective-permute-start.5) | collective-permute-done | bytes 262176 | tf_op jit(solution)/shard_map/ppermute | solution.py:356
  27.7 0.0 slice-done
  27.7 0.0 slice-done.1
  27.7 3.8 %middle.1 = (f32[16,8,512]{2,1,0:T(8,128)S(1)}, f32[16,8,512]{2,1,0:T(8,128)S(1)}, bf16[1280,512]{1,0:T(8,128)(2,1)S(1)}, bf16[1280,512]{1,0:T(8,128)(2,1)S(1)}) custom-call(f32[1280,512]{1,0:T(8,128)S(1)} %near.1.partial, f32[16,8,512]{2,1,0:T(8,128)S(1)} %collective-permute-done.4.corner_a, f32[16,8,512]{2,1,0:T(8,128)S(1)} %collective-permute-done.5.corner_b, ...), custom_call_target="tpu_custom_call" | custom-call | flops 3355443200 | bytes 16777216 | tf_op jit(solution)/shard_map/middle/pallas_call | solution.py:263
  31.5 0.1 collective-permute-start.6
  31.6 0.1 collective-permute-start.7
  31.7 2.2 %spread.2 = (f32[8,16,512]{2,1,0:T(8,128)S(1)}, f32[8,16,512]{2,1,0:T(8,128)S(1)}, f32[16,8,512]{2,1,0:T(8,128)S(1)}, f32[16,8,512]{2,1,0:T(8,128)S(1)}) custom-call(bf16[1024,1280]{1,0:T(8,128)(2,1)S(1)} %get-tuple-element.33.th, bf16[1024,1280]{1,0:T(8,128)(2,1)S(1)} %get-tuple-element.34.tl, bf16[1280,512]{1,0:T(8,128)(2,1)S(1)} %get-tuple-element.55.bh, ...), custom_call_target="tpu_custom_call" | custom-call | flops 2013265920 | bytes 6291456 | tf_op jit(solution)/shard_map/spread/pallas_call | solution.py:294
  33.9 3.8 %collective-permute-start.8 = (f32[16,8,512]{2,1,0:T(8,128)S(1)}, f32[16,8,512]{2,1,0:T(8,128)S(1)}, u32[]{:S(2)}, u32[]{:S(2)}) collective-permute-start(f32[16,8,512]{2,1,0:T(8,128)S(1)} %get-tuple-element.57), channel_id=1, source_target_pairs={{0,15},{1,2},{2,1},{3,4},{4,3},{5,6},{6,5},{7,8},{8,7},{9,10},{10,... | collective-permute-start | bytes 786440 | tf_op jit(solution)/shard_map/ppermute | solution.py:356
  37.7 0.0 collective-permute-start.9
  37.7 3.7 %collective-permute-done.6 = f32[16,8,512]{2,1,0:T(8,128)S(1)} collective-permute-done((f32[16,8,512]{2,1,0:T(8,128)S(1)}, f32[16,8,512]{2,1,0:T(8,128)S(1)}, u32[]{:S(2)}, u32[]{:S(2)}) %collective-permute-start.6) | collective-permute-done | bytes 262176 | tf_op jit(solution)/shard_map/ppermute | solution.py:356
  41.4 0.1 maximum_add_fusion
  41.5 0.0 collective-permute-done.7
  41.5 0.1 select_add_fusion
  41.6 0.1 collective-permute-start.10
  41.7 5.6 %collective-permute-start.11 = (f32[8,16,512]{2,1,0:T(8,128)S(1)}, f32[8,16,512]{2,1,0:T(8,128)S(1)}, u32[]{:S(2)}, u32[]{:S(2)}) collective-permute-start(f32[8,16,512]{2,1,0:T(8,128)S(1)} %get-tuple-element.60), channel_id=1, source_target_pairs={{0,240},{16,0},{32,16},{48,32},{64,48},{80,64},{96,80},{112,96},{1... | collective-permute-start | bytes 786440 | tf_op jit(solution)/shard_map/ppermute | solution.py:346
  47.4 1.2 %spread.3 = f32[16,16,512]{2,1,0:T(8,128)S(1)} custom-call(bf16[1024,1280]{1,0:T(8,128)(2,1)S(1)} %get-tuple-element.33.th, bf16[1024,1280]{1,0:T(8,128)(2,1)S(1)} %get-tuple-element.34.tl, bf16[1280,512]{1,0:T(8,128)(2,1)S(1)} %get-tuple-element.55.bh, bf16[1280,512]{1,0:T(8,128)(2,1)S(1)} %get-tuple-element.56.bl), custom_call_target="tpu_custom_call" | custom-call | flops 1006632960 | bytes 6291456 | tf_op jit(solution)/shard_map/spread/pallas_call | solution.py:294
  48.5 0.0 collective-permute-done.9
  48.5 3.3 %collective-permute-done.8 = f32[16,8,512]{2,1,0:T(8,128)S(1)} collective-permute-done((f32[16,8,512]{2,1,0:T(8,128)S(1)}, f32[16,8,512]{2,1,0:T(8,128)S(1)}, u32[]{:S(2)}, u32[]{:S(2)}) %collective-permute-start.8) | collective-permute-done | bytes 262176 | tf_op jit(solution)/shard_map/ppermute | solution.py:356
  51.8 0.1 fusion
  51.9 0.0 collective-permute-done.11
  51.9 0.0 collective-permute-done.10
  51.9 0.9 %maximum_add_fusion.1 = f32[16,16,512]{2,1,0:T(8,128)} fusion(f32[16,16,512]{2,1,0:T(8,128)S(1)} %fusion, f32[8,16,512]{2,1,0:T(8,128)S(1)} %collective-permute-done.11, f32[8,16,512]{2,1,0:T(8,128)S(1)} %collective-permute-done.10), kind=kLoop, calls=%fused_computation.3 | loop fusion | flops 262144 | bytes 1572864 | tf_op jit(solution)/shard_map/add | solution.py:407
  (5 shorter events, 0.1 us)
Async XLA Ops:
  1.2 14.9 %collective-permute-start = (f32[8,16,512]{2,1,0:T(8,128)S(1)}, f32[8,16,512]{2,1,0:T(8,128)S(1)}, u32[]{:S(2)}, u32[]{:S(2)}) collective-permute-start(f32[8,16,512]{2,1,0:T(8,128)S(1)} %get-tuple-element.36), channel_id=1, source_target_pairs={{0,16},{16,32},{32,48},{48,64},{64,80},{80,96},{96,112},{112,128},... | collective-permute-start | bytes 786440 | tf_op jit(solution)/shard_map/ppermute | solution.py:346
  3.2 12.9 %collective-permute-start.1 = (f32[8,16,512]{2,1,0:T(8,128)S(1)}, f32[8,16,512]{2,1,0:T(8,128)S(1)}, u32[]{:S(2)}, u32[]{:S(2)}) collective-permute-start(f32[8,16,512]{2,1,0:T(8,128)S(1)} %get-tuple-element.37), channel_id=1, source_target_pairs={{0,240},{16,0},{32,16},{48,32},{64,48},{80,64},{96,80},{112,96},{1... | collective-permute-start | bytes 786440 | tf_op jit(solution)/shard_map/ppermute | solution.py:346
  7.2 14.9 %collective-permute-start.3 = (f32[16,8,512]{2,1,0:T(8,128)S(1)}, f32[16,8,512]{2,1,0:T(8,128)S(1)}, u32[]{:S(2)}, u32[]{:S(2)}) collective-permute-start(f32[16,8,512]{2,1,0:T(8,128)S(1)} %get-tuple-element.38), channel_id=1, source_target_pairs={{0,15},{1,2},{2,1},{3,4},{4,3},{5,6},{6,5},{7,8},{8,7},{9,10},{10,... | collective-permute-start | bytes 786440 | tf_op jit(solution)/shard_map/ppermute | solution.py:356
  10.9 6.4 %collective-permute-start.2 = (f32[16,8,512]{2,1,0:T(8,128)S(1)}, f32[16,8,512]{2,1,0:T(8,128)S(1)}, u32[]{:S(2)}, u32[]{:S(2)}) collective-permute-start(f32[16,8,512]{2,1,0:T(8,128)S(1)} %get-tuple-element.40), channel_id=1, source_target_pairs={{0,1},{1,0},{2,3},{3,2},{4,5},{5,4},{6,7},{7,6},{8,9},{9,8},{10,11... | collective-permute-start | bytes 786440 | tf_op jit(solution)/shard_map/ppermute | solution.py:351
  16.1 11.5 %slice-start = ((s8[6553600]{0:T(1024)(128)(4,1)}), s8[4194304]{0:T(1024)(128)(4,1)S(1)}, s32[]{:S(2)}) async-start(s8[6553600]{0:T(1024)(128)(4,1)} %bitcast), calls=%async_computation | async-start | bytes 8388608
  16.2 11.5 %collective-permute-start.5 = (f32[16,8,512]{2,1,0:T(8,128)S(1)}, f32[16,8,512]{2,1,0:T(8,128)S(1)}, u32[]{:S(2)}, u32[]{:S(2)}) collective-permute-start(f32[16,8,512]{2,1,0:T(8,128)S(1)} %get-tuple-element.64), channel_id=1, source_target_pairs={{0,15},{1,2},{2,1},{3,4},{4,3},{5,6},{6,5},{7,8},{8,7},{9,10},{10,... | collective-permute-start | bytes 786440 | tf_op jit(solution)/shard_map/ppermute | solution.py:356
  17.2 8.9 %collective-permute-start.4 = (f32[16,8,512]{2,1,0:T(8,128)S(1)}, f32[16,8,512]{2,1,0:T(8,128)S(1)}, u32[]{:S(2)}, u32[]{:S(2)}) collective-permute-start(f32[16,8,512]{2,1,0:T(8,128)S(1)} %get-tuple-element.43), channel_id=1, source_target_pairs={{0,1},{1,0},{2,3},{3,2},{4,5},{5,4},{6,7},{7,6},{8,9},{9,8},{10,11... | collective-permute-start | bytes 786440 | tf_op jit(solution)/shard_map/ppermute | solution.py:351
  22.0 5.6 %slice-start.1 = ((s8[6553600]{0:T(1024)(128)(4,1)}), s8[2359296]{0:T(1024)(128)(4,1)S(1)}, s32[]{:S(2)}) async-start(s8[6553600]{0:T(1024)(128)(4,1)} %bitcast), calls=%async_computation.1 | async-start | bytes 4718592
  31.5 9.9 %collective-permute-start.6 = (f32[16,8,512]{2,1,0:T(8,128)S(1)}, f32[16,8,512]{2,1,0:T(8,128)S(1)}, u32[]{:S(2)}, u32[]{:S(2)}) collective-permute-start(f32[16,8,512]{2,1,0:T(8,128)S(1)} %get-tuple-element.52), channel_id=1, source_target_pairs={{0,15},{1,2},{2,1},{3,4},{4,3},{5,6},{6,5},{7,8},{8,7},{9,10},{10,... | collective-permute-start | bytes 786440 | tf_op jit(solution)/shard_map/ppermute | solution.py:356
  31.6 9.9 %collective-permute-start.7 = (f32[16,8,512]{2,1,0:T(8,128)S(1)}, f32[16,8,512]{2,1,0:T(8,128)S(1)}, u32[]{:S(2)}, u32[]{:S(2)}) collective-permute-start(f32[16,8,512]{2,1,0:T(8,128)S(1)} %get-tuple-element.54), channel_id=1, source_target_pairs={{0,1},{1,0},{2,3},{3,2},{4,5},{5,4},{6,7},{7,6},{8,9},{9,8},{10,11... | collective-permute-start | bytes 786440 | tf_op jit(solution)/shard_map/ppermute | solution.py:351
  33.9 17.9 %collective-permute-start.8 = (f32[16,8,512]{2,1,0:T(8,128)S(1)}, f32[16,8,512]{2,1,0:T(8,128)S(1)}, u32[]{:S(2)}, u32[]{:S(2)}) collective-permute-start(f32[16,8,512]{2,1,0:T(8,128)S(1)} %get-tuple-element.57), channel_id=1, source_target_pairs={{0,15},{1,2},{2,1},{3,4},{4,3},{5,6},{6,5},{7,8},{8,7},{9,10},{10,... | collective-permute-start | bytes 786440 | tf_op jit(solution)/shard_map/ppermute | solution.py:356
  37.7 10.8 %collective-permute-start.9 = (f32[16,8,512]{2,1,0:T(8,128)S(1)}, f32[16,8,512]{2,1,0:T(8,128)S(1)}, u32[]{:S(2)}, u32[]{:S(2)}) collective-permute-start(f32[16,8,512]{2,1,0:T(8,128)S(1)} %get-tuple-element.59), channel_id=1, source_target_pairs={{0,1},{1,0},{2,3},{3,2},{4,5},{5,4},{6,7},{7,6},{8,9},{9,8},{10,11... | collective-permute-start | bytes 786440 | tf_op jit(solution)/shard_map/ppermute | solution.py:351
  41.6 10.3 %collective-permute-start.10 = (f32[8,16,512]{2,1,0:T(8,128)S(1)}, f32[8,16,512]{2,1,0:T(8,128)S(1)}, u32[]{:S(2)}, u32[]{:S(2)}) collective-permute-start(f32[8,16,512]{2,1,0:T(8,128)S(1)} %get-tuple-element.61), channel_id=1, source_target_pairs={{0,16},{16,32},{32,48},{48,64},{64,80},{80,96},{96,112},{112,128},... | collective-permute-start | bytes 786440 | tf_op jit(solution)/shard_map/ppermute | solution.py:346
  41.7 10.2 %collective-permute-start.11 = (f32[8,16,512]{2,1,0:T(8,128)S(1)}, f32[8,16,512]{2,1,0:T(8,128)S(1)}, u32[]{:S(2)}, u32[]{:S(2)}) collective-permute-start(f32[8,16,512]{2,1,0:T(8,128)S(1)} %get-tuple-element.60), channel_id=1, source_target_pairs={{0,240},{16,0},{32,16},{48,32},{64,48},{80,64},{96,80},{112,96},{1... | collective-permute-start | bytes 786440 | tf_op jit(solution)/shard_map/ppermute | solution.py:346

commit v11 on v10

--- a/solution.py
+++ b/solution.py
@@ -388,8 +388,8 @@
     to_a, to_b, bh, bl = middle(partial, corner_a, corner_b, ch, cl, bands, bands_t, th, tl, hessian)
     from_b, from_a = swapped(to_b, to_a)
 
-    above, below, edge_a, edge_b = spread(
-        1, th, tl, bh, bl, [(reach, span_cols)] * 2 + [(span_rows, reach)] * 2
+    upper, lower, above, below, edge_a, edge_b = spread(
+        0, th, tl, bh, bl, [(reach, span_cols)] * 4 + [(span_rows, reach)] * 2
     )
     edge_from_b, edge_from_a = swapped(edge_b, edge_a)
 
@@ -401,10 +401,11 @@
     above, below = lax.optimization_barrier((above, below))
     side_from_s = shift(above, "gx", -1)
 
-    around, bh, bl = lax.optimization_barrier((around, bh, bl))
-    (own,) = spread(0, th, tl, bh, bl, [(span_rows, span_cols)])
+    own = jnp.concatenate([upper, lower], 0)
     own = lax.optimization_barrier(own + joined(edge_from_a, edge_from_b))
-    return own + jnp.concatenate([side_from_n, side_from_s], 0)
+    blank = jnp.zeros_like(side_from_n)
+    own = lax.optimization_barrier(own + jnp.concatenate([side_from_n, blank], 0))
+    return own + jnp.concatenate([blank, side_from_s], 0)
 
 
 def solution(mesh):

time: 53 us -> 52.7 us (level)
    pallas_call x2 -> x1, Pallas kernels: 3.35 us -> 3.2 us  [spread(): pl.pallas_call(functools.partial(spread_kernel, group), out_shape=[jax.Sh...]
where the time goes in v11:
time: 52.7 us; the launch traced here: 52.5 us
  starting transfers between devices  20.6 us (39%)
  Pallas kernels  17.5 us (33%)
  waiting for transfers between devices  12.9 us (24%)
  other arithmetic  1.2 us (2%)
    ppermute x4, waiting for transfers between devices, swap_b(): lax.ppermute(cells, 'gy', [(j, (j + (1 if j % 2 else -1)) % count) for j...  12.9 us
    ppermute x4, starting transfers between devices, shift(): lax.ppermute(cells, axis, [(i, (i + step) % count) for i in range(count)])  11.7 us
    ppermute x4, starting transfers between devices, swap_b(): lax.ppermute(cells, 'gy', [(j, (j + (1 if j % 2 else -1)) % count) for j...  8.86 us
    pallas_call x1, Pallas kernels, build(): pl.pallas_call(build_kernel, out_shape=[jax.ShapeDtypeStruct(s, jnp.bfloa...  5.17 us
    pallas_call x1, Pallas kernels, near(): pl.pallas_call(near_kernel, out_shape=jax.ShapeDtypeStruct((DENSITIES * C...  4.11 us
    pallas_call x1, Pallas kernels, middle(): pl.pallas_call(middle_kernel, out_shape=[edge, edge, back, back], in_spec...  3.8 us
    pallas_call x1, Pallas kernels, spread(): pl.pallas_call(functools.partial(spread_kernel, group), out_shape=[jax.Sh...  3.2 us
    pallas_call x1, Pallas kernels, cut(): pl.pallas_call(cut_kernel, out_shape=[jax.ShapeDtypeStruct(s + (depth,),...  1.19 us
  transfers between devices with their start and end apart: 12, of which 4 were waited for; matrix products, arithmetic and copies ran while one was open for 1% of the time, Pallas kernels for 24%

profile of v11, /device:TPU:4, one launch (start us, length us, event | category | flops | bytes accessed | tf_op | source)
XLA Modules:
  0.0 52.5 jit_solution(10644801838378794225)
XLA Ops:
  0.0 1.2 %cut.1 = (f32[8,16,512]{2,1,0:T(8,128)S(1)}, f32[8,16,512]{2,1,0:T(8,128)S(1)}, f32[16,8,512]{2,1,0:T(8,128)S(1)}, f32[16,8,512]{2,1,0:T(8,128)S(1)}, f32[16,16,512]{2,1,0:T(8,128)S(1)}) custom-call(f32[16,16,512]{2,1,0:T(8,128)} %tangent.1), custom_call_target="tpu_custom_call" | custom-call | bytes 3145728 | tf_op jit(solution)/shard_map/cut/pallas_call | solution.py:332
  1.2 2.0 %collective-permute-start = (f32[8,16,512]{2,1,0:T(8,128)S(1)}, f32[8,16,512]{2,1,0:T(8,128)S(1)}, u32[]{:S(2)}, u32[]{:S(2)}) collective-permute-start(f32[8,16,512]{2,1,0:T(8,128)S(1)} %get-tuple-element.36), channel_id=1, source_target_pairs={{0,16},{16,32},{32,48},{48,64},{64,80},{80,96},{96,112},{112,128},... | collective-permute-start | bytes 786440 | tf_op jit(solution)/shard_map/ppermute | solution.py:346
  3.2 4.0 %collective-permute-start.1 = (f32[8,16,512]{2,1,0:T(8,128)S(1)}, f32[8,16,512]{2,1,0:T(8,128)S(1)}, u32[]{:S(2)}, u32[]{:S(2)}) collective-permute-start(f32[8,16,512]{2,1,0:T(8,128)S(1)} %get-tuple-element.37), channel_id=1, source_target_pairs={{0,240},{16,0},{32,16},{48,32},{64,48},{80,64},{96,80},{112,96},{1... | collective-permute-start | bytes 786440 | tf_op jit(solution)/shard_map/ppermute | solution.py:346
  7.2 3.7 %collective-permute-start.3 = (f32[16,8,512]{2,1,0:T(8,128)S(1)}, f32[16,8,512]{2,1,0:T(8,128)S(1)}, u32[]{:S(2)}, u32[]{:S(2)}) collective-permute-start(f32[16,8,512]{2,1,0:T(8,128)S(1)} %get-tuple-element.38), channel_id=1, source_target_pairs={{0,15},{1,2},{2,1},{3,4},{4,3},{5,6},{6,5},{7,8},{8,7},{9,10},{10,... | collective-permute-start | bytes 786440 | tf_op jit(solution)/shard_map/ppermute | solution.py:356
  10.9 0.0 collective-permute-start.2
  10.9 5.2 %build.1 = (bf16[1280,768]{1,0:T(8,128)(2,1)S(1)}, bf16[1280,768]{1,0:T(8,128)(2,1)S(1)}, bf16[1280,256]{1,0:T(8,128)(2,1)S(1)}, bf16[1280,256]{1,0:T(8,128)(2,1...) custom-call(f32[5,17]{1,0:T(8,128)} %kr_hbm.1, ...), custom_call_target="tpu_custom_call" | custom-call | flops 31457280 | bytes 16777216 | tf_op jit(solution)/shard_map/build/pallas_call | solution.py:140
  16.1 0.0 collective-permute-done.north
  16.1 0.0 collective-permute-done.1.south
  16.1 0.0 slice-start
  16.2 1.0 %collective-permute-start.5 = (f32[16,8,512]{2,1,0:T(8,128)S(1)}, f32[16,8,512]{2,1,0:T(8,128)S(1)}, u32[]{:S(2)}, u32[]{:S(2)}) collective-permute-start(f32[16,8,512]{2,1,0:T(8,128)S(1)} %get-tuple-element.64), channel_id=1, source_target_pairs={{0,15},{1,2},{2,1},{3,4},{4,3},{5,6},{6,5},{7,8},{8,7},{9,10},{10,... | collective-permute-start | bytes 786440 | tf_op jit(solution)/shard_map/ppermute | solution.py:356
  17.2 0.0 collective-permute-start.4
  17.2 0.0 collective-permute-done.2.side_a
  17.2 4.8 %collective-permute-done.3.side_b = f32[16,8,512]{2,1,0:T(8,128)S(1)} collective-permute-done((f32[16,8,512]{2,1,0:T(8,128)S(1)}, f32[16,8,512]{2,1,0:T(8,128)S(1)}, u32[]{:S(2)}, u32[]{:S(2)}) %collective-permute-start.3) | collective-permute-done | bytes 262176 | tf_op jit(solution)/shard_map/ppermute | solution.py:356
  22.0 0.0 slice-start.1
  22.0 4.1 %near.1.partial = f32[1280,512]{1,0:T(8,128)S(1)} custom-call(f32[16,16,512]{2,1,0:T(8,128)S(1)} %get-tuple-element.35.own, f32[8,16,512]{2,1,0:T(8,128)S(1)} %collective-permute-done.north, f32[8,16,512]{2,1,0:T(8,128)S(1)} %collective-permute-done.1.south, f32[16,8,512]{2,1,0:T(8,128)S(1)} %collective-permute-done.2.side_a, ...), custom_call_target="tpu_custom_call" | custom-call | flops 3019898880 | bytes 10485760 | tf_op jit(solution)/shard_map/near/pallas_call | solution.py:191
  26.2 0.0 collective-permute-done.4.corner_a
  26.2 1.5 %collective-permute-done.5.corner_b = f32[16,8,512]{2,1,0:T(8,128)S(1)} collective-permute-done((f32[16,8,512]{2,1,0:T(8,128)S(1)}, f32[16,8,512]{2,1,0:T(8,128)S(1)}, u32[]{:S(2)}, u32[]{:S(2)}) %collective-permute-start.5) | collective-permute-done | bytes 262176 | tf_op jit(solution)/shard_map/ppermute | solution.py:356
  27.7 0.0 slice-done
  27.7 0.0 slice-done.1
  27.7 3.8 %middle.1 = (f32[16,8,512]{2,1,0:T(8,128)S(1)}, f32[16,8,512]{2,1,0:T(8,128)S(1)}, bf16[1280,512]{1,0:T(8,128)(2,1)S(1)}, bf16[1280,512]{1,0:T(8,128)(2,1)S(1)}) custom-call(f32[1280,512]{1,0:T(8,128)S(1)} %near.1.partial, f32[16,8,512]{2,1,0:T(8,128)S(1)} %collective-permute-done.4.corner_a, f32[16,8,512]{2,1,0:T(8,128)S(1)} %collective-permute-done.5.corner_b, ...), custom_call_target="tpu_custom_call" | custom-call | flops 3355443200 | bytes 16777216 | tf_op jit(solution)/shard_map/middle/pallas_call | solution.py:263
  31.5 0.1 collective-permute-start.8
  31.6 0.1 collective-permute-start.9
  31.7 3.2 %spread.1 = (f32[8,16,512]{2,1,0:T(8,128)S(1)}, f32[8,16,512]{2,1,0:T(8,128)S(1)}, f32[8,16,512]{2,1,0:T(8,128)S(1)}, f32[8,16,512]{2,1,0:T(8,128)S(1)}, f32[16,...) custom-call(bf16[1024,1280]{1,0:T(8,128)(2,1)S(1)} %get-tuple-element.33.th, bf16[1024,1280]{1,0:T(8,128)(2,1)S(1)} %get-tuple-element.34.tl, ...), custom_call_target="tpu_custom_call" | custom-call | flops 3019898880 | bytes 6291456 | tf_op jit(solution)/shard_map/spread/pallas_call | solution.py:294
  34.9 4.0 %collective-permute-start.6 = (f32[16,8,512]{2,1,0:T(8,128)S(1)}, f32[16,8,512]{2,1,0:T(8,128)S(1)}, u32[]{:S(2)}, u32[]{:S(2)}) collective-permute-start(f32[16,8,512]{2,1,0:T(8,128)S(1)} %get-tuple-element.52), channel_id=1, source_target_pairs={{0,15},{1,2},{2,1},{3,4},{4,3},{5,6},{6,5},{7,8},{8,7},{9,10},{10,... | collective-permute-start | bytes 786440 | tf_op jit(solution)/shard_map/ppermute | solution.py:356
  38.9 0.0 collective-permute-start.7
  38.9 1.7 %collective-permute-done.8 = f32[16,8,512]{2,1,0:T(8,128)S(1)} collective-permute-done((f32[16,8,512]{2,1,0:T(8,128)S(1)}, f32[16,8,512]{2,1,0:T(8,128)S(1)}, u32[]{:S(2)}, u32[]{:S(2)}) %collective-permute-start.8) | collective-permute-done | bytes 262176 | tf_op jit(solution)/shard_map/ppermute | solution.py:356
  40.6 0.1 maximum_add_fusion.1
  40.6 0.0 collective-permute-done.9
  40.7 0.1 select_add_fusion
  40.8 0.1 collective-permute-start.10
  40.9 5.6 %collective-permute-start.11 = (f32[8,16,512]{2,1,0:T(8,128)S(1)}, f32[8,16,512]{2,1,0:T(8,128)S(1)}, u32[]{:S(2)}, u32[]{:S(2)}) collective-permute-start(f32[8,16,512]{2,1,0:T(8,128)S(1)} %get-tuple-element.60), channel_id=1, source_target_pairs={{0,240},{16,0},{32,16},{48,32},{64,48},{80,64},{96,80},{112,96},{1... | collective-permute-start | bytes 786440 | tf_op jit(solution)/shard_map/ppermute | solution.py:346
  46.5 0.0 collective-permute-done.7
  46.5 5.0 %collective-permute-done.6 = f32[16,8,512]{2,1,0:T(8,128)S(1)} collective-permute-done((f32[16,8,512]{2,1,0:T(8,128)S(1)}, f32[16,8,512]{2,1,0:T(8,128)S(1)}, u32[]{:S(2)}, u32[]{:S(2)}) %collective-permute-start.6) | collective-permute-done | bytes 262176 | tf_op jit(solution)/shard_map/ppermute | solution.py:356
  51.5 0.1 maximum_add_fusion
  51.6 0.0 collective-permute-done.10
  51.6 0.1 pad_add_fusion.1
  51.6 0.0 collective-permute-done.11
  51.7 0.9 %pad_add_fusion = f32[16,16,512]{2,1,0:T(8,128)} fusion(f32[16,16,512]{2,1,0:T(8,128)S(1)} %pad_add_fusion.1, f32[8,16,512]{2,1,0:T(8,128)S(1)} %collective-permute-done.11), kind=kLoop, calls=%fused_computation.3 | loop fusion | flops 131072 | bytes 1310720 | tf_op jit(solution)/shard_map/add | solution.py:408
  (5 shorter events, 0.1 us)
Async XLA Ops:
  1.2 14.9 %collective-permute-start = (f32[8,16,512]{2,1,0:T(8,128)S(1)}, f32[8,16,512]{2,1,0:T(8,128)S(1)}, u32[]{:S(2)}, u32[]{:S(2)}) collective-permute-start(f32[8,16,512]{2,1,0:T(8,128)S(1)} %get-tuple-element.36), channel_id=1, source_target_pairs={{0,16},{16,32},{32,48},{48,64},{64,80},{80,96},{96,112},{112,128},... | collective-permute-start | bytes 786440 | tf_op jit(solution)/shard_map/ppermute | solution.py:346
  3.2 12.9 %collective-permute-start.1 = (f32[8,16,512]{2,1,0:T(8,128)S(1)}, f32[8,16,512]{2,1,0:T(8,128)S(1)}, u32[]{:S(2)}, u32[]{:S(2)}) collective-permute-start(f32[8,16,512]{2,1,0:T(8,128)S(1)} %get-tuple-element.37), channel_id=1, source_target_pairs={{0,240},{16,0},{32,16},{48,32},{64,48},{80,64},{96,80},{112,96},{1... | collective-permute-start | bytes 786440 | tf_op jit(solution)/shard_map/ppermute | solution.py:346
  7.2 14.9 %collective-permute-start.3 = (f32[16,8,512]{2,1,0:T(8,128)S(1)}, f32[16,8,512]{2,1,0:T(8,128)S(1)}, u32[]{:S(2)}, u32[]{:S(2)}) collective-permute-start(f32[16,8,512]{2,1,0:T(8,128)S(1)} %get-tuple-element.38), channel_id=1, source_target_pairs={{0,15},{1,2},{2,1},{3,4},{4,3},{5,6},{6,5},{7,8},{8,7},{9,10},{10,... | collective-permute-start | bytes 786440 | tf_op jit(solution)/shard_map/ppermute | solution.py:356
  10.9 6.4 %collective-permute-start.2 = (f32[16,8,512]{2,1,0:T(8,128)S(1)}, f32[16,8,512]{2,1,0:T(8,128)S(1)}, u32[]{:S(2)}, u32[]{:S(2)}) collective-permute-start(f32[16,8,512]{2,1,0:T(8,128)S(1)} %get-tuple-element.40), channel_id=1, source_target_pairs={{0,1},{1,0},{2,3},{3,2},{4,5},{5,4},{6,7},{7,6},{8,9},{9,8},{10,11... | collective-permute-start | bytes 786440 | tf_op jit(solution)/shard_map/ppermute | solution.py:351
  16.1 11.5 %slice-start = ((s8[6553600]{0:T(1024)(128)(4,1)}), s8[4194304]{0:T(1024)(128)(4,1)S(1)}, s32[]{:S(2)}) async-start(s8[6553600]{0:T(1024)(128)(4,1)} %bitcast), calls=%async_computation | async-start | bytes 8388608
  16.2 11.5 %collective-permute-start.5 = (f32[16,8,512]{2,1,0:T(8,128)S(1)}, f32[16,8,512]{2,1,0:T(8,128)S(1)}, u32[]{:S(2)}, u32[]{:S(2)}) collective-permute-start(f32[16,8,512]{2,1,0:T(8,128)S(1)} %get-tuple-element.64), channel_id=1, source_target_pairs={{0,15},{1,2},{2,1},{3,4},{4,3},{5,6},{6,5},{7,8},{8,7},{9,10},{10,... | collective-permute-start | bytes 786440 | tf_op jit(solution)/shard_map/ppermute | solution.py:356
  17.2 8.9 %collective-permute-start.4 = (f32[16,8,512]{2,1,0:T(8,128)S(1)}, f32[16,8,512]{2,1,0:T(8,128)S(1)}, u32[]{:S(2)}, u32[]{:S(2)}) collective-permute-start(f32[16,8,512]{2,1,0:T(8,128)S(1)} %get-tuple-element.43), channel_id=1, source_target_pairs={{0,1},{1,0},{2,3},{3,2},{4,5},{5,4},{6,7},{7,6},{8,9},{9,8},{10,11... | collective-permute-start | bytes 786440 | tf_op jit(solution)/shard_map/ppermute | solution.py:351
  22.0 5.6 %slice-start.1 = ((s8[6553600]{0:T(1024)(128)(4,1)}), s8[2359296]{0:T(1024)(128)(4,1)S(1)}, s32[]{:S(2)}) async-start(s8[6553600]{0:T(1024)(128)(4,1)} %bitcast), calls=%async_computation.1 | async-start | bytes 4718592
  31.5 9.1 %collective-permute-start.8 = (f32[16,8,512]{2,1,0:T(8,128)S(1)}, f32[16,8,512]{2,1,0:T(8,128)S(1)}, u32[]{:S(2)}, u32[]{:S(2)}) collective-permute-start(f32[16,8,512]{2,1,0:T(8,128)S(1)} %get-tuple-element.57), channel_id=1, source_target_pairs={{0,15},{1,2},{2,1},{3,4},{4,3},{5,6},{6,5},{7,8},{8,7},{9,10},{10,... | collective-permute-start | bytes 786440 | tf_op jit(solution)/shard_map/ppermute | solution.py:356
  31.6 9.1 %collective-permute-start.9 = (f32[16,8,512]{2,1,0:T(8,128)S(1)}, f32[16,8,512]{2,1,0:T(8,128)S(1)}, u32[]{:S(2)}, u32[]{:S(2)}) collective-permute-start(f32[16,8,512]{2,1,0:T(8,128)S(1)} %get-tuple-element.59), channel_id=1, source_target_pairs={{0,1},{1,0},{2,3},{3,2},{4,5},{5,4},{6,7},{7,6},{8,9},{9,8},{10,11... | collective-permute-start | bytes 786440 | tf_op jit(solution)/shard_map/ppermute | solution.py:351
  34.9 16.6 %collective-permute-start.6 = (f32[16,8,512]{2,1,0:T(8,128)S(1)}, f32[16,8,512]{2,1,0:T(8,128)S(1)}, u32[]{:S(2)}, u32[]{:S(2)}) collective-permute-start(f32[16,8,512]{2,1,0:T(8,128)S(1)} %get-tuple-element.52), channel_id=1, source_target_pairs={{0,15},{1,2},{2,1},{3,4},{4,3},{5,6},{6,5},{7,8},{8,7},{9,10},{10,... | collective-permute-start | bytes 786440 | tf_op jit(solution)/shard_map/ppermute | solution.py:356
  38.9 7.6 %collective-permute-start.7 = (f32[16,8,512]{2,1,0:T(8,128)S(1)}, f32[16,8,512]{2,1,0:T(8,128)S(1)}, u32[]{:S(2)}, u32[]{:S(2)}) collective-permute-start(f32[16,8,512]{2,1,0:T(8,128)S(1)} %get-tuple-element.54), channel_id=1, source_target_pairs={{0,1},{1,0},{2,3},{3,2},{4,5},{5,4},{6,7},{7,6},{8,9},{9,8},{10,11... | collective-permute-start | bytes 786440 | tf_op jit(solution)/shard_map/ppermute | solution.py:351
  40.8 10.8 %collective-permute-start.10 = (f32[8,16,512]{2,1,0:T(8,128)S(1)}, f32[8,16,512]{2,1,0:T(8,128)S(1)}, u32[]{:S(2)}, u32[]{:S(2)}) collective-permute-start(f32[8,16,512]{2,1,0:T(8,128)S(1)} %get-tuple-element.62), channel_id=1, source_target_pairs={{0,16},{16,32},{32,48},{48,64},{64,80},{80,96},{96,112},{112,128},... | collective-permute-start | bytes 786440 | tf_op jit(solution)/shard_map/ppermute | solution.py:346
  40.9 10.8 %collective-permute-start.11 = (f32[8,16,512]{2,1,0:T(8,128)S(1)}, f32[8,16,512]{2,1,0:T(8,128)S(1)}, u32[]{:S(2)}, u32[]{:S(2)}) collective-permute-start(f32[8,16,512]{2,1,0:T(8,128)S(1)} %get-tuple-element.60), channel_id=1, source_target_pairs={{0,240},{16,0},{32,16},{48,32},{64,48},{80,64},{96,80},{112,96},{1... | collective-permute-start | bytes 786440 | tf_op jit(solution)/shard_map/ppermute | solution.py:346
